TPU v7x, 128 devices: a whole 4x4x4 slice. The times are simulated.
128 devices in a mesh: sector: 16 (over z, y), ops: 8 (over x, core).
Axes of the slice: x: 4, y: 4, z: 4, core: 2. Of those that a mesh axis runs over, the one named last changes fastest.
Arguments:
- wavefunction: float32 [16, 640, 640], P('sector'), may hold values from -160 to 160
- left_env: float32 [16, 32, 640, 640], P('sector', 'ops'), may hold values from -0.25 to 0.25
- right_env: float32 [16, 32, 640, 640], P('sector', 'ops'), may hold values from -0.25 to 0.25
- shift_map: int32 [8, 16], P('ops'), may hold values from 0 to 15, each once within a row
- op_counts: int32 [8, 16], P('ops', 'sector'), may hold values from 1 to 4
Outputs:
- updated_tensor: float32 [16, 640, 640], P('sector', None, 'ops')
- rotated_env: float32 [16, 32, 640, 640], P('sector', 'ops')
Inputs may be any that keep to these rules, and one draw needn't show every extreme that they name: `shift_map`: each row lists every sector once.
All inputs are finite; a program needn't handle non-finite values.
Results may differ from a plain program's by a relative error of at most 0.0003.
Values sent between devices are 32-bit elements; how exact they have to be, the bound alone decides.
No kernel may reach another device: no remote copies, remote signals or barrier semaphores. Data moves between devices by JAX's collectives and lax.ppermute only.
A program may use at most 128 MiB of HBM per device.

v0:
```python
import functools
import math

import jax
import jax.numpy as jnp
from jax import lax
from jax.experimental import pallas as pl
from jax.experimental.pallas import tpu as pltpu
from jax.sharding import Mesh
from jax.sharding import PartitionSpec as P

POLAR = 5
F32, BF16 = jnp.float32, jnp.bfloat16
VMEM_LIMIT = 48 << 20
WHOLE = pl.BlockSpec(memory_space=pltpu.VMEM)


def halves(v):
    high = v.astype(BF16)
    return high, (v - high.astype(F32)).astype(BF16)


def side_by_side(ref, a, b, c):
    n = a.shape[1]
    ref[:, 0:n] = a
    ref[:, n : 2 * n] = b
    ref[:, 2 * n : 3 * n] = c


def stacked(ref, a, b, c):
    n = a.shape[0]
    ref[0:n] = a
    ref[n : 2 * n] = b
    ref[2 * n : 3 * n] = c


def left_form(ref, v):
    high, low = halves(v)
    side_by_side(ref, high, high, low)


def right_form(ref, v):
    high, low = halves(v)
    stacked(ref, high, low, high)


def mm(a, b):
    return jnp.dot(a, b, preferred_element_type=F32)


def mm_nt(a, b):
    return lax.dot_general(a, b, (((1,), (1,)), ((), ())), preferred_element_type=F32)


def params():
    return pltpu.CompilerParams(vmem_limit_bytes=VMEM_LIMIT)


def cost(flops, nbytes):
    return pl.CostEstimate(flops=int(flops), bytes_accessed=int(nbytes), transcendentals=0)


def prepare_kernel(l_ref, r_ref, lo_ref, ro_ref):
    left_form(lo_ref.at[0], l_ref[0])
    right_form(ro_ref.at[0], r_ref[0])


def prepare(left, right):
    k, n, _ = left.shape
    block = pl.BlockSpec((1, n, n), lambda w: (w, 0, 0))
    return pl.pallas_call(
        prepare_kernel,
        grid=(k,),
        out_shape=(jax.ShapeDtypeStruct((k, n, 3 * n), BF16), jax.ShapeDtypeStruct((k, 3 * n, n), BF16)),
        in_specs=[block, block],
        out_specs=(pl.BlockSpec((1, n, 3 * n), lambda w: (w, 0, 0)), pl.BlockSpec((1, 3 * n, n), lambda w: (w, 0, 0))),
        compiler_params=params(),
        cost_estimate=cost(8 * k * n * n, 20 * k * n * n),
        name="prepare",
    )(left, right)


def sigma_kernel(scalars, w_ref, l_ref, r_ref, own_ref, other_ref, w3, mid, acc):
    step = pl.program_id(0)
    half = own_ref.shape[0]

    @pl.when(step == 0)
    def _():
        right_form(w3, w_ref[...])

    @pl.when(step < scalars[0])
    def _():
        left_form(mid, mm(l_ref[0], w3[...]))
        term = mm(mid[...], r_ref[0])

        @pl.when(step == 0)
        def _():
            acc[...] = term

        @pl.when(step > 0)
        def _():
            acc[...] += term

    @pl.when(step == pl.num_programs(0) - 1)
    def _():
        core = scalars[1]
        own_ref[...] = acc[pl.ds(pl.multiple_of(core * half, half), half)]
        other_ref[...] = acc[pl.ds(pl.multiple_of((1 - core) * half, half), half)]


def partial_sigma(scalars, block, left3, right3):
    k, n = left3.shape[0], block.shape[0]
    half = n // 2

    def active(w, s):
        return (jnp.minimum(w, s[0] - 1), 0, 0)

    return pl.pallas_call(
        sigma_kernel,
        out_shape=(jax.ShapeDtypeStruct((half, n), F32),) * 2,
        grid_spec=pltpu.PrefetchScalarGridSpec(
            num_scalar_prefetch=1,
            grid=(k,),
            in_specs=[
                pl.BlockSpec((n, n), lambda w, s: (0, 0)),
                pl.BlockSpec((1, n, 3 * n), active),
                pl.BlockSpec((1, 3 * n, n), active),
            ],
            out_specs=(pl.BlockSpec((half, n), lambda w, s: (0, 0)),) * 2,
            scratch_shapes=[pltpu.VMEM((3 * n, n), BF16), pltpu.VMEM((n, 3 * n), BF16), pltpu.VMEM((n, n), F32)],
        ),
        compiler_params=params(),
        cost_estimate=cost(12 * k * n**3, 16 * k * n * n),
        name="partial_sigma",
    )(scalars, block, left3, right3)


def polar_kernel(core_ref, mine_ref, other_ref, u_ref, ut_ref, x, a, b, r):
    n = x.shape[0]
    half = n // 2
    core = core_ref[0]
    mine, other = mine_ref[...], other_ref[...]
    mean_sq = (jnp.sum(mine * mine) + jnp.sum(other * other)) / float(n * n)
    factor = lax.rsqrt(n * mean_sq + 1e-06) / 2.2
    x[pl.ds(pl.multiple_of(core * half, half), half)] = mine * factor
    x[pl.ds(pl.multiple_of((1 - core) * half, half), half)] = other * factor

    def iteration(_, carry):
        high, low = halves(x[...])
        side_by_side(a, high, high, low)
        side_by_side(b, high, low, high)
        stacked(r, high, low, high)
        first = mm_nt(a[...], b[0:256])
        second = mm_nt(a[256:n], b[256:512])
        third = mm_nt(a[512:n], b[512:n])
        rows = (
            (0, (first[0:256], first[256:n].T)),
            (256, (first[256:512], second[0:256], second[256 : n - 256].T)),
            (512, (first[512:n], second[256 : n - 256], third)),
        )
        for start, blocks in rows:
            high, low = halves(jnp.concatenate(blocks, 1))
            side_by_side(a.at[start : start + high.shape[0]], high, high, low)
        x[...] = 1.5 * x[...] - 0.5 * mm(a[...], r[...])
        return carry

    lax.fori_loop(0, POLAR, iteration, 0)
    updated = x[...] * math.sqrt(n)
    u_ref[...] = updated
    left_form(ut_ref, updated.T)


def polar(core, mine, other):
    n = mine.shape[1]
    return pl.pallas_call(
        polar_kernel,
        out_shape=(jax.ShapeDtypeStruct((n, n), F32), jax.ShapeDtypeStruct((n, 3 * n), BF16)),
        in_specs=[pl.BlockSpec(memory_space=pltpu.SMEM), WHOLE, WHOLE],
        out_specs=(WHOLE, WHOLE),
        scratch_shapes=[
            pltpu.VMEM((n, n), F32),
            pltpu.VMEM((n, 3 * n), BF16),
            pltpu.VMEM((n, 3 * n), BF16),
            pltpu.VMEM((3 * n, n), BF16),
        ],
        compiler_params=params(),
        cost_estimate=cost(POLAR * 12 * n**3, 14 * n * n),
        name="polar",
    )(core, mine, other)


def half_kernel(ut_ref, l_ref, o_ref, l3):
    right_form(l3, l_ref[0])
    left_form(o_ref.at[0], mm(ut_ref[...], l3[...]))


def half_rotated(ut3, left):
    k, n, _ = left.shape
    return pl.pallas_call(
        half_kernel,
        grid=(k,),
        out_shape=jax.ShapeDtypeStruct((k, n, 3 * n), BF16),
        in_specs=[pl.BlockSpec((n, 3 * n), lambda w: (0, 0)), pl.BlockSpec((1, n, n), lambda w: (w, 0, 0))],
        out_specs=pl.BlockSpec((1, n, 3 * n), lambda w: (w, 0, 0)),
        scratch_shapes=[pltpu.VMEM((3 * n, n), BF16)],
        compiler_params=params(),
        cost_estimate=cost(6 * k * n**3, 10 * k * n * n),
        name="half_rotated",
    )(ut3, left)


def rotate_kernel(h_ref, u_ref, o_ref, u3):
    @pl.when(pl.program_id(0) == 0)
    def _():
        right_form(u3, u_ref[...])

    o_ref[0] = mm(h_ref[0], u3[...])


def rotate(half3, source):
    k, n = half3.shape[0], source.shape[0]
    return pl.pallas_call(
        rotate_kernel,
        grid=(k,),
        out_shape=jax.ShapeDtypeStruct((k, n, n), F32),
        in_specs=[pl.BlockSpec((1, n, 3 * n), lambda w: (w, 0, 0)), pl.BlockSpec((n, n), lambda w: (0, 0))],
        out_specs=pl.BlockSpec((1, n, n), lambda w: (w, 0, 0)),
        scratch_shapes=[pltpu.VMEM((3 * n, n), BF16)],
        compiler_params=params(),
        cost_estimate=cost(6 * k * n**3, 10 * k * n * n),
        name="rotate",
    )(half3, source)


def fetch_block(block, sources):
    sectors, states = lax.axis_size("sector"), block.shape[0]
    pieces = block.reshape(sectors, states // sectors, states)
    spread = lax.all_to_all(pieces, "sector", split_axis=0, concat_axis=0, tiled=True)
    picked = jnp.take(spread, sources, axis=0, mode="clip")
    return lax.all_to_all(picked, "sector", split_axis=0, concat_axis=0, tiled=True).reshape(states, states)


def swap_cores(block):
    return lax.ppermute(block, "core", [(0, 1), (1, 0)])


def shards(wavefunction, left_env, right_env, shift_map, op_counts):
    chips = lax.axis_size("x")
    core = lax.axis_index("core")
    group_size = chips * lax.axis_size("core")
    group_here = lax.axis_index("x") * lax.axis_size("core") + core
    states = wavefunction.shape[1]
    half = states // 2
    sources = shift_map[0]
    left3, right3 = prepare(left_env[0], right_env[0])
    moved_block = fetch_block(wavefunction[0], sources)

    scalars = jnp.stack([op_counts[0, 0], core.astype(jnp.int32)])
    own, other = partial_sigma(scalars, moved_block, left3, right3)
    pair = (own + swap_cores(other)).reshape(chips, half // chips, states)
    rows = jnp.sum(lax.all_to_all(pair, "x", split_axis=0, concat_axis=0, tiled=True), axis=0)
    mine = lax.all_gather(rows, "x", tiled=True)
    updated, ut3 = polar(scalars[1:], mine, swap_cores(mine))

    column_width = states // group_size
    own_columns = lax.dynamic_slice_in_dim(updated, group_here * column_width, column_width, 1)
    source_tensor = fetch_block(updated, sources)
    rotated = rotate(half_rotated(ut3, left_env[0]), source_tensor)
    return (own_columns[None], rotated[None])


def solution(mesh):
    sectors, groups = mesh.devices.shape
    fine = Mesh(mesh.devices.reshape(sectors, groups // 2, 2), ("sector", "x", "core"))
    ops = ("x", "core")
    return jax.shard_map(
        shards,
        mesh=fine,
        in_specs=(
            P("sector", None, None),
            P("sector", ops, None, None),
            P("sector", ops, None, None),
            P(ops, None),
            P(ops, "sector"),
        ),
        out_specs=(P("sector", None, ops), P("sector", ops, None, None)),
        check_vma=False,
    )
```

profile of v0, /device:TPU:0, one launch (start us, length us, event | category | flops | bytes accessed | tf_op | source)
XLA Modules:
  0.0 215.1 jit_solution(11463484996035969662)
XLA Ops:
  0.6 0.0 copy-start.2
  0.6 8.1 %all-to-all-start = ((f32[16,40,640]{2,1,0:T(8,128)}), f32[16,40,640]{2,1,0:T(8,128)S(1)}, u32[]{:S(2)}, u32[]{:S(2)}) async-start(f32[16,40,640]{2,1,0:T(8,128)} %bitcast.20), calls=%async_computation | async-start | bytes 3276800 | tf_op jit(solution)/shard_map/all_to_all | solution.py:238
  8.8 0.0 copy-done.2
  8.8 25.3 %all-to-all-done = f32[16,40,640]{2,1,0:T(8,128)S(1)} async-done(((f32[16,40,640]{2,1,0:T(8,128)}), f32[16,40,640]{2,1,0:T(8,128)S(1)}, u32[]{:S(2)}, u32[]{:S(2)}) %all-to-all-start) | async-done | bytes 1638432 | tf_op jit(solution)/shard_map/all_to_all | solution.py:238
  34.1 1.8 gather_fusion
  35.9 3.7 %all-to-all-start.1 = ((f32[16,40,640]{2,1,0:T(8,128)}), f32[16,40,640]{2,1,0:T(8,128)S(1)}, u32[]{:S(2)}, u32[]{:S(2)}) async-start(f32[16,40,640]{2,1,0:T(8,128)} %gather_fusion), calls=%async_computation.1 | async-start | bytes 3276800 | tf_op jit(solution)/shard_map/all_to_all | solution.py:240
  40.3 12.3 %prepare.1 = (bf16[4,640,1920]{2,1,0:T(8,128)(2,1)}, bf16[4,1920,640]{2,1,0:T(8,128)(2,1)}) custom-call(f32[4,640,640]{2,1,0:T(8,128)} %bitcast.17, f32[4,640,640]{2,1,0:T(8,128)} %bitcast.16), custom_call_target="tpu_custom_call" | custom-call | flops 13107200 | bytes 32768000 | tf_op jit(solution)/shard_map/prepare/pallas_call | solution.py:71
  52.6 0.1 pad_add_fusion.scalars
  52.7 11.2 %all-to-all-done.1 = f32[16,40,640]{2,1,0:T(8,128)S(1)} async-done(((f32[16,40,640]{2,1,0:T(8,128)}), f32[16,40,640]{2,1,0:T(8,128)S(1)}, u32[]{:S(2)}, u32[]{:S(2)}) %all-to-all-start.1) | async-done | bytes 1638432 | tf_op jit(solution)/shard_map/all_to_all | solution.py:240
  63.8 23.7 %partial_sigma.1 = (f32[320,640]{1,0:T(8,128)S(1)}, f32[320,640]{1,0:T(8,128)S(1)}) custom-call(s32[2]{0:T(128)S(1)} %pad_add_fusion.scalars, f32[640,640]{1,0:T(8,128)S(1)} %bitcast.15, bf16[4,640,1920]{2,1,0:T(8,128)(2,1)} %get-tuple-element.8.l_ref, bf16[4,1920,640]{2,1,0:T(8,128)(2,1)} %get-tuple-element.9.r_ref), custom_call_target="tpu_custom_call" | custom-call | flops 12582912000 | bytes 26214400 | tf_op jit(solution)/shard_map/partial_sigma/pallas_call | solution.py:118
  87.5 0.1 collective-permute-start
  87.6 2.3 %collective-permute-done = f32[320,640]{1,0:T(8,128)S(1)} collective-permute-done((f32[320,640]{1,0:T(8,128)S(1)}, f32[320,640]{1,0:T(8,128)S(1)}, u32[]{:S(2)}, u32[]{:S(2)}) %collective-permute-start) | collective-permute-done | bytes 819232 | tf_op jit(solution)/shard_map/ppermute | solution.py:244
  90.0 0.1 add.9
  90.0 17.0 %all_to_all.25 = f32[4,80,640]{2,1,0:T(8,128)S(1)} all-to-all(f32[4,80,640]{2,1,0:T(8,128)S(1)} %bitcast.19), channel_id=1, replica_groups=mesh['sector'=16,'x'=4,'core'=2] {'x'}, dimensions={0} | all-to-all | bytes 1638400 | tf_op jit(solution)/shard_map/all_to_all | solution.py:261
  107.1 14.3 %all_gather.3.mine_ref = f32[320,640]{1,0:T(8,128)S(1)} all-gather(f32[80,640]{1,0:T(8,128)S(1)} %reduce_sum.9), channel_id=1, replica_groups=mesh['sector'=16,'x'=4,'core'=2] {'x'}, dimensions={0}, use_global_device_ids=true | all-gather | bytes 1024000 | tf_op jit(solution)/shard_map/all_gather | solution.py:262
  121.5 0.0 collective-permute-start.1
  121.5 2.3 %collective-permute-done.1.other_ref = f32[320,640]{1,0:T(8,128)S(1)} collective-permute-done((f32[320,640]{1,0:T(8,128)S(1)}, f32[320,640]{1,0:T(8,128)S(1)}, u32[]{:S(2)}, u32[]{:S(2)}) %collective-permute-start.1) | collective-permute-done | bytes 819232 | tf_op jit(solution)/shard_map/ppermute | solution.py:244
  123.8 20.8 %polar.1 = (f32[640,640]{1,0:T(8,128)S(1)}, bf16[640,1920]{1,0:T(8,128)(2,1)S(1)}) custom-call(s32[1]{0:T(128)} %bitcast.core_ref, f32[320,640]{1,0:T(8,128)S(1)} %all_gather.3.mine_ref, f32[320,640]{1,0:T(8,128)S(1)} %collective-permute-done.1.other_ref), custom_call_target="tpu_custom_call" | custom-call | flops 15728640000 | bytes 5734400 | tf_op jit(solution)/shard_map/polar/pallas_call | solution.py:175
  144.6 0.0 copy-start
  144.6 1.4 copy-done
  146.1 26.7 %all_to_all.26 = f32[16,40,640]{2,1,0:T(8,128)S(1)} all-to-all(f32[16,40,640]{2,1,0:T(8,128)S(1)} %bitcast.13), channel_id=1, replica_groups=mesh['sector'=16,'x'=4,'core'=2] {'sector'}, dimensions={0} | all-to-all | bytes 3276800 | tf_op jit(solution)/shard_map/all_to_all | solution.py:238
  172.8 1.8 gather_fusion.1
  174.6 3.9 %all-to-all-start.4 = ((f32[16,40,640]{2,1,0:T(8,128)}), f32[16,40,640]{2,1,0:T(8,128)S(1)}, u32[]{:S(2)}, u32[]{:S(2)}) async-start(f32[16,40,640]{2,1,0:T(8,128)} %gather_fusion.1), calls=%async_computation.4 | async-start | bytes 3276800 | tf_op jit(solution)/shard_map/all_to_all | solution.py:240
  178.5 0.9 constant_dynamic-slice_fusion
  179.4 1.8 copy.7
  181.2 0.0 copy-start.1
  181.2 1.7 copy-done.1
  182.9 12.0 %half_rotated.1.h_ref = bf16[4,640,1920]{2,1,0:T(8,128)(2,1)} custom-call(bf16[640,1920]{1,0:T(8,128)(2,1)S(1)} %copy-done.1, f32[4,640,640]{2,1,0:T(8,128)} %bitcast.18), custom_call_target="tpu_custom_call" | custom-call | flops 6291456000 | bytes 16384000 | tf_op jit(solution)/shard_map/half_rotated/pallas_call | solution.py:199
  194.9 8.2 %all-to-all-done.4 = f32[16,40,640]{2,1,0:T(8,128)S(1)} async-done(((f32[16,40,640]{2,1,0:T(8,128)}), f32[16,40,640]{2,1,0:T(8,128)S(1)}, u32[]{:S(2)}, u32[]{:S(2)}) %all-to-all-start.4) | async-done | bytes 1638432 | tf_op jit(solution)/shard_map/all_to_all | solution.py:240
  203.1 11.9 %rotate.1 = f32[4,640,640]{2,1,0:T(8,128)} custom-call(bf16[4,640,1920]{2,1,0:T(8,128)(2,1)} %half_rotated.1.h_ref, f32[640,640]{1,0:T(8,128)S(1)} %bitcast.14), custom_call_target="tpu_custom_call" | custom-call | flops 6291456000 | bytes 16384000 | tf_op jit(solution)/shard_map/rotate/pallas_call | solution.py:222
  (2 shorter events, 0.0 us)
Async XLA Ops:
  0.6 8.2 %copy-start.2 = (s32[1,16]{1,0:T(1,128)S(1)}, s32[1,16]{1,0:T(1,128)}, u32[]{:S(2)}) copy-start(s32[1,16]{1,0:T(1,128)} %param.8) | copy-start | bytes 196
  0.6 33.5 %all-to-all-start = ((f32[16,40,640]{2,1,0:T(8,128)}), f32[16,40,640]{2,1,0:T(8,128)S(1)}, u32[]{:S(2)}, u32[]{:S(2)}) async-start(f32[16,40,640]{2,1,0:T(8,128)} %bitcast.20), calls=%async_computation | async-start | bytes 3276800 | tf_op jit(solution)/shard_map/all_to_all | solution.py:238
  35.9 27.9 %all-to-all-start.1 = ((f32[16,40,640]{2,1,0:T(8,128)}), f32[16,40,640]{2,1,0:T(8,128)S(1)}, u32[]{:S(2)}, u32[]{:S(2)}) async-start(f32[16,40,640]{2,1,0:T(8,128)} %gather_fusion), calls=%async_computation.1 | async-start | bytes 3276800 | tf_op jit(solution)/shard_map/all_to_all | solution.py:240
  87.5 2.4 %collective-permute-start = (f32[320,640]{1,0:T(8,128)S(1)}, f32[320,640]{1,0:T(8,128)S(1)}, u32[]{:S(2)}, u32[]{:S(2)}) collective-permute-start(f32[320,640]{1,0:T(8,128)S(1)} %get-tuple-element.11), channel_id=1, source_target_pairs={{0,1},{1,0},{2,3},{3,2},{4,5},{5,4},{6,7},{7,6},{8,9},{9,8},{10,11... | collective-permute-start | bytes 2457608 | tf_op jit(solution)/shard_map/ppermute | solution.py:244
  121.5 2.3 %collective-permute-start.1 = (f32[320,640]{1,0:T(8,128)S(1)}, f32[320,640]{1,0:T(8,128)S(1)}, u32[]{:S(2)}, u32[]{:S(2)}) collective-permute-start(f32[320,640]{1,0:T(8,128)S(1)} %all_gather.3.mine_ref), channel_id=1, source_target_pairs={{0,1},{1,0},{2,3},{3,2},{4,5},{5,4},{6,7},{7,6},{8,9},{9,8},{10,11... | collective-permute-start | bytes 2457608 | tf_op jit(solution)/shard_map/ppermute | solution.py:244
  144.6 1.4 copy-start
  174.6 28.5 %all-to-all-start.4 = ((f32[16,40,640]{2,1,0:T(8,128)}), f32[16,40,640]{2,1,0:T(8,128)S(1)}, u32[]{:S(2)}, u32[]{:S(2)}) async-start(f32[16,40,640]{2,1,0:T(8,128)} %gather_fusion.1), calls=%async_computation.4 | async-start | bytes 3276800 | tf_op jit(solution)/shard_map/all_to_all | solution.py:240
  181.2 1.7 copy-start.1
where the time goes:
time: 215 us
  Pallas kernels  80.8 us (38%)
  blocking collectives  58.1 us (27%)
  waiting for transfers between devices  49.3 us (23%)
  starting transfers between devices  15.8 us (7%)
  local copies, waits for them, and re-layouts  9.45 us (4%)
    all_to_all x1, blocking collectives, fetch_block(): lax.all_to_all(pieces, 'sector', split_axis=0, concat_axis=0, tiled=True)  26.7 us
    all_to_all x1, waiting for transfers between devices, fetch_block(): lax.all_to_all(pieces, 'sector', split_axis=0, concat_axis=0, tiled=True)  25.3 us
    pallas_call x1, Pallas kernels, partial_sigma(): pl.pallas_call(sigma_kernel, out_shape=(jax.ShapeDtypeStruct((half, n), F...  23.7 us
    pallas_call x1, Pallas kernels, polar(): pl.pallas_call(polar_kernel, out_shape=(jax.ShapeDtypeStruct((n, n), F32)...  20.8 us
    all_to_all x2, waiting for transfers between devices, fetch_block(): lax.all_to_all(picked, 'sector', split_axis=0, concat_axis=0, tiled=True)  19.4 us
    all_to_all x1, blocking collectives, shards(): lax.all_to_all(pair, 'x', split_axis=0, concat_axis=0, tiled=True)  17 us
    all_gather x1, blocking collectives, shards(): mine = lax.all_gather(rows, 'x', tiled=True)  14.3 us
    pallas_call x1, Pallas kernels, prepare(): pl.pallas_call(prepare_kernel, grid=(k,), out_shape=(jax.ShapeDtypeStruct...  12.3 us
  transfers between devices with their start and end apart: 5, of which 5 were waited for; matrix products, arithmetic and copies ran while one was open for 1% of the time, Pallas kernels for 11%

commit v1 on v0

v1 whole, which is shorter than its diff:
```python
import functools
import math

import jax
import jax.numpy as jnp
from jax import lax
from jax.experimental import pallas as pl
from jax.experimental.pallas import tpu as pltpu
from jax.sharding import Mesh
from jax.sharding import PartitionSpec as P

POLAR = 5
SECTORS = 16
LANES = 128
F32, BF16 = jnp.float32, jnp.bfloat16
VMEM_LIMIT = 48 << 20
WHOLE = pl.BlockSpec(memory_space=pltpu.VMEM)


def halves(v):
    high = v.astype(BF16)
    return high, (v - high.astype(F32)).astype(BF16)


def side_by_side(ref, a, b, c):
    n = a.shape[1]
    ref[:, 0:n] = a
    ref[:, n : 2 * n] = b
    ref[:, 2 * n : 3 * n] = c


def stacked(ref, a, b, c):
    n = a.shape[0]
    ref[0:n] = a
    ref[n : 2 * n] = b
    ref[2 * n : 3 * n] = c


def left_form(ref, v):
    high, low = halves(v)
    side_by_side(ref, high, high, low)


def right_form(ref, v):
    high, low = halves(v)
    stacked(ref, high, low, high)


def mm(a, b):
    return jnp.dot(a, b, preferred_element_type=F32)


def mm_nt(a, b):
    return lax.dot_general(a, b, (((1,), (1,)), ((), ())), preferred_element_type=F32)


def params():
    return pltpu.CompilerParams(vmem_limit_bytes=VMEM_LIMIT)


def cost(flops, nbytes):
    return pl.CostEstimate(flops=int(flops), bytes_accessed=int(nbytes), transcendentals=0)


def prepare_kernel(l_ref, r_ref, lo_ref, ro_ref):
    left_form(lo_ref.at[0], l_ref[0])
    right_form(ro_ref.at[0], r_ref[0])


def prepare(left, right):
    k, n, _ = left.shape
    block = pl.BlockSpec((1, n, n), lambda w: (w, 0, 0))
    return pl.pallas_call(
        prepare_kernel,
        grid=(k,),
        out_shape=(jax.ShapeDtypeStruct((k, n, 3 * n), BF16), jax.ShapeDtypeStruct((k, 3 * n, n), BF16)),
        in_specs=[block, block],
        out_specs=(pl.BlockSpec((1, n, 3 * n), lambda w: (w, 0, 0)), pl.BlockSpec((1, 3 * n, n), lambda w: (w, 0, 0))),
        compiler_params=params(),
        cost_estimate=cost(8 * k * n * n, 20 * k * n * n),
        name="prepare",
    )(left, right)


def columns_to_rows(ref, v):
    n = v.shape[0]
    for t in range(n // LANES):
        ref[t * n : (t + 1) * n] = v[:, t * LANES : (t + 1) * LANES]


def halves_at(ref, core):
    half = ref.shape[0] // 2
    return (
        pl.ds(pl.multiple_of(core * half, half), half),
        pl.ds(pl.multiple_of((1 - core) * half, half), half),
    )


def sigma_kernel(scalars, w_ref, l_ref, r_ref, own_ref, other_ref, w3, mid, acc, rows):
    step = pl.program_id(0)
    n = acc.shape[0]

    @pl.when(step == 0)
    def _():
        pieces, count, _ = w_ref.shape
        chips = pieces // SECTORS
        for piece in range(pieces):
            start = (piece % chips * SECTORS + piece // chips) * count
            rows[start : start + count] = w_ref[piece]
        for t in range(n // LANES):
            high, low = halves(rows[t * n : (t + 1) * n])
            stacked(w3.at[:, t * LANES : (t + 1) * LANES], high, low, high)

    @pl.when(step < scalars[0])
    def _():
        left_form(mid, mm(l_ref[0], w3[...]))
        term = mm(mid[...], r_ref[0])

        @pl.when(step == 0)
        def _():
            acc[...] = term

        @pl.when(step > 0)
        def _():
            acc[...] += term

    @pl.when(step == pl.num_programs(0) - 1)
    def _():
        columns_to_rows(rows, acc)
        own, other = halves_at(rows, scalars[1])
        own_ref[...] = rows[own]
        other_ref[...] = rows[other]


def partial_sigma(scalars, pieces, left3, right3):
    k, n = left3.shape[:2]
    lines = n * n // LANES

    def active(w, s):
        return (jnp.minimum(w, s[0] - 1), 0, 0)

    return pl.pallas_call(
        sigma_kernel,
        out_shape=(jax.ShapeDtypeStruct((lines // 2, LANES), F32),) * 2,
        grid_spec=pltpu.PrefetchScalarGridSpec(
            num_scalar_prefetch=1,
            grid=(k,),
            in_specs=[
                pl.BlockSpec(pieces.shape, lambda w, s: (0, 0, 0)),
                pl.BlockSpec((1, n, 3 * n), active),
                pl.BlockSpec((1, 3 * n, n), active),
            ],
            out_specs=(pl.BlockSpec((lines // 2, LANES), lambda w, s: (0, 0)),) * 2,
            scratch_shapes=[
                pltpu.VMEM((3 * n, n), BF16),
                pltpu.VMEM((n, 3 * n), BF16),
                pltpu.VMEM((n, n), F32),
                pltpu.VMEM((lines, LANES), F32),
            ],
        ),
        compiler_params=params(),
        cost_estimate=cost(12 * k * n**3, 16 * k * n * n),
        name="partial_sigma",
    )(scalars, pieces, left3, right3)


def iterate_polar(rows, x, a, b, r):
    n = x.shape[0]
    mean_sq = jnp.sum(rows[...] * rows[...]) / float(n * n)
    factor = lax.rsqrt(n * mean_sq + 1e-06) / 2.2
    for t in range(n // LANES):
        x[:, t * LANES : (t + 1) * LANES] = rows[t * n : (t + 1) * n] * factor

    def iteration(_, carry):
        high, low = halves(x[...])
        side_by_side(a, high, high, low)
        side_by_side(b, high, low, high)
        stacked(r, high, low, high)
        first = mm_nt(a[...], b[0:256])
        second = mm_nt(a[256:n], b[256:512])
        third = mm_nt(a[512:n], b[512:n])
        blocks_of = (
            (0, (first[0:256], first[256:n].T)),
            (256, (first[256:512], second[0:256], second[256 : n - 256].T)),
            (512, (first[512:n], second[256 : n - 256], third)),
        )
        for start, blocks in blocks_of:
            high, low = halves(jnp.concatenate(blocks, 1))
            side_by_side(a.at[start : start + high.shape[0]], high, high, low)
        x[...] = 1.5 * x[...] - 0.5 * mm(a[...], r[...])
        return carry

    lax.fori_loop(0, POLAR, iteration, 0)


def polar_scratch(n):
    return [
        pltpu.VMEM((n * n // LANES, LANES), F32),
        pltpu.VMEM((n, n), F32),
        pltpu.VMEM((n, 3 * n), BF16),
        pltpu.VMEM((n, 3 * n), BF16),
        pltpu.VMEM((3 * n, n), BF16),
    ]


def own_polar_kernel(scalars, p_ref, columns_ref, ut_ref, rows, x, a, b, r):
    pieces, count, _ = p_ref.shape
    mine, other = halves_at(rows, scalars[0])
    for piece in range(pieces // 2):
        lines = pl.ds(piece * count, count)
        rows.at[mine][lines] = p_ref[2 * piece]
        rows.at[other][lines] = p_ref[2 * piece + 1]
    iterate_polar(rows, x, a, b, r)
    updated = (x[...] * math.sqrt(x.shape[0])).T
    left_form(ut_ref, updated)
    x[...] = updated
    width = columns_ref.shape[0]
    columns_ref[...] = x[pl.ds(pl.multiple_of(scalars[1] * width, width), width)]


def own_polar(scalars, pieces, n):
    return pl.pallas_call(
        own_polar_kernel,
        out_shape=(jax.ShapeDtypeStruct((n // pieces.shape[0], n), F32), jax.ShapeDtypeStruct((n, 3 * n), BF16)),
        in_specs=[pl.BlockSpec(memory_space=pltpu.SMEM), WHOLE],
        out_specs=(WHOLE, WHOLE),
        scratch_shapes=polar_scratch(n),
        compiler_params=params(),
        cost_estimate=cost(POLAR * 12 * n**3, 14 * n * n),
        name="own_polar",
    )(scalars, pieces)


def source_polar_kernel(core_ref, p_ref, u_ref, rows, x, a, b, r, mine_rows, other_rows):
    pieces, count, _ = p_ref.shape
    chips, part = pieces // SECTORS, count // 2
    for piece in range(pieces):
        start = (piece % chips * SECTORS + piece // chips) * part
        mine_rows[start : start + part] = p_ref[piece, 0:part]
        other_rows[start : start + part] = p_ref[piece, part:count]
    mine, other = halves_at(rows, core_ref[0])
    rows[mine] = mine_rows[...]
    rows[other] = other_rows[...]
    iterate_polar(rows, x, a, b, r)
    right_form(u_ref, x[...] * math.sqrt(x.shape[0]))


def source_polar(core, pieces, n):
    half_rows = pltpu.VMEM((n * n // LANES // 2, LANES), F32)
    return pl.pallas_call(
        source_polar_kernel,
        out_shape=jax.ShapeDtypeStruct((3 * n, n), BF16),
        in_specs=[pl.BlockSpec(memory_space=pltpu.SMEM), WHOLE],
        out_specs=WHOLE,
        scratch_shapes=polar_scratch(n) + [half_rows, half_rows],
        compiler_params=params(),
        cost_estimate=cost(POLAR * 12 * n**3, 10 * n * n),
        name="source_polar",
    )(core, pieces)


def half_kernel(ut_ref, l_ref, o_ref, l3):
    right_form(l3, l_ref[0])
    left_form(o_ref.at[0], mm(ut_ref[...], l3[...]))


def half_rotated(ut3, left):
    k, n, _ = left.shape
    return pl.pallas_call(
        half_kernel,
        grid=(k,),
        out_shape=jax.ShapeDtypeStruct((k, n, 3 * n), BF16),
        in_specs=[pl.BlockSpec((n, 3 * n), lambda w: (0, 0)), pl.BlockSpec((1, n, n), lambda w: (w, 0, 0))],
        out_specs=pl.BlockSpec((1, n, 3 * n), lambda w: (w, 0, 0)),
        scratch_shapes=[pltpu.VMEM((3 * n, n), BF16)],
        compiler_params=params(),
        cost_estimate=cost(6 * k * n**3, 10 * k * n * n),
        name="half_rotated",
    )(ut3, left)


def rotate_kernel(h_ref, u_ref, o_ref):
    o_ref[0] = mm(h_ref[0], u_ref[...])


def rotate(half3, source3):
    k, n, _ = half3.shape
    return pl.pallas_call(
        rotate_kernel,
        grid=(k,),
        out_shape=jax.ShapeDtypeStruct((k, n, n), F32),
        in_specs=[pl.BlockSpec((1, n, 3 * n), lambda w: (w, 0, 0)), pl.BlockSpec((3 * n, n), lambda w: (0, 0))],
        out_specs=pl.BlockSpec((1, n, n), lambda w: (w, 0, 0)),
        compiler_params=params(),
        cost_estimate=cost(6 * k * n**3, 10 * k * n * n),
        name="rotate",
    )(half3, source3)


def cut_kernel(chip_ref, w_ref, o_ref, rows, part):
    columns_to_rows(rows, w_ref)
    lines = part.shape[0]
    part[...] = rows[pl.ds(pl.multiple_of(chip_ref[0] * lines, lines), lines)]
    pieces, count, _ = o_ref.shape
    for piece in range(pieces):
        o_ref[piece] = part[piece * count : (piece + 1) * count]


def cut(chip, block, chips):
    n = block.shape[0]
    lines = n * n // LANES
    return pl.pallas_call(
        cut_kernel,
        out_shape=jax.ShapeDtypeStruct((SECTORS, lines // chips // SECTORS, LANES), F32),
        in_specs=[pl.BlockSpec(memory_space=pltpu.SMEM), WHOLE],
        out_specs=WHOLE,
        scratch_shapes=[pltpu.VMEM((lines, LANES), F32), pltpu.VMEM((lines // chips, LANES), F32)],
        compiler_params=params(),
        cost_estimate=cost(n * n, 5 * n * n),
        name="cut",
    )(chip, block)


def pair_kernel(mine_ref, other_ref, o_ref):
    pieces, count, _ = o_ref.shape
    part = count // 2
    for piece in range(pieces):
        lines = slice(piece * part, (piece + 1) * part)
        o_ref[piece, 0:part] = mine_ref[lines]
        o_ref[piece, part:count] = other_ref[lines]


def pair_up(mine, other):
    lines = mine.shape[0]
    return pl.pallas_call(
        pair_kernel,
        out_shape=jax.ShapeDtypeStruct((SECTORS, 2 * lines // SECTORS, LANES), F32),
        in_specs=[WHOLE, WHOLE],
        out_specs=WHOLE,
        compiler_params=params(),
        cost_estimate=cost(lines, 16 * lines * LANES),
        name="pair_up",
    )(mine, other)


def swap_cores(block):
    return lax.ppermute(block, "core", [(0, 1), (1, 0)])


def exchange(pieces, axes):
    return lax.all_to_all(pieces, axes, split_axis=0, concat_axis=0, tiled=True)


def fetch(pieces, readers):
    spread = exchange(pieces, "sector")
    return exchange(jnp.take(spread, readers, axis=0, mode="clip"), ("sector", "x"))


def shards(wavefunction, left_env, right_env, shift_map, op_counts):
    chips = lax.axis_size("x")
    chip, core = lax.axis_index("x"), lax.axis_index("core")
    group_here = chip * lax.axis_size("core") + core
    n = wavefunction.shape[1]
    lines = n * n // LANES
    scalars = jnp.stack([op_counts[0, 0], core.astype(jnp.int32)])
    readers = lax.all_gather(shift_map[0], "x").T.reshape(-1)
    left3, right3 = prepare(left_env[0], right_env[0])

    moved = fetch(cut(chip.astype(jnp.int32)[None], wavefunction[0], chips), readers)

    own, other = partial_sigma(scalars, moved, left3, right3)
    pair = (own + swap_cores(other)).reshape(chips, lines // 2 // chips, LANES)
    chunk = jnp.sum(exchange(pair, "x"), axis=0)

    other_chunk = swap_cores(chunk)
    source_pieces = fetch(pair_up(chunk, other_chunk), readers)

    own_pieces = lax.all_gather(jnp.stack([chunk, other_chunk]), "x", tiled=True)
    own_rows, ut3 = own_polar(jnp.stack([core, group_here]).astype(jnp.int32), own_pieces, n)
    half3, source_pieces = lax.optimization_barrier((half_rotated(ut3, left_env[0]), source_pieces))
    rotated = rotate(half3, source_polar(scalars[1:], source_pieces, n))
    return (own_rows.T[None], rotated[None])


def solution(mesh):
    sectors, groups = mesh.devices.shape
    fine = Mesh(mesh.devices.reshape(sectors, groups // 2, 2), ("sector", "x", "core"))
    ops = ("x", "core")
    return jax.shard_map(
        shards,
        mesh=fine,
        in_specs=(
            P("sector", None, None),
            P("sector", ops, None, None),
            P("sector", ops, None, None),
            P(ops, None),
            P(ops, "sector"),
        ),
        out_specs=(P("sector", None, ops), P("sector", ops, None, None)),
        check_vma=False,
    )
```

time: 215 us -> 207 us (0.963)
  blocking collectives: 58.1 us -> 28.4 us
  waiting for transfers between devices: 49.3 us -> 28.2 us
  Pallas kernels: 80.8 us -> 100 us
  between operations: 1.38 us -> 14.8 us
  starting transfers between devices: 15.8 us -> 26.1 us
  local copies, waits for them, and re-layouts: 9.45 us -> 6.82 us
    all_to_all x2 -> x1, blocking collectives: 43.8 us -> 18.8 us  [exchange(): return lax.all_to_all(pieces, axes, split_axis=0, concat_axis=0, tiled=True)]
    all_to_all x3 -> x4, waiting for transfers between devices: 44.7 us -> 24.4 us  [exchange(): return lax.all_to_all(pieces, axes, split_axis=0, concat_axis=0, tiled=True)]
    pallas_call x2 -> x5, Pallas kernels: 44.5 us -> 64.2 us  [the longest x1 22.3 us: own_polar(): pl.pallas_call(own_polar_kernel, out_shape=(jax.ShapeDtypeStruct((n // pi...]
    all_to_all x3 -> x4, starting transfers between devices: 15.7 us -> 24.1 us  [exchange(): return lax.all_to_all(pieces, axes, split_axis=0, concat_axis=0, tiled=True)]
    all_gather x1, blocking collectives: 14.3 us -> 9.67 us  [shards(): readers = lax.all_gather(shift_map[0], 'x').T.reshape(-1)]
    dynamic_slice x2 -> x0, local copies, waits for them, and re-layouts: 2.69 us -> none  [shards(): lax.dynamic_slice_in_dim(updated, group_here * column_width, column_width...]
  transfers between devices with their start and end apart: 5 -> 7, of which waited for: 5 -> 6; matrix products, arithmetic and copies ran while one was open for 1% -> 1% of each run, Pallas kernels for 11% -> 23%
where the time goes in v1:
time: 207 us; the launch traced here: 206 us
  Pallas kernels  100 us (48%)
  blocking collectives  28.4 us (14%)
  waiting for transfers between devices  28.2 us (14%)
  starting transfers between devices  26.1 us (13%)
  between operations  14.8 us (7%)
  local copies, waits for them, and re-layouts  6.82 us (3%)
    all_to_all x4, waiting for transfers between devices, exchange(): return lax.all_to_all(pieces, axes, split_axis=0, concat_axis=0, tiled=True)  24.4 us
    all_to_all x4, starting transfers between devices, exchange(): return lax.all_to_all(pieces, axes, split_axis=0, concat_axis=0, tiled=True)  24.1 us
    pallas_call x1, Pallas kernels, own_polar(): pl.pallas_call(own_polar_kernel, out_shape=(jax.ShapeDtypeStruct((n // pi...  22.3 us
    pallas_call x1, Pallas kernels, source_polar(): pl.pallas_call(source_polar_kernel, out_shape=jax.ShapeDtypeStruct((3 * n...  21.1 us
    pallas_call x1, Pallas kernels, partial_sigma(): pl.pallas_call(sigma_kernel, out_shape=(jax.ShapeDtypeStruct((lines // 2,...  19 us
    all_to_all x1, blocking collectives, exchange(): return lax.all_to_all(pieces, axes, split_axis=0, concat_axis=0, tiled=True)  18.8 us
    pallas_call x1, Pallas kernels, prepare(): pl.pallas_call(prepare_kernel, grid=(k,), out_shape=(jax.ShapeDtypeStruct...  12.4 us
    pallas_call x1, Pallas kernels, half_rotated(): pl.pallas_call(half_kernel, grid=(k,), out_shape=jax.ShapeDtypeStruct((k,...  12 us
  transfers between devices with their start and end apart: 7, of which 6 were waited for; matrix products, arithmetic and copies ran while one was open for 1% of the time, Pallas kernels for 23%

profile of v1, /device:TPU:0, one launch (start us, length us, event | category | flops | bytes accessed | tf_op | source)
XLA Modules:
  0.0 205.7 jit_solution(1655297539526843329)
XLA Ops:
  7.2 0.0 copy-start.2
  7.2 0.0 copy-start
  7.2 1.4 copy-done
  8.6 0.9 cut.1
  9.5 8.1 %all-to-all-start = ((f32[16,50,128]{2,1,0:T(8,128)}), f32[16,50,128]{2,1,0:T(8,128)S(1)}, u32[]{:S(2)}, u32[]{:S(2)}) async-start(f32[16,50,128]{2,1,0:T(8,128)} %cut.1), calls=%async_computation | async-start | bytes 917504 | tf_op jit(solution)/shard_map/all_to_all | solution.py:351
  17.7 0.0 copy-done.2
  17.7 9.7 %all-gather = s32[4,1,16]{2,1,0:T(1,128)S(1)} all-gather(s32[1,1,16]{2,1,0:T(1,128)S(1)} %bitcast.27), channel_id=1, replica_groups=mesh['sector'=16,'x'=4,'core'=2] {'x'}, dimensions={0}, use_global_device_ids=true | all-gather | bytes 320 | tf_op jit(solution)/shard_map/all_gather | solution.py:366
  27.4 0.1 copy.9
  27.4 0.1 reshape.12
  27.5 0.9 all-to-all-done
  28.5 1.9 gather_fusion
  30.4 7.5 %all-to-all-start.1 = ((f32[64,50,128]{2,1,0:T(8,128)}), f32[64,50,128]{2,1,0:T(8,128)S(1)}, u32[]{:S(2)}, u32[]{:S(2)}) async-start(f32[64,50,128]{2,1,0:T(8,128)} %gather_fusion), calls=%async_computation.1 | async-start | bytes 3670016 | tf_op jit(solution)/shard_map/all_to_all | solution.py:351
  37.9 0.0 all-gather.3.cloned.1.call-start
  38.6 12.4 %prepare.1 = (bf16[4,640,1920]{2,1,0:T(8,128)(2,1)}, bf16[4,1920,640]{2,1,0:T(8,128)(2,1)}) custom-call(f32[4,640,640]{2,1,0:T(8,128)} %bitcast.23, f32[4,640,640]{2,1,0:T(8,128)} %bitcast.22), custom_call_target="tpu_custom_call" | custom-call | flops 13107200 | bytes 32768000 | tf_op jit(solution)/shard_map/prepare/pallas_call | solution.py:73
  50.9 0.1 pad_add_fusion.1.scalars
  51.0 12.2 %all-to-all-done.1.w_ref = f32[64,50,128]{2,1,0:T(8,128)S(1)} async-done(((f32[64,50,128]{2,1,0:T(8,128)}), f32[64,50,128]{2,1,0:T(8,128)S(1)}, u32[]{:S(2)}, u32[]{:S(2)}) %all-to-all-start.1) | async-done | bytes 1638432 | tf_op jit(solution)/shard_map/all_to_all | solution.py:351
  63.2 19.0 %partial_sigma.1 = (f32[1600,128]{1,0:T(8,128)S(1)}, f32[1600,128]{1,0:T(8,128)S(1)}) custom-call(s32[2]{0:T(128)S(1)} %pad_add_fusion.1.scalars, f32[64,50,128]{2,1,0:T(8,128)S(1)} %all-to-all-done.1.w_ref, bf16[4,640,1920]{2,1,0:T(8,128)(2,1)} %get-tuple-element.10.l_ref, bf16[4,1920,640]{2,1,0:T(8,128)(2,1)} %get-tuple-element.11.r_ref), custom_call_target="tpu_custom_call" | custom-call | flops 12582912000 | bytes 26214400 | tf_op jit(solution)/shard_map/partial_sigma/pallas_call | solution.py:142
  82.2 1.9 collective-permute-start
  84.2 2.0 collective-permute-done
  86.1 0.1 add.7
  86.2 18.8 %all_to_all.25 = f32[4,400,128]{2,1,0:T(8,128)S(1)} all-to-all(f32[4,400,128]{2,1,0:T(8,128)S(1)} %bitcast.25), channel_id=1, replica_groups=mesh['sector'=16,'x'=4,'core'=2] {'x'}, dimensions={0} | all-to-all | bytes 1638400 | tf_op jit(solution)/shard_map/all_to_all | solution.py:351
  105.0 0.1 collective-permute-start.1
  105.1 1.4 collective-permute-done.1.other_ref
  106.6 0.8 pad_maximum_fusion
  107.4 0.0 all-gather.3.cloned.1.call-update
  107.4 0.8 pair_up.1
  108.2 3.6 %all-to-all-start.3 = ((f32[16,50,128]{2,1,0:T(8,128)}), f32[16,50,128]{2,1,0:T(8,128)S(1)}, u32[]{:S(2)}, u32[]{:S(2)}) async-start(f32[16,50,128]{2,1,0:T(8,128)} %pair_up.1), calls=%async_computation.3 | async-start | bytes 917504 | tf_op jit(solution)/shard_map/all_to_all | solution.py:351
  111.8 0.1 pad_add_fusion.scalars
  111.8 11.3 %all-to-all-done.3 = f32[16,50,128]{2,1,0:T(8,128)S(1)} async-done(((f32[16,50,128]{2,1,0:T(8,128)}), f32[16,50,128]{2,1,0:T(8,128)S(1)}, u32[]{:S(2)}, u32[]{:S(2)}) %all-to-all-start.3) | async-done | bytes 409632 | tf_op jit(solution)/shard_map/all_to_all | solution.py:351
  123.1 1.9 gather_fusion.1
  125.0 4.9 %all-to-all-start.4 = ((f32[64,50,128]{2,1,0:T(8,128)}), f32[64,50,128]{2,1,0:T(8,128)S(1)}, u32[]{:S(2)}, u32[]{:S(2)}) async-start(f32[64,50,128]{2,1,0:T(8,128)} %gather_fusion.1), calls=%async_computation.4 | async-start | bytes 3670016 | tf_op jit(solution)/shard_map/all_to_all | solution.py:351
  129.9 0.4 all-gather.3.cloned.1.call-done.p_ref
  130.3 0.0 copy-start.1
  130.3 1.4 copy-done.1
  131.7 22.3 %own_polar.1 = (f32[80,640]{1,0:T(8,128)}, bf16[640,1920]{1,0:T(8,128)(2,1)S(1)}) custom-call(s32[2]{0:T(128)S(1)} %pad_add_fusion.scalars, f32[8,400,128]{2,1,0:T(8,128)S(1)} %copy-done.1), custom_call_target="tpu_custom_call" | custom-call | flops 15728640000 | bytes 5734400 | tf_op jit(solution)/shard_map/own_polar/pallas_call | solution.py:222
  154.0 12.0 %half_rotated.1.h_ref = bf16[4,640,1920]{2,1,0:T(8,128)(2,1)} custom-call(bf16[640,1920]{1,0:T(8,128)(2,1)S(1)} %get-tuple-element.15.ut_ref, f32[4,640,640]{2,1,0:T(8,128)} %bitcast.24), custom_call_target="tpu_custom_call" | custom-call | flops 6291456000 | bytes 16384000 | tf_op jit(solution)/shard_map/half_rotated/pallas_call | solution.py:269
  166.0 0.0 all-to-all-done.4.p_ref
  166.0 21.1 %source_polar.1.u_ref = bf16[1920,640]{1,0:T(8,128)(2,1)S(1)} custom-call(s32[1]{0:T(128)} %bitcast.core_ref, f32[64,50,128]{2,1,0:T(8,128)S(1)} %all-to-all-done.4.p_ref), custom_call_target="tpu_custom_call" | custom-call | flops 15728640000 | bytes 4096000 | tf_op jit(solution)/shard_map/source_polar/pallas_call | solution.py:250
  187.1 11.7 %rotate.1 = f32[4,640,640]{2,1,0:T(8,128)} custom-call(bf16[4,640,1920]{2,1,0:T(8,128)(2,1)} %half_rotated.1.h_ref, bf16[1920,640]{1,0:T(8,128)(2,1)S(1)} %source_polar.1.u_ref), custom_call_target="tpu_custom_call" | custom-call | flops 6291456000 | bytes 16384000 | tf_op jit(solution)/shard_map/rotate/pallas_call | solution.py:288
  (2 shorter events, 0.0 us)
Async XLA Ops:
  7.2 10.5 %copy-start.2 = (s32[1,16]{1,0:T(1,128)S(1)}, s32[1,16]{1,0:T(1,128)}, u32[]{:S(2)}) copy-start(s32[1,16]{1,0:T(1,128)} %param.8) | copy-start | bytes 196
  7.2 1.4 copy-start
  9.5 18.9 %all-to-all-start = ((f32[16,50,128]{2,1,0:T(8,128)}), f32[16,50,128]{2,1,0:T(8,128)S(1)}, u32[]{:S(2)}, u32[]{:S(2)}) async-start(f32[16,50,128]{2,1,0:T(8,128)} %cut.1), calls=%async_computation | async-start | bytes 917504 | tf_op jit(solution)/shard_map/all_to_all | solution.py:351
  30.4 32.8 %all-to-all-start.1 = ((f32[64,50,128]{2,1,0:T(8,128)}), f32[64,50,128]{2,1,0:T(8,128)S(1)}, u32[]{:S(2)}, u32[]{:S(2)}) async-start(f32[64,50,128]{2,1,0:T(8,128)} %gather_fusion), calls=%async_computation.1 | async-start | bytes 3670016 | tf_op jit(solution)/shard_map/all_to_all | solution.py:351
  37.9 92.4 %all-gather.3.cloned.1.call-start = ((), (), s32[]{:S(2)}) async-start(), calls=%async_computation.5 | async-start | bytes 2048000 | tf_op jit(solution)/shard_map/all_gather | solution.py:378
  82.2 3.9 %collective-permute-start = (f32[1600,128]{1,0:T(8,128)S(1)}, f32[1600,128]{1,0:T(8,128)S(1)}, u32[]{:S(2)}, u32[]{:S(2)}) collective-permute-start(f32[1600,128]{1,0:T(8,128)S(1)} %get-tuple-element.13), channel_id=1, source_target_pairs={{0,1},{1,0},{2,3},{3,2},{4,5},{5,4},{6,7},{7,6},{8,9},{9,8},{10,11... | collective-permute-start | bytes 2457608 | tf_op jit(solution)/shard_map/ppermute | solution.py:347
  105.0 1.5 collective-permute-start.1
  108.2 14.9 %all-to-all-start.3 = ((f32[16,50,128]{2,1,0:T(8,128)}), f32[16,50,128]{2,1,0:T(8,128)S(1)}, u32[]{:S(2)}, u32[]{:S(2)}) async-start(f32[16,50,128]{2,1,0:T(8,128)} %pair_up.1), calls=%async_computation.3 | async-start | bytes 917504 | tf_op jit(solution)/shard_map/all_to_all | solution.py:351
  125.0 41.0 %all-to-all-start.4 = ((f32[64,50,128]{2,1,0:T(8,128)}), f32[64,50,128]{2,1,0:T(8,128)S(1)}, u32[]{:S(2)}, u32[]{:S(2)}) async-start(f32[64,50,128]{2,1,0:T(8,128)} %gather_fusion.1), calls=%async_computation.4 | async-start | bytes 3670016 | tf_op jit(solution)/shard_map/all_to_all | solution.py:351
  130.3 1.4 copy-start.1
Sparse Core Ops, SparseCore 0:
  107.5 22.7 all-gather.2

commit v2 on v1

v2 whole, which is shorter than its diff:
```python
import functools
import math

import jax
import jax.numpy as jnp
from jax import lax
from jax.experimental import pallas as pl
from jax.experimental.pallas import tpu as pltpu
from jax.sharding import Mesh
from jax.sharding import PartitionSpec as P

POLAR = 5
SECTORS = 16
GROUPS = 8
EARLY = 2
LANES = 128
F32, BF16 = jnp.float32, jnp.bfloat16
VMEM_LIMIT = 48 << 20
WHOLE = pl.BlockSpec(memory_space=pltpu.VMEM)


def halves(v):
    high = v.astype(BF16)
    return high, (v - high.astype(F32)).astype(BF16)


def side_by_side(ref, a, b, c):
    n = a.shape[1]
    ref[:, 0:n] = a
    ref[:, n : 2 * n] = b
    ref[:, 2 * n : 3 * n] = c


def stacked(ref, a, b, c):
    n = a.shape[0]
    ref[0:n] = a
    ref[n : 2 * n] = b
    ref[2 * n : 3 * n] = c


def left_form(ref, v):
    high, low = halves(v)
    side_by_side(ref, high, high, low)


def right_form(ref, v):
    high, low = halves(v)
    stacked(ref, high, low, high)


def mm(a, b):
    return jnp.dot(a, b, preferred_element_type=F32)


def mm_nt(a, b):
    return lax.dot_general(a, b, (((1,), (1,)), ((), ())), preferred_element_type=F32)


def params():
    return pltpu.CompilerParams(vmem_limit_bytes=VMEM_LIMIT)


def cost(flops, nbytes):
    return pl.CostEstimate(flops=int(flops), bytes_accessed=int(nbytes), transcendentals=0)


def prepare_kernel(l_ref, r_ref, lo_ref, ro_ref):
    left_form(lo_ref.at[0], l_ref[0])
    right_form(ro_ref.at[0], r_ref[0])


def prepare(left, right):
    k, n, _ = left.shape
    block = pl.BlockSpec((1, n, n), lambda w: (w, 0, 0))
    return pl.pallas_call(
        prepare_kernel,
        grid=(k,),
        out_shape=(jax.ShapeDtypeStruct((k, n, 3 * n), BF16), jax.ShapeDtypeStruct((k, 3 * n, n), BF16)),
        in_specs=[block, block],
        out_specs=(pl.BlockSpec((1, n, 3 * n), lambda w: (w, 0, 0)), pl.BlockSpec((1, 3 * n, n), lambda w: (w, 0, 0))),
        compiler_params=params(),
        cost_estimate=cost(8 * k * n * n, 20 * k * n * n),
        name="prepare",
    )(left, right)


def tiles(n):
    return [(t, slice(t * LANES, (t + 1) * LANES)) for t in range(n // LANES)]


def lines_of(ref, v):
    count = v.shape[0]
    for t, lanes in tiles(v.shape[1]):
        ref[t * count : (t + 1) * count] = v[:, lanes]


def half_starts(core, half):
    return pl.multiple_of(core * half, half), pl.multiple_of((1 - core) * half, half)


def sigma_kernel(scalars, w_ref, l_ref, r_ref, own_ref, other_ref, w3, mid, acc, lines):
    step = pl.program_id(0)
    n = acc.shape[0]

    @pl.when(step == 0)
    def _():
        pieces, count, _ = w_ref.shape
        chips = pieces // SECTORS
        for piece in range(pieces):
            start = (piece % chips * SECTORS + piece // chips) * count
            lines[start : start + count] = w_ref[piece]
        part = n // chips
        for chip in range(chips):
            for t, lanes in tiles(n):
                start = chip * SECTORS * count + t * part
                high, low = halves(lines[start : start + part])
                for third, v in enumerate((high, low, high)):
                    w3[third * n + chip * part : third * n + (chip + 1) * part, lanes] = v

    @pl.when(step < scalars[0])
    def _():
        left_form(mid, mm(l_ref[0], w3[...]))
        term = mm(mid[...], r_ref[0])

        @pl.when(step == 0)
        def _():
            acc[...] = term

        @pl.when(step > 0)
        def _():
            acc[...] += term

    @pl.when(step == pl.num_programs(0) - 1)
    def _():
        chunk = n // GROUPS
        count = chunk * n // LANES
        for ref, start in zip((own_ref, other_ref), half_starts(scalars[1], n // 2), strict=True):
            for chip in range(GROUPS // 2):
                rows = pl.ds(pl.multiple_of(start + chip * chunk, chunk), chunk)
                lines_of(ref.at[chip * count : (chip + 1) * count], acc[rows])


def partial_sigma(scalars, pieces, left3, right3):
    k, n = left3.shape[:2]
    lines = n * n // LANES

    def active(w, s):
        return (jnp.minimum(w, s[0] - 1), 0, 0)

    return pl.pallas_call(
        sigma_kernel,
        out_shape=(jax.ShapeDtypeStruct((lines // 2, LANES), F32),) * 2,
        grid_spec=pltpu.PrefetchScalarGridSpec(
            num_scalar_prefetch=1,
            grid=(k,),
            in_specs=[
                pl.BlockSpec(pieces.shape, lambda w, s: (0, 0, 0)),
                pl.BlockSpec((1, n, 3 * n), active),
                pl.BlockSpec((1, 3 * n, n), active),
            ],
            out_specs=(pl.BlockSpec((lines // 2, LANES), lambda w, s: (0, 0)),) * 2,
            scratch_shapes=[
                pltpu.VMEM((3 * n, n), BF16),
                pltpu.VMEM((n, 3 * n), BF16),
                pltpu.VMEM((n, n), F32),
                pltpu.VMEM((lines, LANES), F32),
            ],
        ),
        compiler_params=params(),
        cost_estimate=cost(12 * k * n**3, 16 * k * n * n),
        name="partial_sigma",
    )(scalars, pieces, left3, right3)


def start_polar(core, mine, other, x):
    n = x.shape[0]
    total = jnp.sum(mine[...] * mine[...]) + jnp.sum(other[...] * other[...])
    factor = lax.rsqrt(n * (total / float(n * n)) + 1e-06) / 2.2
    chunk = n // GROUPS
    count = chunk * n // LANES
    for ref, start in zip((mine, other), half_starts(core, n // 2), strict=True):
        for chip in range(GROUPS // 2):
            rows = pl.ds(pl.multiple_of(start + chip * chunk, chunk), chunk)
            for t, lanes in tiles(n):
                first = chip * count + t * chunk
                x[rows, lanes] = ref[first : first + chunk] * factor


def iterate_polar(iterations, x, a, b, r):
    n = x.shape[0]

    def iteration(_, carry):
        high, low = halves(x[...])
        side_by_side(a, high, high, low)
        side_by_side(b, high, low, high)
        stacked(r, high, low, high)
        first = mm_nt(a[...], b[0:256])
        second = mm_nt(a[256:n], b[256:512])
        third = mm_nt(a[512:n], b[512:n])
        blocks_of = (
            (0, (first[0:256], first[256:n].T)),
            (256, (first[256:512], second[0:256], second[256 : n - 256].T)),
            (512, (first[512:n], second[256 : n - 256], third)),
        )
        for start, blocks in blocks_of:
            high, low = halves(jnp.concatenate(blocks, 1))
            side_by_side(a.at[start : start + high.shape[0]], high, high, low)
        x[...] = 1.5 * x[...] - 0.5 * mm(a[...], r[...])
        return carry

    lax.fori_loop(0, iterations, iteration, 0)


def polar_scratch(n):
    return [
        pltpu.VMEM((n, n), F32),
        pltpu.VMEM((n, 3 * n), BF16),
        pltpu.VMEM((n, 3 * n), BF16),
        pltpu.VMEM((3 * n, n), BF16),
    ]


def own_start_kernel(scalars, mine_ref, other_ref, o_ref, x, a, b, r):
    start_polar(scalars[0], mine_ref, other_ref, x)
    iterate_polar(EARLY, x, a, b, r)
    o_ref[...] = x[...]


def own_start(scalars, mine, other, n):
    return pl.pallas_call(
        own_start_kernel,
        grid=(1,),
        out_shape=jax.ShapeDtypeStruct((n, n), F32),
        in_specs=[pl.BlockSpec(memory_space=pltpu.SMEM), WHOLE, WHOLE],
        out_specs=pl.BlockSpec((n, n), lambda i: (0, 0)),
        scratch_shapes=polar_scratch(n),
        compiler_params=params(),
        cost_estimate=cost(EARLY * 12 * n**3, 8 * n * n),
        name="own_start",
    )(scalars, mine, other)


def own_finish_kernel(scalars, x_ref, l_ref, columns_ref, o_ref, x, a, b, r):
    @pl.when(pl.program_id(0) == 0)
    def _():
        x[...] = x_ref[...]
        iterate_polar(POLAR - EARLY, x, a, b, r)
        updated = (x[...] * math.sqrt(x.shape[0])).T
        left_form(a, updated)
        x[...] = updated
        width = columns_ref.shape[0]
        columns_ref[...] = x[pl.ds(pl.multiple_of(scalars[1] * width, width), width)]

    right_form(r, l_ref[0])
    left_form(o_ref.at[0], mm(a[...], r[...]))


def own_finish(scalars, iterate, left):
    k, n, _ = left.shape
    return pl.pallas_call(
        own_finish_kernel,
        out_shape=(jax.ShapeDtypeStruct((n // GROUPS, n), F32), jax.ShapeDtypeStruct((k, n, 3 * n), BF16)),
        grid_spec=pltpu.PrefetchScalarGridSpec(
            num_scalar_prefetch=1,
            grid=(k,),
            in_specs=[
                pl.BlockSpec((n, n), lambda w, s: (0, 0)),
                pl.BlockSpec((1, n, n), lambda w, s: (w, 0, 0)),
            ],
            out_specs=(
                pl.BlockSpec((n // GROUPS, n), lambda w, s: (0, 0)),
                pl.BlockSpec((1, n, 3 * n), lambda w, s: (w, 0, 0)),
            ),
            scratch_shapes=polar_scratch(n),
        ),
        compiler_params=params(),
        cost_estimate=cost(((POLAR - EARLY) * 12 + 6 * k) * n**3, 10 * k * n * n),
        name="own_finish",
    )(scalars, iterate, left)


def source_kernel(scalars, p_ref, h_ref, o_ref, x, a, b, r, mine, other):
    @pl.when(pl.program_id(0) == 0)
    def _():
        pieces, count, _ = p_ref.shape
        chips, part = pieces // SECTORS, count // 2
        for piece in range(pieces):
            start = (piece % chips * SECTORS + piece // chips) * part
            mine[start : start + part] = p_ref[piece, 0:part]
            other[start : start + part] = p_ref[piece, part:count]
        start_polar(scalars[0], mine, other, x)
        iterate_polar(POLAR, x, a, b, r)
        right_form(r, x[...] * math.sqrt(x.shape[0]))

    o_ref[0] = mm(h_ref[0], r[...])


def rotate_by_source(scalars, pieces, half3):
    k, n, _ = half3.shape
    half_lines = pltpu.VMEM((n * n // LANES // 2, LANES), F32)
    return pl.pallas_call(
        source_kernel,
        out_shape=jax.ShapeDtypeStruct((k, n, n), F32),
        grid_spec=pltpu.PrefetchScalarGridSpec(
            num_scalar_prefetch=1,
            grid=(k,),
            in_specs=[
                pl.BlockSpec(pieces.shape, lambda w, s: (0, 0, 0)),
                pl.BlockSpec((1, n, 3 * n), lambda w, s: (w, 0, 0)),
            ],
            out_specs=pl.BlockSpec((1, n, n), lambda w, s: (w, 0, 0)),
            scratch_shapes=polar_scratch(n) + [half_lines, half_lines],
        ),
        compiler_params=params(),
        cost_estimate=cost((POLAR * 12 + 6 * k) * n**3, 10 * k * n * n),
        name="rotate_by_source",
    )(scalars, pieces, half3)


def cut_kernel(scalars, w_ref, o_ref, part):
    lines_of(part, w_ref)
    pieces, count, _ = o_ref.shape
    for piece in range(pieces):
        o_ref[piece] = part[piece * count : (piece + 1) * count]


def cut(chip, block, chips):
    n = block.shape[0]
    rows = n // chips
    lines = rows * n // LANES
    piece_shape = (SECTORS, lines // SECTORS, LANES)
    return pl.pallas_call(
        cut_kernel,
        out_shape=jax.ShapeDtypeStruct(piece_shape, F32),
        grid_spec=pltpu.PrefetchScalarGridSpec(
            num_scalar_prefetch=1,
            grid=(1,),
            in_specs=[pl.BlockSpec((rows, n), lambda i, s: (s[0], 0))],
            out_specs=pl.BlockSpec(piece_shape, lambda i, s: (0, 0, 0)),
            scratch_shapes=[pltpu.VMEM((lines, LANES), F32)],
        ),
        compiler_params=params(),
        cost_estimate=cost(rows * n, 8 * rows * n),
        name="cut",
    )(chip, block)


def pair_kernel(mine_ref, other_ref, o_ref):
    pieces, count, _ = o_ref.shape
    part = count // 2
    for piece in range(pieces):
        lines = slice(piece * part, (piece + 1) * part)
        o_ref[piece, 0:part] = mine_ref[lines]
        o_ref[piece, part:count] = other_ref[lines]


def pair_up(mine, other):
    lines = mine.shape[0]
    return pl.pallas_call(
        pair_kernel,
        out_shape=jax.ShapeDtypeStruct((SECTORS, 2 * lines // SECTORS, LANES), F32),
        in_specs=[WHOLE, WHOLE],
        out_specs=WHOLE,
        compiler_params=params(),
        cost_estimate=cost(lines, 16 * lines * LANES),
        name="pair_up",
    )(mine, other)


def swap_cores(block):
    return lax.ppermute(block, "core", [(0, 1), (1, 0)])


def exchange(pieces, axes):
    return lax.all_to_all(pieces, axes, split_axis=0, concat_axis=0, tiled=True)


def deliver(spread, readers):
    return exchange(jnp.take(spread, readers, axis=0, mode="clip"), ("sector", "x"))


def shards(wavefunction, left_env, right_env, shift_map, op_counts):
    chips = lax.axis_size("x")
    chip, core = lax.axis_index("x"), lax.axis_index("core")
    group_here = chip * lax.axis_size("core") + core
    n = wavefunction.shape[1]
    lines = n * n // LANES
    scalars = jnp.stack([op_counts[0, 0], core.astype(jnp.int32)])
    readers = lax.all_gather(shift_map[0], "x").T.reshape(-1)
    left3, right3 = prepare(left_env[0], right_env[0])

    spread = exchange(cut(chip.astype(jnp.int32)[None], wavefunction[0], chips), "sector")
    moved = deliver(spread, readers)

    own, other = partial_sigma(scalars, moved, left3, right3)
    pair = (own + swap_cores(other)).reshape(chips, lines // 2 // chips, LANES)
    chunk = jnp.sum(exchange(pair, "x"), axis=0)

    other_chunk = swap_cores(chunk)
    spread = exchange(pair_up(chunk, other_chunk), "sector")

    where = jnp.stack([core, group_here]).astype(jnp.int32)
    mine = lax.all_gather(chunk, "x", tiled=True)
    early, spread = lax.optimization_barrier((own_start(where, mine, swap_cores(mine), n), spread))
    source_pieces = deliver(spread, readers)
    own_rows, half3 = own_finish(where, early, left_env[0])
    half3, source_pieces = lax.optimization_barrier((half3, source_pieces))
    rotated = rotate_by_source(where, source_pieces, half3)
    return (own_rows.T[None], rotated[None])


def solution(mesh):
    sectors, groups = mesh.devices.shape
    fine = Mesh(mesh.devices.reshape(sectors, groups // 2, 2), ("sector", "x", "core"))
    ops = ("x", "core")
    return jax.shard_map(
        shards,
        mesh=fine,
        in_specs=(
            P("sector", None, None),
            P("sector", ops, None, None),
            P("sector", ops, None, None),
            P(ops, None),
            P(ops, "sector"),
        ),
        out_specs=(P("sector", None, ops), P("sector", ops, None, None)),
        check_vma=False,
    )
```

time: 207 us -> 202 us (0.976)
  blocking collectives: 28.4 us -> 49.3 us
  between operations: 14.8 us -> 1.42 us
  waiting for transfers between devices: 28.2 us -> 19.1 us
  Pallas kernels: 100 us -> 94.9 us
    all_gather x0 -> x1, blocking collectives: none -> 14.3 us  [shards(): mine = lax.all_gather(chunk, 'x', tiled=True)]
    all_to_all x4, waiting for transfers between devices: 24.4 us -> 14.8 us  [exchange(): return lax.all_to_all(pieces, axes, split_axis=0, concat_axis=0, tiled=True)]
    all_to_all x1, blocking collectives: 18.8 us -> 25.3 us  [exchange(): return lax.all_to_all(pieces, axes, split_axis=0, concat_axis=0, tiled=True)]
    pallas_call x1, Pallas kernels: 19 us -> 13.8 us  [partial_sigma(): pl.pallas_call(sigma_kernel, out_shape=(jax.ShapeDtypeStruct((lines // 2,...]
    all_to_all x4, starting transfers between devices: 24.1 us -> 27.2 us  [exchange(): return lax.all_to_all(pieces, axes, split_axis=0, concat_axis=0, tiled=True)]
    ppermute x2 -> x3, waiting for transfers between devices: 3.4 us -> 4.36 us  [swap_cores(): return lax.ppermute(block, 'core', [(0, 1), (1, 0)])]
    pallas_call x5 -> x4, Pallas kernels: 68 us -> 67.9 us  [the longest x1 33 us: rotate_by_source(): pl.pallas_call(source_kernel, out_shape=jax.ShapeDtypeStruct((k, n, n), F...]
  transfers between devices with their start and end apart: 7 -> 7, of which waited for: 6 -> 6; matrix products, arithmetic and copies ran while one was open for 1% -> 0% of each run, Pallas kernels for 23% -> 24%
where the time goes in v2:
time: 202 us; the launch traced here: 201 us
  Pallas kernels  94.9 us (47%)
  blocking collectives  49.3 us (24%)
  starting transfers between devices  27.8 us (14%)
  waiting for transfers between devices  19.1 us (9%)
  local copies, waits for them, and re-layouts  8.01 us (4%)
    pallas_call x1, Pallas kernels, rotate_by_source(): pl.pallas_call(source_kernel, out_shape=jax.ShapeDtypeStruct((k, n, n), F...  33 us
    all_to_all x4, starting transfers between devices, exchange(): return lax.all_to_all(pieces, axes, split_axis=0, concat_axis=0, tiled=True)  27.2 us
    all_to_all x1, blocking collectives, exchange(): return lax.all_to_all(pieces, axes, split_axis=0, concat_axis=0, tiled=True)  25.3 us
    pallas_call x1, Pallas kernels, own_finish(): pl.pallas_call(own_finish_kernel, out_shape=(jax.ShapeDtypeStruct((n // G...  25.1 us
    all_to_all x4, waiting for transfers between devices, exchange(): return lax.all_to_all(pieces, axes, split_axis=0, concat_axis=0, tiled=True)  14.8 us
    all_gather x1, blocking collectives, shards(): mine = lax.all_gather(chunk, 'x', tiled=True)  14.3 us
    pallas_call x1, Pallas kernels, partial_sigma(): pl.pallas_call(sigma_kernel, out_shape=(jax.ShapeDtypeStruct((lines // 2,...  13.8 us
    pallas_call x1, Pallas kernels, prepare(): pl.pallas_call(prepare_kernel, grid=(k,), out_shape=(jax.ShapeDtypeStruct...  12.4 us
  transfers between devices with their start and end apart: 7, of which 6 were waited for; matrix products, arithmetic and copies ran while one was open for 0% of the time, Pallas kernels for 24%

profile of v2, /device:TPU:0, one launch (start us, length us, event | category | flops | bytes accessed | tf_op | source)
XLA Modules:
  0.0 200.8 jit_solution(18070001484474668865)
XLA Ops:
  0.6 0.0 copy-start.3
  0.6 0.0 copy-start
  0.7 1.4 copy-done
  2.1 0.8 cut.1
  2.9 8.1 %all-to-all-start = ((f32[16,50,128]{2,1,0:T(8,128)}), f32[16,50,128]{2,1,0:T(8,128)S(1)}, u32[]{:S(2)}, u32[]{:S(2)}) async-start(f32[16,50,128]{2,1,0:T(8,128)} %cut.1), calls=%async_computation | async-start | bytes 917504 | tf_op jit(solution)/shard_map/all_to_all | solution.py:375
  11.0 0.0 copy-done.3
  11.0 9.7 %all-gather = s32[4,1,16]{2,1,0:T(1,128)S(1)} all-gather(s32[1,1,16]{2,1,0:T(1,128)S(1)} %bitcast.23), channel_id=1, replica_groups=mesh['sector'=16,'x'=4,'core'=2] {'x'}, dimensions={0}, use_global_device_ids=true | all-gather | bytes 320 | tf_op jit(solution)/shard_map/all_gather | solution.py:389
  20.7 0.1 copy.9
  20.8 0.1 reshape.12
  20.9 0.9 all-to-all-done
  21.8 1.9 gather_fusion
  23.7 7.5 %all-to-all-start.1 = ((f32[64,50,128]{2,1,0:T(8,128)}), f32[64,50,128]{2,1,0:T(8,128)S(1)}, u32[]{:S(2)}, u32[]{:S(2)}) async-start(f32[64,50,128]{2,1,0:T(8,128)} %gather_fusion), calls=%async_computation.1 | async-start | bytes 3670016 | tf_op jit(solution)/shard_map/all_to_all | solution.py:375
  31.9 12.4 %prepare.1 = (bf16[4,640,1920]{2,1,0:T(8,128)(2,1)}, bf16[4,1920,640]{2,1,0:T(8,128)(2,1)}) custom-call(f32[4,640,640]{2,1,0:T(8,128)} %bitcast.19, f32[4,640,640]{2,1,0:T(8,128)} %bitcast.18), custom_call_target="tpu_custom_call" | custom-call | flops 13107200 | bytes 32768000 | tf_op jit(solution)/shard_map/prepare/pallas_call | solution.py:75
  44.3 0.1 pad_add_fusion.1.scalars
  44.3 12.2 %all-to-all-done.1.w_ref = f32[64,50,128]{2,1,0:T(8,128)S(1)} async-done(((f32[64,50,128]{2,1,0:T(8,128)}), f32[64,50,128]{2,1,0:T(8,128)S(1)}, u32[]{:S(2)}, u32[]{:S(2)}) %all-to-all-start.1) | async-done | bytes 1638432 | tf_op jit(solution)/shard_map/all_to_all | solution.py:375
  56.5 13.8 %partial_sigma.1 = (f32[1600,128]{1,0:T(8,128)S(1)}, f32[1600,128]{1,0:T(8,128)S(1)}) custom-call(s32[2]{0:T(128)S(1)} %pad_add_fusion.1.scalars, f32[64,50,128]{2,1,0:T(8,128)S(1)} %all-to-all-done.1.w_ref, bf16[4,640,1920]{2,1,0:T(8,128)(2,1)} %get-tuple-element.12.l_ref, bf16[4,1920,640]{2,1,0:T(8,128)(2,1)} %get-tuple-element.13.r_ref), custom_call_target="tpu_custom_call" | custom-call | flops 12582912000 | bytes 26214400 | tf_op jit(solution)/shard_map/partial_sigma/pallas_call | solution.py:150
  70.3 0.1 collective-permute-start
  70.4 2.3 %collective-permute-done = f32[1600,128]{1,0:T(8,128)S(1)} collective-permute-done((f32[1600,128]{1,0:T(8,128)S(1)}, f32[1600,128]{1,0:T(8,128)S(1)}, u32[]{:S(2)}, u32[]{:S(2)}) %collective-permute-start) | collective-permute-done | bytes 819232 | tf_op jit(solution)/shard_map/ppermute | solution.py:371
  72.7 0.1 add.7
  72.8 25.3 %all_to_all.25 = f32[4,400,128]{2,1,0:T(8,128)S(1)} all-to-all(f32[4,400,128]{2,1,0:T(8,128)S(1)} %bitcast.21), channel_id=1, replica_groups=mesh['sector'=16,'x'=4,'core'=2] {'x'}, dimensions={0} | all-to-all | bytes 1638400 | tf_op jit(solution)/shard_map/all_to_all | solution.py:375
  98.2 14.3 %all_gather.7.mine_ref = f32[1600,128]{1,0:T(8,128)S(1)} all-gather(f32[400,128]{1,0:T(8,128)S(1)} %reduce_sum.9.mine_ref), channel_id=1, replica_groups=mesh['sector'=16,'x'=4,'core'=2] {'x'}, dimensions={0}, use_global_device_ids=true | all-gather | bytes 1024000 | tf_op jit(solution)/shard_map/all_gather | solution.py:403
  112.5 0.0 collective-permute-start.1
  112.5 0.5 collective-permute-start.2
  113.0 0.1 pad_add_fusion.scalars
  113.1 2.0 %collective-permute-done.2.other_ref = f32[400,128]{1,0:T(8,128)S(1)} collective-permute-done((f32[400,128]{1,0:T(8,128)S(1)}, f32[400,128]{1,0:T(8,128)S(1)}, u32[]{:S(2)}, u32[]{:S(2)}) %collective-permute-start.2) | collective-permute-done | bytes 204832 | tf_op jit(solution)/shard_map/ppermute | solution.py:371
  115.1 0.8 pair_up.1
  115.9 3.6 %all-to-all-start.3 = ((f32[16,50,128]{2,1,0:T(8,128)}), f32[16,50,128]{2,1,0:T(8,128)S(1)}, u32[]{:S(2)}, u32[]{:S(2)}) async-start(f32[16,50,128]{2,1,0:T(8,128)} %pair_up.1), calls=%async_computation.3 | async-start | bytes 917504 | tf_op jit(solution)/shard_map/all_to_all | solution.py:375
  119.5 0.0 collective-permute-done.1.other_ref
  119.5 9.0 %own_start.1.x_ref = f32[640,640]{1,0:T(8,128)S(1)} custom-call(s32[2]{0:T(128)S(1)} %pad_add_fusion.scalars, f32[1600,128]{1,0:T(8,128)S(1)} %all_gather.7.mine_ref, f32[1600,128]{1,0:T(8,128)S(1)} %collective-permute-done.1.other_ref), custom_call_target="tpu_custom_call" | custom-call | flops 6291456000 | bytes 3276800 | tf_op jit(solution)/shard_map/own_start/pallas_call | solution.py:230
  128.6 0.0 copy-start.1
  128.6 1.2 copy-done.1
  129.8 1.1 all-to-all-done.3
  130.9 1.9 gather_fusion.1
  132.8 8.0 %all-to-all-start.4 = ((f32[64,50,128]{2,1,0:T(8,128)}), f32[64,50,128]{2,1,0:T(8,128)S(1)}, u32[]{:S(2)}, u32[]{:S(2)}) async-start(f32[64,50,128]{2,1,0:T(8,128)} %gather_fusion.1), calls=%async_computation.4 | async-start | bytes 3670016 | tf_op jit(solution)/shard_map/all_to_all | solution.py:375
  140.8 0.0 copy-start.2
  140.8 1.4 copy-done.2
  142.3 25.1 %own_finish.1 = (f32[80,640]{1,0:T(8,128)}, bf16[4,640,1920]{2,1,0:T(8,128)(2,1)}) custom-call(s32[2]{0:T(128)S(1)} %pad_add_fusion.scalars, f32[640,640]{1,0:T(8,128)S(1)} %copy-done.2, f32[4,640,640]{2,1,0:T(8,128)} %bitcast.20), custom_call_target="tpu_custom_call" | custom-call | flops 15728640000 | bytes 16384000 | tf_op jit(solution)/shard_map/own_finish/pallas_call | solution.py:260
  167.3 0.5 all-to-all-done.4.p_ref
  167.9 33.0 %rotate_by_source.1 = f32[4,640,640]{2,1,0:T(8,128)} custom-call(s32[2]{0:T(128)S(1)} %pad_add_fusion.scalars, f32[64,50,128]{2,1,0:T(8,128)S(1)} %all-to-all-done.4.p_ref, bf16[4,640,1920]{2,1,0:T(8,128)(2,1)} %get-tuple-element.21.h_ref), custom_call_target="tpu_custom_call" | custom-call | flops 22020096000 | bytes 16384000 | tf_op jit(solution)/shard_map/rotate_by_source/pallas_call | solution.py:301
  (2 shorter events, 0.0 us)
Async XLA Ops:
  0.6 10.4 %copy-start.3 = (s32[1,16]{1,0:T(1,128)S(1)}, s32[1,16]{1,0:T(1,128)}, u32[]{:S(2)}) copy-start(s32[1,16]{1,0:T(1,128)} %param.8) | copy-start | bytes 196
  0.6 1.4 copy-start
  2.9 18.9 %all-to-all-start = ((f32[16,50,128]{2,1,0:T(8,128)}), f32[16,50,128]{2,1,0:T(8,128)S(1)}, u32[]{:S(2)}, u32[]{:S(2)}) async-start(f32[16,50,128]{2,1,0:T(8,128)} %cut.1), calls=%async_computation | async-start | bytes 917504 | tf_op jit(solution)/shard_map/all_to_all | solution.py:375
  23.7 32.8 %all-to-all-start.1 = ((f32[64,50,128]{2,1,0:T(8,128)}), f32[64,50,128]{2,1,0:T(8,128)S(1)}, u32[]{:S(2)}, u32[]{:S(2)}) async-start(f32[64,50,128]{2,1,0:T(8,128)} %gather_fusion), calls=%async_computation.1 | async-start | bytes 3670016 | tf_op jit(solution)/shard_map/all_to_all | solution.py:375
  70.3 2.4 %collective-permute-start = (f32[1600,128]{1,0:T(8,128)S(1)}, f32[1600,128]{1,0:T(8,128)S(1)}, u32[]{:S(2)}, u32[]{:S(2)}) collective-permute-start(f32[1600,128]{1,0:T(8,128)S(1)} %get-tuple-element.15), channel_id=1, source_target_pairs={{0,1},{1,0},{2,3},{3,2},{4,5},{5,4},{6,7},{7,6},{8,9},{9,8},{10,11... | collective-permute-start | bytes 2457608 | tf_op jit(solution)/shard_map/ppermute | solution.py:371
  112.5 7.0 %collective-permute-start.1 = (f32[1600,128]{1,0:T(8,128)S(1)}, f32[1600,128]{1,0:T(8,128)S(1)}, u32[]{:S(2)}, u32[]{:S(2)}) collective-permute-start(f32[1600,128]{1,0:T(8,128)S(1)} %all_gather.7.mine_ref), channel_id=1, source_target_pairs={{0,1},{1,0},{2,3},{3,2},{4,5},{5,4},{6,7},{7,6},{8,9},{9,8},{10,11... | collective-permute-start | bytes 2457608 | tf_op jit(solution)/shard_map/ppermute | solution.py:371
  112.5 2.6 %collective-permute-start.2 = (f32[400,128]{1,0:T(8,128)S(1)}, f32[400,128]{1,0:T(8,128)S(1)}, u32[]{:S(2)}, u32[]{:S(2)}) collective-permute-start(f32[400,128]{1,0:T(8,128)S(1)} %reduce_sum.9.mine_ref), channel_id=1, source_target_pairs={{0,1},{1,0},{2,3},{3,2},{4,5},{5,4},{6,7},{7,6},{8,9},{9,8},{10,11... | collective-permute-start | bytes 614408 | tf_op jit(solution)/shard_map/ppermute | solution.py:371
  115.9 14.9 %all-to-all-start.3 = ((f32[16,50,128]{2,1,0:T(8,128)}), f32[16,50,128]{2,1,0:T(8,128)S(1)}, u32[]{:S(2)}, u32[]{:S(2)}) async-start(f32[16,50,128]{2,1,0:T(8,128)} %pair_up.1), calls=%async_computation.3 | async-start | bytes 917504 | tf_op jit(solution)/shard_map/all_to_all | solution.py:375
  128.6 1.2 copy-start.1
  132.8 35.1 %all-to-all-start.4 = ((f32[64,50,128]{2,1,0:T(8,128)}), f32[64,50,128]{2,1,0:T(8,128)S(1)}, u32[]{:S(2)}, u32[]{:S(2)}) async-start(f32[64,50,128]{2,1,0:T(8,128)} %gather_fusion.1), calls=%async_computation.4 | async-start | bytes 3670016 | tf_op jit(solution)/shard_map/all_to_all | solution.py:375
  140.8 1.4 copy-start.2

commit v3 on v2

--- a/solution.py
+++ b/solution.py
@@ -16,6 +16,7 @@
 LANES = 128
 F32, BF16 = jnp.float32, jnp.bfloat16
 VMEM_LIMIT = 48 << 20
+ALL_VMEM = 58 << 20
 WHOLE = pl.BlockSpec(memory_space=pltpu.VMEM)
 
 
@@ -56,16 +57,17 @@
     return lax.dot_general(a, b, (((1,), (1,)), ((), ())), preferred_element_type=F32)
 
 
-def params():
-    return pltpu.CompilerParams(vmem_limit_bytes=VMEM_LIMIT)
+def params(limit=VMEM_LIMIT):
+    return pltpu.CompilerParams(vmem_limit_bytes=limit)
 
 
 def cost(flops, nbytes):
     return pl.CostEstimate(flops=int(flops), bytes_accessed=int(nbytes), transcendentals=0)
 
 
-def prepare_kernel(l_ref, r_ref, lo_ref, ro_ref):
+def prepare_kernel(l_ref, r_ref, lo_ref, ro_ref, ls_ref):
     left_form(lo_ref.at[0], l_ref[0])
+    right_form(ls_ref, l_ref[0])
     right_form(ro_ref.at[0], r_ref[0])
 
 
@@ -75,11 +77,19 @@
     return pl.pallas_call(
         prepare_kernel,
         grid=(k,),
-        out_shape=(jax.ShapeDtypeStruct((k, n, 3 * n), BF16), jax.ShapeDtypeStruct((k, 3 * n, n), BF16)),
+        out_shape=(
+            jax.ShapeDtypeStruct((k, n, 3 * n), BF16),
+            jax.ShapeDtypeStruct((k, 3 * n, n), BF16),
+            jax.ShapeDtypeStruct((3 * n, k * n), BF16),
+        ),
         in_specs=[block, block],
-        out_specs=(pl.BlockSpec((1, n, 3 * n), lambda w: (w, 0, 0)), pl.BlockSpec((1, 3 * n, n), lambda w: (w, 0, 0))),
+        out_specs=(
+            pl.BlockSpec((1, n, 3 * n), lambda w: (w, 0, 0)),
+            pl.BlockSpec((1, 3 * n, n), lambda w: (w, 0, 0)),
+            pl.BlockSpec((3 * n, n), lambda w: (0, w)),
+        ),
         compiler_params=params(),
-        cost_estimate=cost(8 * k * n * n, 20 * k * n * n),
+        cost_estimate=cost(12 * k * n * n, 26 * k * n * n),
         name="prepare",
     )(left, right)
 
@@ -186,29 +196,69 @@
                 x[rows, lanes] = ref[first : first + chunk] * factor
 
 
-def iterate_polar(iterations, x, a, b, r):
+def symmetric_rows(a, b):
+    n = a.shape[0]
+    first = mm_nt(a[...], b[0:256])
+    second = mm_nt(a[256:n], b[256:512])
+    third = mm_nt(a[512:n], b[512:n])
+    return (
+        (slice(0, 256), jnp.concatenate((first[0:256], first[256:n].T), 1)),
+        (slice(256, 512), jnp.concatenate((first[256:512], second[0:256], second[256 : n - 256].T), 1)),
+        (slice(512, n), jnp.concatenate((first[512:n], second[256 : n - 256], third), 1)),
+    )
+
+
+def split_iterate(x, a, b, r):
+    high, low = halves(x[...])
+    side_by_side(a, high, high, low)
+    side_by_side(b, high, low, high)
+    stacked(r, high, low, high)
+
+
+def iterate_once(x, a, b, r):
+    split_iterate(x, a, b, r)
+    for rows, v in symmetric_rows(a, b):
+        left_form(a.at[rows], v)
+    x[...] = 1.5 * x[...] - 0.5 * mm(a[...], r[...])
+
+
+def iterate_twice(x, a, b, r, g):
+    split_iterate(x, a, b, r)
+    for rows, v in symmetric_rows(a, b):
+        g[rows] = v
+    high, low = halves(g[...])
+    side_by_side(a, high, high, low)
+    side_by_side(b, high, low, high)
     n = x.shape[0]
-
-    def iteration(_, carry):
-        high, low = halves(x[...])
-        side_by_side(a, high, high, low)
-        side_by_side(b, high, low, high)
-        stacked(r, high, low, high)
-        first = mm_nt(a[...], b[0:256])
-        second = mm_nt(a[256:n], b[256:512])
-        third = mm_nt(a[512:n], b[512:n])
-        blocks_of = (
-            (0, (first[0:256], first[256:n].T)),
-            (256, (first[256:512], second[0:256], second[256 : n - 256].T)),
-            (512, (first[512:n], second[256 : n - 256], third)),
-        )
-        for start, blocks in blocks_of:
-            high, low = halves(jnp.concatenate(blocks, 1))
-            side_by_side(a.at[start : start + high.shape[0]], high, high, low)
-        x[...] = 1.5 * x[...] - 0.5 * mm(a[...], r[...])
+    for rows, q in symmetric_rows(a, b):
+        gram = g[rows]
+        left_form(a.at[rows], q)
+        high, low = halves(0.0625 * q - 0.5625 * gram)
+        side_by_side(b.at[rows], high, low, high)
+        row = lax.broadcasted_iota(jnp.int32, q.shape, 0) + rows.start
+        diagonal = row == lax.broadcasted_iota(jnp.int32, q.shape, 1)
+        g[rows] = 1.6875 * q - 2.4375 * gram + jnp.where(diagonal, 2.25, 0.0)
+    for rows, v in symmetric_rows(a, b):
+        left_form(a.at[rows], g[rows] + v)
+    x[...] = mm(a[...], r[...])
+
+
+def iterate_polar(iterations, x, a, b, r, g):
+    def twice(_, carry):
+        iterate_twice(x, a, b, r, g)
         return carry
 
-    lax.fori_loop(0, iterations, iteration, 0)
+    lax.fori_loop(0, iterations // 2, twice, 0)
+    if iterations % 2:
+        iterate_once(x, a, b, r)
+
+
+def iterate_singly(iterations, x, a, b, r):
+    def once(_, carry):
+        iterate_once(x, a, b, r)
+        return carry
+
+    lax.fori_loop(0, iterations, once, 0)
 
 
 def polar_scratch(n):
@@ -217,108 +267,152 @@
         pltpu.VMEM((n, 3 * n), BF16),
         pltpu.VMEM((n, 3 * n), BF16),
         pltpu.VMEM((3 * n, n), BF16),
+        pltpu.VMEM((n, n), F32),
     ]
 
 
-def own_start_kernel(scalars, mine_ref, other_ref, o_ref, x, a, b, r):
+def own_start_kernel(scalars, mine_ref, other_ref, o_ref, x, a, b, r, g, sem):
     start_polar(scalars[0], mine_ref, other_ref, x)
-    iterate_polar(EARLY, x, a, b, r)
-    o_ref[...] = x[...]
+    iterate_singly(EARLY, x, a, b, r)
+    copy = pltpu.make_async_copy(x, o_ref, sem)
+    copy.start()
+    copy.wait()
 
 
 def own_start(scalars, mine, other, n):
     return pl.pallas_call(
         own_start_kernel,
-        grid=(1,),
         out_shape=jax.ShapeDtypeStruct((n, n), F32),
         in_specs=[pl.BlockSpec(memory_space=pltpu.SMEM), WHOLE, WHOLE],
-        out_specs=pl.BlockSpec((n, n), lambda i: (0, 0)),
-        scratch_shapes=polar_scratch(n),
-        compiler_params=params(),
+        out_specs=pl.BlockSpec(memory_space=pltpu.HBM),
+        scratch_shapes=polar_scratch(n) + [pltpu.SemaphoreType.DMA],
+        compiler_params=params(ALL_VMEM),
         cost_estimate=cost(EARLY * 12 * n**3, 8 * n * n),
         name="own_start",
     )(scalars, mine, other)
 
 
-def own_finish_kernel(scalars, x_ref, l_ref, columns_ref, o_ref, x, a, b, r):
-    @pl.when(pl.program_id(0) == 0)
-    def _():
-        x[...] = x_ref[...]
-        iterate_polar(POLAR - EARLY, x, a, b, r)
-        updated = (x[...] * math.sqrt(x.shape[0])).T
-        left_form(a, updated)
-        x[...] = updated
-        width = columns_ref.shape[0]
-        columns_ref[...] = x[pl.ds(pl.multiple_of(scalars[1] * width, width), width)]
-
-    right_form(r, l_ref[0])
-    left_form(o_ref.at[0], mm(a[...], r[...]))
-
-
-def own_finish(scalars, iterate, left):
-    k, n, _ = left.shape
+def own_finish_kernel(scalars, x_ref, l_ref, columns_ref, o_ref, x, a, b, r, g, blocks, result, sems, out_sems):
+    n = x.shape[0]
+    steps, _, width = blocks.shape
+    state = pltpu.make_async_copy(x_ref, x, sems.at[steps])
+    state.start()
+    reads = [
+        pltpu.make_async_copy(l_ref.at[:, pl.ds(step * width, width)], blocks.at[step], sems.at[step])
+        for step in range(steps)
+    ]
+    for read in reads:
+        read.start()
+    state.wait()
+    iterate_singly(POLAR - EARLY, x, a, b, r)
+    updated = (x[...] * math.sqrt(n)).T
+    left_form(a, updated)
+    x[...] = updated
+    count = columns_ref.shape[0]
+    columns_ref[...] = x[pl.ds(pl.multiple_of(scalars[1] * count, count), count)]
+    per_step = width // n
+
+    def write(w):
+        return pltpu.make_async_copy(result.at[w], o_ref.at[w], out_sems.at[w])
+
+    def pair(step, carry):
+        columns = pl.ds(pl.multiple_of(step * width, width), width)
+        pltpu.make_async_copy(l_ref.at[:, columns], blocks.at[step], sems.at[step]).wait()
+        product = mm(a[...], blocks[step])
+        for k in range(per_step):
+            w = step * per_step + k
+            left_form(result.at[w], product[:, k * n : (k + 1) * n])
+            write(w).start()
+        return carry
+
+    lax.fori_loop(0, steps, pair, 0)
+    for w in range(steps * per_step):
+        write(w).wait()
+
+
+def own_finish(scalars, iterate, stacked_left):
+    n = iterate.shape[0]
+    k = stacked_left.shape[1] // n
+    hbm = pl.BlockSpec(memory_space=pltpu.HBM)
     return pl.pallas_call(
         own_finish_kernel,
         out_shape=(jax.ShapeDtypeStruct((n // GROUPS, n), F32), jax.ShapeDtypeStruct((k, n, 3 * n), BF16)),
-        grid_spec=pltpu.PrefetchScalarGridSpec(
-            num_scalar_prefetch=1,
-            grid=(k,),
-            in_specs=[
-                pl.BlockSpec((n, n), lambda w, s: (0, 0)),
-                pl.BlockSpec((1, n, n), lambda w, s: (w, 0, 0)),
-            ],
-            out_specs=(
-                pl.BlockSpec((n // GROUPS, n), lambda w, s: (0, 0)),
-                pl.BlockSpec((1, n, 3 * n), lambda w, s: (w, 0, 0)),
-            ),
-            scratch_shapes=polar_scratch(n),
-        ),
+        in_specs=[pl.BlockSpec(memory_space=pltpu.SMEM), hbm, hbm],
+        out_specs=(WHOLE, hbm),
+        scratch_shapes=polar_scratch(n)
+        + [
+            pltpu.VMEM((k // 2, 3 * n, 2 * n), BF16),
+            pltpu.VMEM((k, n, 3 * n), BF16),
+            pltpu.SemaphoreType.DMA((k // 2 + 1,)),
+            pltpu.SemaphoreType.DMA((k,)),
+        ],
         compiler_params=params(),
-        cost_estimate=cost(((POLAR - EARLY) * 12 + 6 * k) * n**3, 10 * k * n * n),
+        cost_estimate=cost(((POLAR - EARLY) * 12 + 6 * k) * n**3, 14 * k * n * n),
         name="own_finish",
-    )(scalars, iterate, left)
-
-
-def source_kernel(scalars, p_ref, h_ref, o_ref, x, a, b, r, mine, other):
-    @pl.when(pl.program_id(0) == 0)
-    def _():
-        pieces, count, _ = p_ref.shape
-        chips, part = pieces // SECTORS, count // 2
-        for piece in range(pieces):
-            start = (piece % chips * SECTORS + piece // chips) * part
-            mine[start : start + part] = p_ref[piece, 0:part]
-            other[start : start + part] = p_ref[piece, part:count]
-        start_polar(scalars[0], mine, other, x)
-        iterate_polar(POLAR, x, a, b, r)
-        right_form(r, x[...] * math.sqrt(x.shape[0]))
-
-    o_ref[0] = mm(h_ref[0], r[...])
+    )(scalars, iterate, stacked_left)
+
+
+def source_kernel(scalars, p_ref, h_ref, o_ref, x, a, b, r, g, mine, other, blocks, result, sems, out_sems):
+    n = x.shape[0]
+    operators = blocks.shape[0]
+    reads = [pltpu.make_async_copy(h_ref.at[w], blocks.at[w], sems.at[w]) for w in range(operators)]
+    for read in reads:
+        read.start()
+    pieces, count, _ = p_ref.shape
+    chips, part = pieces // SECTORS, count // 2
+    for piece in range(pieces):
+        start = (piece % chips * SECTORS + piece // chips) * part
+        mine[start : start + part] = p_ref[piece, 0:part]
+        other[start : start + part] = p_ref[piece, part:count]
+    start_polar(scalars[0], mine, other, x)
+    iterate_polar(POLAR, x, a, b, r, g)
+    right_form(r, x[...] * math.sqrt(n))
+
+    def write(w):
+        return pltpu.make_async_copy(result.at[w], o_ref.at[w], out_sems.at[w])
+
+    def operator(w, carry):
+        pltpu.make_async_copy(h_ref.at[w], blocks.at[w], sems.at[w]).wait()
+        result[w] = mm(blocks[w], r[...])
+        write(w).start()
+        return carry
+
+    lax.fori_loop(0, operators, operator, 0)
+    for w in range(operators):
+        write(w).wait()
 
 
 def rotate_by_source(scalars, pieces, half3):
     k, n, _ = half3.shape
     half_lines = pltpu.VMEM((n * n // LANES // 2, LANES), F32)
+    hbm = pl.BlockSpec(memory_space=pltpu.HBM)
     return pl.pallas_call(
         source_kernel,
         out_shape=jax.ShapeDtypeStruct((k, n, n), F32),
-        grid_spec=pltpu.PrefetchScalarGridSpec(
-            num_scalar_prefetch=1,
-            grid=(k,),
-            in_specs=[
-                pl.BlockSpec(pieces.shape, lambda w, s: (0, 0, 0)),
-                pl.BlockSpec((1, n, 3 * n), lambda w, s: (w, 0, 0)),
-            ],
-            out_specs=pl.BlockSpec((1, n, n), lambda w, s: (w, 0, 0)),
-            scratch_shapes=polar_scratch(n) + [half_lines, half_lines],
-        ),
+        in_specs=[pl.BlockSpec(memory_space=pltpu.SMEM), WHOLE, hbm],
+        out_specs=hbm,
+        scratch_shapes=polar_scratch(n)
+        + [
+            half_lines,
+            half_lines,
+            pltpu.VMEM((k, n, 3 * n), BF16),
+            pltpu.VMEM((k, n, n), F32),
+            pltpu.SemaphoreType.DMA((k,)),
+            pltpu.SemaphoreType.DMA((k,)),
+        ],
         compiler_params=params(),
         cost_estimate=cost((POLAR * 12 + 6 * k) * n**3, 10 * k * n * n),
         name="rotate_by_source",
     )(scalars, pieces, half3)
 
 
-def cut_kernel(scalars, w_ref, o_ref, part):
-    lines_of(part, w_ref)
+def cut_kernel(chip_ref, w_ref, o_ref, block, part, sem):
+    rows = block.shape[0]
+    here = pl.ds(pl.multiple_of(chip_ref[0] * rows, rows), rows)
+    copy = pltpu.make_async_copy(w_ref.at[here], block, sem)
+    copy.start()
+    copy.wait()
+    lines_of(part, block)
     pieces, count, _ = o_ref.shape
     for piece in range(pieces):
         o_ref[piece] = part[piece * count : (piece + 1) * count]
@@ -328,18 +422,13 @@
     n = block.shape[0]
     rows = n // chips
     lines = rows * n // LANES
-    piece_shape = (SECTORS, lines // SECTORS, LANES)
     return pl.pallas_call(
         cut_kernel,
-        out_shape=jax.ShapeDtypeStruct(piece_shape, F32),
-        grid_spec=pltpu.PrefetchScalarGridSpec(
-            num_scalar_prefetch=1,
-            grid=(1,),
-            in_specs=[pl.BlockSpec((rows, n), lambda i, s: (s[0], 0))],
-            out_specs=pl.BlockSpec(piece_shape, lambda i, s: (0, 0, 0)),
-            scratch_shapes=[pltpu.VMEM((lines, LANES), F32)],
-        ),
-        compiler_params=params(),
+        out_shape=jax.ShapeDtypeStruct((SECTORS, lines // SECTORS, LANES), F32),
+        in_specs=[pl.BlockSpec(memory_space=pltpu.SMEM), pl.BlockSpec(memory_space=pltpu.HBM)],
+        out_specs=WHOLE,
+        scratch_shapes=[pltpu.VMEM((rows, n), F32), pltpu.VMEM((lines, LANES), F32), pltpu.SemaphoreType.DMA],
+        compiler_params=params(ALL_VMEM),
         cost_estimate=cost(rows * n, 8 * rows * n),
         name="cut",
     )(chip, block)
@@ -387,7 +476,7 @@
     lines = n * n // LANES
     scalars = jnp.stack([op_counts[0, 0], core.astype(jnp.int32)])
     readers = lax.all_gather(shift_map[0], "x").T.reshape(-1)
-    left3, right3 = prepare(left_env[0], right_env[0])
+    left3, right3, stacked_left = prepare(left_env[0], right_env[0])
 
     spread = exchange(cut(chip.astype(jnp.int32)[None], wavefunction[0], chips), "sector")
     moved = deliver(spread, readers)
@@ -403,7 +492,7 @@
     mine = lax.all_gather(chunk, "x", tiled=True)
     early, spread = lax.optimization_barrier((own_start(where, mine, swap_cores(mine), n), spread))
     source_pieces = deliver(spread, readers)
-    own_rows, half3 = own_finish(where, early, left_env[0])
+    own_rows, half3 = own_finish(where, early, stacked_left)
     half3, source_pieces = lax.optimization_barrier((half3, source_pieces))
     rotated = rotate_by_source(where, source_pieces, half3)
     return (own_rows.T[None], rotated[None])

time: 202 us -> 200 us (0.990)
  Pallas kernels: 94.9 us -> 89.1 us
  blocking collectives: 49.3 us -> 53.1 us
  local copies, waits for them, and re-layouts: 8.01 us -> 4.88 us
  starting transfers between devices: 27.8 us -> 30.7 us
    pallas_call x1, Pallas kernels: 13.8 us -> 8.71 us  [partial_sigma(): pl.pallas_call(sigma_kernel, out_shape=(jax.ShapeDtypeStruct((lines // 2,...]
    all_to_all x1, blocking collectives: 25.3 us -> 29.1 us  [exchange(): return lax.all_to_all(pieces, axes, split_axis=0, concat_axis=0, tiled=True)]
    unnamed x8 -> x10, local copies, waits for them, and re-layouts: 4.04 us -> 0.91 us
    pallas_call x2, Pallas kernels: 9.87 us -> 12.8 us  [the longest x1 11 us: own_start(): pl.pallas_call(own_start_kernel, out_shape=jax.ShapeDtypeStruct((n, n), F...]
    pallas_call x1, Pallas kernels: 33 us -> 30.2 us  [rotate_by_source(): pl.pallas_call(source_kernel, out_shape=jax.ShapeDtypeStruct((k, n, n), F...]
    pallas_call x1, Pallas kernels: 25.1 us -> 22.5 us  [own_finish(): pl.pallas_call(own_finish_kernel, out_shape=(jax.ShapeDtypeStruct((n // G...]
  transfers between devices with their start and end apart: 7 -> 7, of which waited for: 6 -> 5; matrix products, arithmetic and copies ran while one was open for 0% -> 0% of each run, Pallas kernels for 24% -> 24%
where the time goes in v3:
time: 200 us
  Pallas kernels  89.1 us (45%)
  blocking collectives  53.1 us (27%)
  starting transfers between devices  30.7 us (15%)
  waiting for transfers between devices  19.6 us (10%)
  local copies, waits for them, and re-layouts  4.88 us (2%)
    pallas_call x1, Pallas kernels, rotate_by_source(): pl.pallas_call(source_kernel, out_shape=jax.ShapeDtypeStruct((k, n, n), F...  30.2 us
    all_to_all x1, blocking collectives, exchange(): return lax.all_to_all(pieces, axes, split_axis=0, concat_axis=0, tiled=True)  29.1 us
    all_to_all x4, starting transfers between devices, exchange(): return lax.all_to_all(pieces, axes, split_axis=0, concat_axis=0, tiled=True)  28.3 us
    pallas_call x1, Pallas kernels, own_finish(): pl.pallas_call(own_finish_kernel, out_shape=(jax.ShapeDtypeStruct((n // G...  22.5 us
    all_to_all x4, waiting for transfers between devices, exchange(): return lax.all_to_all(pieces, axes, split_axis=0, concat_axis=0, tiled=True)  16.1 us
    all_gather x1, blocking collectives, shards(): mine = lax.all_gather(chunk, 'x', tiled=True)  14.3 us
    pallas_call x1, Pallas kernels, prepare(): pl.pallas_call(prepare_kernel, grid=(k,), out_shape=(jax.ShapeDtypeStruct...  14 us
    pallas_call x1, Pallas kernels, own_start(): pl.pallas_call(own_start_kernel, out_shape=jax.ShapeDtypeStruct((n, n), F...  11 us
  transfers between devices with their start and end apart: 7, of which 5 were waited for; matrix products, arithmetic and copies ran while one was open for 0% of the time, Pallas kernels for 24%

profile of v3, /device:TPU:0, one launch (start us, length us, event | category | flops | bytes accessed | tf_op | source)
XLA Modules:
  0.0 199.9 jit_solution(396966054373574920)
XLA Ops:
  0.6 0.0 copy-start.3
  0.6 1.8 cut.1
  2.5 8.1 %all-to-all-start = ((f32[16,50,128]{2,1,0:T(8,128)}), f32[16,50,128]{2,1,0:T(8,128)S(1)}, u32[]{:S(2)}, u32[]{:S(2)}) async-start(f32[16,50,128]{2,1,0:T(8,128)} %cut.1), calls=%async_computation | async-start | bytes 917504 | tf_op jit(solution)/shard_map/all_to_all | solution.py:464
  10.6 0.0 copy-done.3
  10.6 9.7 %all-gather = s32[4,1,16]{2,1,0:T(1,128)S(1)} all-gather(s32[1,1,16]{2,1,0:T(1,128)S(1)} %bitcast.22), channel_id=1, replica_groups=mesh['sector'=16,'x'=4,'core'=2] {'x'}, dimensions={0}, use_global_device_ids=true | all-gather | bytes 320 | tf_op jit(solution)/shard_map/all_gather | solution.py:478
  20.3 0.1 copy.9
  20.4 0.1 reshape.12
  20.5 0.9 all-to-all-done
  21.4 1.9 gather_fusion
  23.3 7.5 %all-to-all-start.1 = ((f32[64,50,128]{2,1,0:T(8,128)}), f32[64,50,128]{2,1,0:T(8,128)S(1)}, u32[]{:S(2)}, u32[]{:S(2)}) async-start(f32[64,50,128]{2,1,0:T(8,128)} %gather_fusion), calls=%async_computation.1 | async-start | bytes 3670016 | tf_op jit(solution)/shard_map/all_to_all | solution.py:464
  31.5 14.0 %prepare.1 = (bf16[4,640,1920]{2,1,0:T(8,128)(2,1)}, bf16[4,1920,640]{2,1,0:T(8,128)(2,1)}, bf16[1920,2560]{1,0:T(8,128)(2,1)}) custom-call(f32[4,640,640]{2,1,0:T(8,128)} %bitcast.17, f32[4,640,640]{2,1,0:T(8,128)} %bitcast.18), custom_call_target="tpu_custom_call" | custom-call | flops 19660800 | bytes 42598400 | tf_op jit(solution)/shard_map/prepare/pallas_call | solution.py:77
  45.5 0.1 pad_add_fusion.1.scalars
  45.6 10.5 %all-to-all-done.1.w_ref = f32[64,50,128]{2,1,0:T(8,128)S(1)} async-done(((f32[64,50,128]{2,1,0:T(8,128)}), f32[64,50,128]{2,1,0:T(8,128)S(1)}, u32[]{:S(2)}, u32[]{:S(2)}) %all-to-all-start.1) | async-done | bytes 1638432 | tf_op jit(solution)/shard_map/all_to_all | solution.py:464
  56.1 8.7 %partial_sigma.1 = (f32[1600,128]{1,0:T(8,128)S(1)}, f32[1600,128]{1,0:T(8,128)S(1)}) custom-call(s32[2]{0:T(128)S(1)} %pad_add_fusion.1.scalars, f32[64,50,128]{2,1,0:T(8,128)S(1)} %all-to-all-done.1.w_ref, bf16[4,640,1920]{2,1,0:T(8,128)(2,1)} %get-tuple-element.13.l_ref, bf16[4,1920,640]{2,1,0:T(8,128)(2,1)} %get-tuple-element.14.r_ref), custom_call_target="tpu_custom_call" | custom-call | flops 12582912000 | bytes 26214400 | tf_op jit(solution)/shard_map/partial_sigma/pallas_call | solution.py:160
  64.9 1.9 collective-permute-start
  66.8 2.0 collective-permute-done
  68.7 0.1 add.7
  68.8 29.1 %all_to_all.25 = f32[4,400,128]{2,1,0:T(8,128)S(1)} all-to-all(f32[4,400,128]{2,1,0:T(8,128)S(1)} %bitcast.19), channel_id=1, replica_groups=mesh['sector'=16,'x'=4,'core'=2] {'x'}, dimensions={0} | all-to-all | bytes 1638400 | tf_op jit(solution)/shard_map/all_to_all | solution.py:464
  98.0 14.3 %all_gather.7.mine_ref = f32[1600,128]{1,0:T(8,128)S(1)} all-gather(f32[400,128]{1,0:T(8,128)S(1)} %reduce_sum.9.mine_ref), channel_id=1, replica_groups=mesh['sector'=16,'x'=4,'core'=2] {'x'}, dimensions={0}, use_global_device_ids=true | all-gather | bytes 1024000 | tf_op jit(solution)/shard_map/all_gather | solution.py:492
  112.3 0.0 copy-start.2
  112.3 0.0 collective-permute-start.1
  112.3 0.5 collective-permute-start.2
  112.8 0.6 pad_add_fusion.scalars
  113.5 1.5 collective-permute-done.2.other_ref
  115.0 0.8 pair_up.1
  115.8 3.6 %all-to-all-start.3 = ((f32[16,50,128]{2,1,0:T(8,128)}), f32[16,50,128]{2,1,0:T(8,128)S(1)}, u32[]{:S(2)}, u32[]{:S(2)}) async-start(f32[16,50,128]{2,1,0:T(8,128)} %pair_up.1), calls=%async_computation.3 | async-start | bytes 917504 | tf_op jit(solution)/shard_map/all_to_all | solution.py:464
  119.4 0.0 collective-permute-done.1.other_ref
  119.4 0.0 copy-done.2
  119.4 0.0 copy-start.4
  119.4 0.9 copy-done.4
  120.3 11.0 %own_start.1.x_ref = f32[640,640]{1,0:T(8,128)} custom-call(s32[2]{0:T(128)} %pad_add_fusion.scalars, f32[1600,128]{1,0:T(8,128)} %copy-done.2, f32[1600,128]{1,0:T(8,128)} %copy-done.4), custom_call_target="tpu_custom_call" | custom-call | flops 6291456000 | bytes 3276800 | tf_op jit(solution)/shard_map/own_start/pallas_call | solution.py:283
  131.3 0.0 all-to-all-done.3
  131.3 1.9 gather_fusion.1
  133.2 0.0 copy-start
  133.2 0.0 copy-start.1
  133.2 9.1 %all-to-all-start.4 = ((f32[64,50,128]{2,1,0:T(8,128)}), f32[64,50,128]{2,1,0:T(8,128)S(1)}, u32[]{:S(2)}, u32[]{:S(2)}) async-start(f32[64,50,128]{2,1,0:T(8,128)} %gather_fusion.1), calls=%async_computation.4 | async-start | bytes 3670016 | tf_op jit(solution)/shard_map/all_to_all | solution.py:464
  142.3 0.0 copy-done
  142.3 0.0 copy-done.1
  142.3 22.5 %own_finish.1 = (f32[80,640]{1,0:T(8,128)}, bf16[4,640,1920]{2,1,0:T(8,128)(2,1)}) custom-call(s32[2]{0:T(128)S(1)} %copy-done, f32[640,640]{1,0:T(8,128)S(1)} %copy-done.1, bf16[1920,2560]{1,0:T(8,128)(2,1)} %get-tuple-element.18.l_ref), custom_call_target="tpu_custom_call" | custom-call | flops 15728640000 | bytes 22937600 | tf_op jit(solution)/shard_map/own_finish/pallas_call | solution.py:337
  164.8 4.7 %all-to-all-done.4.p_ref = f32[64,50,128]{2,1,0:T(8,128)S(1)} async-done(((f32[64,50,128]{2,1,0:T(8,128)}), f32[64,50,128]{2,1,0:T(8,128)S(1)}, u32[]{:S(2)}, u32[]{:S(2)}) %all-to-all-start.4) | async-done | bytes 1638432 | tf_op jit(solution)/shard_map/all_to_all | solution.py:464
  169.5 30.2 %rotate_by_source.1 = f32[4,640,640]{2,1,0:T(8,128)} custom-call(s32[2]{0:T(128)S(1)} %copy-done, f32[64,50,128]{2,1,0:T(8,128)S(1)} %all-to-all-done.4.p_ref, bf16[4,640,1920]{2,1,0:T(8,128)(2,1)} %get-tuple-element.23.h_ref), custom_call_target="tpu_custom_call" | custom-call | flops 22020096000 | bytes 16384000 | tf_op jit(solution)/shard_map/rotate_by_source/pallas_call | solution.py:389
  (2 shorter events, 0.0 us)
Async XLA Ops:
  0.6 10.0 %copy-start.3 = (s32[1,16]{1,0:T(1,128)S(1)}, s32[1,16]{1,0:T(1,128)}, u32[]{:S(2)}) copy-start(s32[1,16]{1,0:T(1,128)} %param.8) | copy-start | bytes 196
  2.5 18.9 %all-to-all-start = ((f32[16,50,128]{2,1,0:T(8,128)}), f32[16,50,128]{2,1,0:T(8,128)S(1)}, u32[]{:S(2)}, u32[]{:S(2)}) async-start(f32[16,50,128]{2,1,0:T(8,128)} %cut.1), calls=%async_computation | async-start | bytes 917504 | tf_op jit(solution)/shard_map/all_to_all | solution.py:464
  23.3 32.8 %all-to-all-start.1 = ((f32[64,50,128]{2,1,0:T(8,128)}), f32[64,50,128]{2,1,0:T(8,128)S(1)}, u32[]{:S(2)}, u32[]{:S(2)}) async-start(f32[64,50,128]{2,1,0:T(8,128)} %gather_fusion), calls=%async_computation.1 | async-start | bytes 3670016 | tf_op jit(solution)/shard_map/all_to_all | solution.py:464
  64.9 3.9 %collective-permute-start = (f32[1600,128]{1,0:T(8,128)S(1)}, f32[1600,128]{1,0:T(8,128)S(1)}, u32[]{:S(2)}, u32[]{:S(2)}) collective-permute-start(f32[1600,128]{1,0:T(8,128)S(1)} %get-tuple-element.16), channel_id=1, source_target_pairs={{0,1},{1,0},{2,3},{3,2},{4,5},{5,4},{6,7},{7,6},{8,9},{9,8},{10,11... | collective-permute-start | bytes 2457608 | tf_op jit(solution)/shard_map/ppermute | solution.py:460
  112.3 7.0 %copy-start.2 = (f32[1600,128]{1,0:T(8,128)}, f32[1600,128]{1,0:T(8,128)S(1)}, u32[]{:S(2)}) copy-start(f32[1600,128]{1,0:T(8,128)S(1)} %all_gather.7.mine_ref) | copy-start | bytes 2457604
  112.3 7.0 %collective-permute-start.1 = (f32[1600,128]{1,0:T(8,128)S(1)}, f32[1600,128]{1,0:T(8,128)S(1)}, u32[]{:S(2)}, u32[]{:S(2)}) collective-permute-start(f32[1600,128]{1,0:T(8,128)S(1)} %all_gather.7.mine_ref), channel_id=1, source_target_pairs={{0,1},{1,0},{2,3},{3,2},{4,5},{5,4},{6,7},{7,6},{8,9},{9,8},{10,11... | collective-permute-start | bytes 2457608 | tf_op jit(solution)/shard_map/ppermute | solution.py:460
  112.3 2.6 %collective-permute-start.2 = (f32[400,128]{1,0:T(8,128)S(1)}, f32[400,128]{1,0:T(8,128)S(1)}, u32[]{:S(2)}, u32[]{:S(2)}) collective-permute-start(f32[400,128]{1,0:T(8,128)S(1)} %reduce_sum.9.mine_ref), channel_id=1, source_target_pairs={{0,1},{1,0},{2,3},{3,2},{4,5},{5,4},{6,7},{7,6},{8,9},{9,8},{10,11... | collective-permute-start | bytes 614408 | tf_op jit(solution)/shard_map/ppermute | solution.py:460
  115.8 15.5 %all-to-all-start.3 = ((f32[16,50,128]{2,1,0:T(8,128)}), f32[16,50,128]{2,1,0:T(8,128)S(1)}, u32[]{:S(2)}, u32[]{:S(2)}) async-start(f32[16,50,128]{2,1,0:T(8,128)} %pair_up.1), calls=%async_computation.3 | async-start | bytes 917504 | tf_op jit(solution)/shard_map/all_to_all | solution.py:464
  119.4 0.9 copy-start.4
  133.2 9.1 %copy-start = (s32[2]{0:T(128)S(1)}, s32[2]{0:T(128)}, u32[]{:S(2)}) copy-start(s32[2]{0:T(128)} %pad_add_fusion.scalars) | copy-start | bytes 28
  133.2 9.1 %copy-start.1 = (f32[640,640]{1,0:T(8,128)S(1)}, f32[640,640]{1,0:T(8,128)}, u32[]{:S(2)}) copy-start(f32[640,640]{1,0:T(8,128)} %own_start.1.x_ref) | copy-start | bytes 4915204
  133.2 36.3 %all-to-all-start.4 = ((f32[64,50,128]{2,1,0:T(8,128)}), f32[64,50,128]{2,1,0:T(8,128)S(1)}, u32[]{:S(2)}, u32[]{:S(2)}) async-start(f32[64,50,128]{2,1,0:T(8,128)} %gather_fusion.1), calls=%async_computation.4 | async-start | bytes 3670016 | tf_op jit(solution)/shard_map/all_to_all | solution.py:464

commit v4 on v3

--- a/solution.py
+++ b/solution.py
@@ -12,7 +12,7 @@
 POLAR = 5
 SECTORS = 16
 GROUPS = 8
-EARLY = 2
+EARLY = 1
 LANES = 128
 F32, BF16 = jnp.float32, jnp.bfloat16
 VMEM_LIMIT = 48 << 20
@@ -182,18 +182,15 @@
     )(scalars, pieces, left3, right3)
 
 
-def start_polar(core, mine, other, x):
+def start_polar(parts, x):
     n = x.shape[0]
-    total = jnp.sum(mine[...] * mine[...]) + jnp.sum(other[...] * other[...])
+    total = sum(jnp.sum(lines[...] * lines[...]) for lines, _ in parts)
     factor = lax.rsqrt(n * (total / float(n * n)) + 1e-06) / 2.2
-    chunk = n // GROUPS
-    count = chunk * n // LANES
-    for ref, start in zip((mine, other), half_starts(core, n // 2), strict=True):
-        for chip in range(GROUPS // 2):
-            rows = pl.ds(pl.multiple_of(start + chip * chunk, chunk), chunk)
-            for t, lanes in tiles(n):
-                first = chip * count + t * chunk
-                x[rows, lanes] = ref[first : first + chunk] * factor
+    for lines, start in parts:
+        count = lines.shape[0] * LANES // n
+        rows = pl.ds(pl.multiple_of(start, count), count)
+        for t, lanes in tiles(n):
+            x[rows, lanes] = lines[t * count : (t + 1) * count] * factor
 
 
 def symmetric_rows(a, b):
@@ -271,25 +268,33 @@
     ]
 
 
-def own_start_kernel(scalars, mine_ref, other_ref, o_ref, x, a, b, r, g, sem):
-    start_polar(scalars[0], mine_ref, other_ref, x)
+def own_start_kernel(scalars, *refs):
+    gathered, (o_ref, x, a, b, r, _, sem) = refs[:GROUPS], refs[GROUPS:]
+    n = x.shape[0]
+    chips = GROUPS // 2
+    parts = []
+    for core, first in enumerate(half_starts(scalars[0], n // 2)):
+        for ahead in range(chips):
+            start = first + lax.rem(scalars[2] + ahead, chips) * (n // GROUPS)
+            parts.append((gathered[core * chips + ahead], start))
+    start_polar(parts, x)
     iterate_singly(EARLY, x, a, b, r)
     copy = pltpu.make_async_copy(x, o_ref, sem)
     copy.start()
     copy.wait()
 
 
-def own_start(scalars, mine, other, n):
+def own_start(scalars, gathered, n):
     return pl.pallas_call(
         own_start_kernel,
         out_shape=jax.ShapeDtypeStruct((n, n), F32),
-        in_specs=[pl.BlockSpec(memory_space=pltpu.SMEM), WHOLE, WHOLE],
+        in_specs=[pl.BlockSpec(memory_space=pltpu.SMEM)] + [WHOLE] * GROUPS,
         out_specs=pl.BlockSpec(memory_space=pltpu.HBM),
         scratch_shapes=polar_scratch(n) + [pltpu.SemaphoreType.DMA],
         compiler_params=params(ALL_VMEM),
         cost_estimate=cost(EARLY * 12 * n**3, 8 * n * n),
         name="own_start",
-    )(scalars, mine, other)
+    )(scalars, *gathered)
 
 
 def own_finish_kernel(scalars, x_ref, l_ref, columns_ref, o_ref, x, a, b, r, g, blocks, result, sems, out_sems):
@@ -364,7 +369,12 @@
         start = (piece % chips * SECTORS + piece // chips) * part
         mine[start : start + part] = p_ref[piece, 0:part]
         other[start : start + part] = p_ref[piece, part:count]
-    start_polar(scalars[0], mine, other, x)
+    lines, rows = mine.shape[0] // chips, n // GROUPS
+    parts = []
+    for ref, first in zip((mine, other), half_starts(scalars[0], n // 2), strict=True):
+        for chip in range(chips):
+            parts.append((ref.at[chip * lines : (chip + 1) * lines], first + chip * rows))
+    start_polar(parts, x)
     iterate_polar(POLAR, x, a, b, r, g)
     right_form(r, x[...] * math.sqrt(n))
 
@@ -456,6 +466,13 @@
     )(mine, other)
 
 
+def from_chips(block):
+    chips = lax.axis_size("x")
+    return [block] + [
+        lax.ppermute(block, "x", [(j, (j - ahead) % chips) for j in range(chips)]) for ahead in range(1, chips)
+    ]
+
+
 def swap_cores(block):
     return lax.ppermute(block, "core", [(0, 1), (1, 0)])
 
@@ -488,9 +505,9 @@
     other_chunk = swap_cores(chunk)
     spread = exchange(pair_up(chunk, other_chunk), "sector")
 
-    where = jnp.stack([core, group_here]).astype(jnp.int32)
-    mine = lax.all_gather(chunk, "x", tiled=True)
-    early, spread = lax.optimization_barrier((own_start(where, mine, swap_cores(mine), n), spread))
+    where = jnp.stack([core, group_here, chip]).astype(jnp.int32)
+    gathered = from_chips(chunk) + from_chips(other_chunk)
+    early, spread = lax.optimization_barrier((own_start(where, gathered, n), spread))
     source_pieces = deliver(spread, readers)
     own_rows, half3 = own_finish(where, early, stacked_left)
     half3, source_pieces = lax.optimization_barrier((half3, source_pieces))

time: 200 us -> 194 us (0.970)
  blocking collectives: 53.1 us -> 25.6 us
  starting transfers between devices: 30.7 us -> 48.7 us
  waiting for transfers between devices: 19.6 us -> 23 us
    all_gather x1 -> x0, blocking collectives: 14.3 us -> none  [shards(): mine = lax.all_gather(chunk, 'x', tiled=True)]
    all_to_all x1, blocking collectives: 29.1 us -> 16 us  [exchange(): return lax.all_to_all(pieces, axes, split_axis=0, concat_axis=0, tiled=True)]
    ppermute x3 -> x2, starting transfers between devices: 2.44 us -> 12.1 us  [swap_cores(): return lax.ppermute(block, 'core', [(0, 1), (1, 0)])]
    ppermute x0 -> x6, waiting for transfers between devices: none -> 8.9 us  [from_chips(): lax.ppermute(block, 'x', [(j, (j - ahead) % chips) for j in range(chips)])]
    ppermute x0 -> x6, starting transfers between devices: none -> 6.32 us  [from_chips(): lax.ppermute(block, 'x', [(j, (j - ahead) % chips) for j in range(chips)])]
    all_to_all x4, waiting for transfers between devices: 16.1 us -> 12.2 us  [exchange(): return lax.all_to_all(pieces, axes, split_axis=0, concat_axis=0, tiled=True)]
    pallas_call x1, Pallas kernels: 22.5 us -> 26.4 us  [own_finish(): pl.pallas_call(own_finish_kernel, out_shape=(jax.ShapeDtypeStruct((n // G...]
    pallas_call x1, Pallas kernels: 11 us -> 7.18 us  [own_start(): pl.pallas_call(own_start_kernel, out_shape=jax.ShapeDtypeStruct((n, n), F...]
  transfers between devices with their start and end apart: 7 -> 12, of which waited for: 5 -> 7; matrix products, arithmetic and copies ran while one was open for 0% -> 0% of each run, Pallas kernels for 24% -> 25%
where the time goes in v4:
time: 194 us
  Pallas kernels  89.1 us (46%)
  starting transfers between devices  48.7 us (25%)
  blocking collectives  25.6 us (13%)
  waiting for transfers between devices  23 us (12%)
  local copies, waits for them, and re-layouts  4.77 us (2%)
    all_to_all x4, starting transfers between devices, exchange(): return lax.all_to_all(pieces, axes, split_axis=0, concat_axis=0, tiled=True)  30.3 us
    pallas_call x1, Pallas kernels, rotate_by_source(): pl.pallas_call(source_kernel, out_shape=jax.ShapeDtypeStruct((k, n, n), F...  30.2 us
    pallas_call x1, Pallas kernels, own_finish(): pl.pallas_call(own_finish_kernel, out_shape=(jax.ShapeDtypeStruct((n // G...  26.4 us
    all_to_all x1, blocking collectives, exchange(): return lax.all_to_all(pieces, axes, split_axis=0, concat_axis=0, tiled=True)  16 us
    pallas_call x1, Pallas kernels, prepare(): pl.pallas_call(prepare_kernel, grid=(k,), out_shape=(jax.ShapeDtypeStruct...  14 us
    all_to_all x4, waiting for transfers between devices, exchange(): return lax.all_to_all(pieces, axes, split_axis=0, concat_axis=0, tiled=True)  12.2 us
    ppermute x2, starting transfers between devices, swap_cores(): return lax.ppermute(block, 'core', [(0, 1), (1, 0)])  12.1 us
    all_gather x1, blocking collectives, shards(): readers = lax.all_gather(shift_map[0], 'x').T.reshape(-1)  9.67 us
  transfers between devices with their start and end apart: 12, of which 7 were waited for; matrix products, arithmetic and copies ran while one was open for 0% of the time, Pallas kernels for 25%

profile of v4, /device:TPU:0, one launch (start us, length us, event | category | flops | bytes accessed | tf_op | source)
XLA Modules:
  0.0 193.7 jit_solution(586966241604953277)
XLA Ops:
  0.6 0.0 copy-start.4
  0.6 1.8 cut.1
  2.5 8.1 %all-to-all-start = ((f32[16,50,128]{2,1,0:T(8,128)}), f32[16,50,128]{2,1,0:T(8,128)S(1)}, u32[]{:S(2)}, u32[]{:S(2)}) async-start(f32[16,50,128]{2,1,0:T(8,128)} %cut.1), calls=%async_computation | async-start | bytes 917504 | tf_op jit(solution)/shard_map/all_to_all | solution.py:481
  10.6 0.0 copy-done.4
  10.6 9.7 %all-gather = s32[4,1,16]{2,1,0:T(1,128)S(1)} all-gather(s32[1,1,16]{2,1,0:T(1,128)S(1)} %bitcast.22), channel_id=1, replica_groups=mesh['sector'=16,'x'=4,'core'=2] {'x'}, dimensions={0}, use_global_device_ids=true | all-gather | bytes 320 | tf_op jit(solution)/shard_map/all_gather | solution.py:495
  20.3 0.1 copy.9
  20.4 0.1 reshape.12
  20.5 0.9 all-to-all-done
  21.4 1.9 gather_fusion
  23.3 7.5 %all-to-all-start.1 = ((f32[64,50,128]{2,1,0:T(8,128)}), f32[64,50,128]{2,1,0:T(8,128)S(1)}, u32[]{:S(2)}, u32[]{:S(2)}) async-start(f32[64,50,128]{2,1,0:T(8,128)} %gather_fusion), calls=%async_computation.1 | async-start | bytes 3670016 | tf_op jit(solution)/shard_map/all_to_all | solution.py:481
  31.5 14.0 %prepare.1 = (bf16[4,640,1920]{2,1,0:T(8,128)(2,1)}, bf16[4,1920,640]{2,1,0:T(8,128)(2,1)}, bf16[1920,2560]{1,0:T(8,128)(2,1)}) custom-call(f32[4,640,640]{2,1,0:T(8,128)} %bitcast.17, f32[4,640,640]{2,1,0:T(8,128)} %bitcast.18), custom_call_target="tpu_custom_call" | custom-call | flops 19660800 | bytes 42598400 | tf_op jit(solution)/shard_map/prepare/pallas_call | solution.py:77
  45.4 0.1 pad_add_fusion.1.scalars
  45.5 10.6 %all-to-all-done.1.w_ref = f32[64,50,128]{2,1,0:T(8,128)S(1)} async-done(((f32[64,50,128]{2,1,0:T(8,128)}), f32[64,50,128]{2,1,0:T(8,128)S(1)}, u32[]{:S(2)}, u32[]{:S(2)}) %all-to-all-start.1) | async-done | bytes 1638432 | tf_op jit(solution)/shard_map/all_to_all | solution.py:481
  56.1 8.7 %partial_sigma.1 = (f32[1600,128]{1,0:T(8,128)S(1)}, f32[1600,128]{1,0:T(8,128)S(1)}) custom-call(s32[2]{0:T(128)S(1)} %pad_add_fusion.1.scalars, f32[64,50,128]{2,1,0:T(8,128)S(1)} %all-to-all-done.1.w_ref, bf16[4,640,1920]{2,1,0:T(8,128)(2,1)} %get-tuple-element.13.l_ref, bf16[4,1920,640]{2,1,0:T(8,128)(2,1)} %get-tuple-element.14.r_ref), custom_call_target="tpu_custom_call" | custom-call | flops 12582912000 | bytes 26214400 | tf_op jit(solution)/shard_map/partial_sigma/pallas_call | solution.py:160
  64.9 12.1 %collective-permute-start = (f32[1600,128]{1,0:T(8,128)S(1)}, f32[1600,128]{1,0:T(8,128)S(1)}, u32[]{:S(2)}, u32[]{:S(2)}) collective-permute-start(f32[1600,128]{1,0:T(8,128)S(1)} %get-tuple-element.16), channel_id=1, source_target_pairs={{0,1},{1,0},{2,3},{3,2},{4,5},{5,4},{6,7},{7,6},{8,9},{9,8},{10,11... | collective-permute-start | bytes 2457608 | tf_op jit(solution)/shard_map/ppermute | solution.py:477
  76.9 2.0 %collective-permute-done = f32[1600,128]{1,0:T(8,128)S(1)} collective-permute-done((f32[1600,128]{1,0:T(8,128)S(1)}, f32[1600,128]{1,0:T(8,128)S(1)}, u32[]{:S(2)}, u32[]{:S(2)}) %collective-permute-start) | collective-permute-done | bytes 819232 | tf_op jit(solution)/shard_map/ppermute | solution.py:477
  78.9 0.1 add.7
  79.0 16.0 %all_to_all.25 = f32[4,400,128]{2,1,0:T(8,128)S(1)} all-to-all(f32[4,400,128]{2,1,0:T(8,128)S(1)} %bitcast.19), channel_id=1, replica_groups=mesh['sector'=16,'x'=4,'core'=2] {'x'}, dimensions={0} | all-to-all | bytes 1638400 | tf_op jit(solution)/shard_map/all_to_all | solution.py:481
  95.0 0.0 copy-start
  95.0 0.1 collective-permute-start.4
  95.1 0.6 collective-permute-start.3
  95.7 2.1 %collective-permute-start.2 = (f32[400,128]{1,0:T(8,128)S(1)}, f32[400,128]{1,0:T(8,128)S(1)}, u32[]{:S(2)}, u32[]{:S(2)}) collective-permute-start(f32[400,128]{1,0:T(8,128)S(1)} %reduce_sum.9.refs_0_.mine_ref), channel_id=1, source_target_pairs={{0,4},{2,6},{4,0},{6,2},{1,5},{3,7},{5,1},{7,3},{8,12},{10,14},{12... | collective-permute-start | bytes 614408 | tf_op jit(solution)/shard_map/ppermute | solution.py:472
  97.8 1.1 collective-permute-start.1
  98.9 0.0 collective-permute-done.4.refs_4_.other_ref
  98.9 0.9 collective-permute-start.7
  99.8 1.6 collective-permute-start.6
  101.4 7.2 %collective-permute-done.3.refs_3_ = f32[400,128]{1,0:T(8,128)S(1)} collective-permute-done((f32[400,128]{1,0:T(8,128)S(1)}, f32[400,128]{1,0:T(8,128)S(1)}, u32[]{:S(2)}, u32[]{:S(2)}) %collective-permute-start.3) | collective-permute-done | bytes 204832 | tf_op jit(solution)/shard_map/ppermute | solution.py:472
  108.6 0.0 collective-permute-start.5
  108.6 0.8 pair_up.1
  109.5 5.8 %all-to-all-start.3 = ((f32[16,50,128]{2,1,0:T(8,128)}), f32[16,50,128]{2,1,0:T(8,128)S(1)}, u32[]{:S(2)}, u32[]{:S(2)}) async-start(f32[16,50,128]{2,1,0:T(8,128)} %pair_up.1), calls=%async_computation.3 | async-start | bytes 917504 | tf_op jit(solution)/shard_map/all_to_all | solution.py:481
  115.3 0.6 pad_add_fusion.scalars
  115.9 0.0 collective-permute-done.2.refs_2_
  115.9 0.0 collective-permute-done.1.refs_1_
  115.9 0.0 copy-start.7
  115.9 1.0 collective-permute-done.7.refs_7_
  117.0 0.0 collective-permute-done.6.refs_6_
  117.0 0.7 collective-permute-done.5.refs_5_
  117.6 0.0 copy-done
  117.6 0.0 copy-done.5
  117.7 0.1 copy-done.9
  117.7 0.7 copy-done.10
  118.4 7.2 %own_start.1.x_ref = f32[640,640]{1,0:T(8,128)} custom-call(s32[3]{0:T(128)} %pad_add_fusion.scalars, f32[400,128]{1,0:T(8,128)} %copy-done, f32[400,128]{1,0:T(8,128)} %copy-done.7, f32[400,128]{1,0:T(8,128)} %copy-done.6, f32[400,128]{1,0:T(8,128)} %copy-done.5, f32[400,128]{1,0:T(8,128)} %copy-done.1, f32[400,128]{1,0:T(8,128)} %copy-done.10, ...), custom_call_target="tpu_custom_call" | custom-call | flops 3145728000 | bytes 3276800 | tf_op jit(solution)/shard_map/own_start/pallas_call | solution.py:288
  125.6 0.0 all-to-all-done.3
  125.6 1.9 gather_fusion.1
  127.5 8.8 %all-to-all-start.4 = ((f32[64,50,128]{2,1,0:T(8,128)}), f32[64,50,128]{2,1,0:T(8,128)S(1)}, u32[]{:S(2)}, u32[]{:S(2)}) async-start(f32[64,50,128]{2,1,0:T(8,128)} %gather_fusion.1), calls=%async_computation.4 | async-start | bytes 3670016 | tf_op jit(solution)/shard_map/all_to_all | solution.py:481
  136.4 26.4 %own_finish.1 = (f32[80,640]{1,0:T(8,128)}, bf16[4,640,1920]{2,1,0:T(8,128)(2,1)}) custom-call(s32[3]{0:T(128)S(1)} %copy-done.2, f32[640,640]{1,0:T(8,128)S(1)} %copy-done.3, bf16[1920,2560]{1,0:T(8,128)(2,1)} %get-tuple-element.18.l_ref), custom_call_target="tpu_custom_call" | custom-call | flops 18874368000 | bytes 22937600 | tf_op jit(solution)/shard_map/own_finish/pallas_call | solution.py:342
  162.8 0.6 all-to-all-done.4.p_ref
  163.4 30.2 %rotate_by_source.1 = f32[4,640,640]{2,1,0:T(8,128)} custom-call(s32[3]{0:T(128)S(1)} %copy-done.2, f32[64,50,128]{2,1,0:T(8,128)S(1)} %all-to-all-done.4.p_ref, bf16[4,640,1920]{2,1,0:T(8,128)(2,1)} %get-tuple-element.23.h_ref), custom_call_target="tpu_custom_call" | custom-call | flops 22020096000 | bytes 16384000 | tf_op jit(solution)/shard_map/rotate_by_source/pallas_call | solution.py:399
  (16 shorter events, 0.1 us)
Async XLA Ops:
  0.6 10.0 %copy-start.4 = (s32[1,16]{1,0:T(1,128)S(1)}, s32[1,16]{1,0:T(1,128)}, u32[]{:S(2)}) copy-start(s32[1,16]{1,0:T(1,128)} %param.8) | copy-start | bytes 196
  2.5 18.9 %all-to-all-start = ((f32[16,50,128]{2,1,0:T(8,128)}), f32[16,50,128]{2,1,0:T(8,128)S(1)}, u32[]{:S(2)}, u32[]{:S(2)}) async-start(f32[16,50,128]{2,1,0:T(8,128)} %cut.1), calls=%async_computation | async-start | bytes 917504 | tf_op jit(solution)/shard_map/all_to_all | solution.py:481
  23.3 32.8 %all-to-all-start.1 = ((f32[64,50,128]{2,1,0:T(8,128)}), f32[64,50,128]{2,1,0:T(8,128)S(1)}, u32[]{:S(2)}, u32[]{:S(2)}) async-start(f32[64,50,128]{2,1,0:T(8,128)} %gather_fusion), calls=%async_computation.1 | async-start | bytes 3670016 | tf_op jit(solution)/shard_map/all_to_all | solution.py:481
  64.9 14.0 %collective-permute-start = (f32[1600,128]{1,0:T(8,128)S(1)}, f32[1600,128]{1,0:T(8,128)S(1)}, u32[]{:S(2)}, u32[]{:S(2)}) collective-permute-start(f32[1600,128]{1,0:T(8,128)S(1)} %get-tuple-element.16), channel_id=1, source_target_pairs={{0,1},{1,0},{2,3},{3,2},{4,5},{5,4},{6,7},{7,6},{8,9},{9,8},{10,11... | collective-permute-start | bytes 2457608 | tf_op jit(solution)/shard_map/ppermute | solution.py:477
  95.0 22.6 %copy-start = (f32[400,128]{1,0:T(8,128)}, f32[400,128]{1,0:T(8,128)S(1)}, u32[]{:S(2)}) copy-start(f32[400,128]{1,0:T(8,128)S(1)} %reduce_sum.9.refs_0_.mine_ref) | copy-start | bytes 614404
  95.0 3.9 %collective-permute-start.4 = (f32[400,128]{1,0:T(8,128)S(1)}, f32[400,128]{1,0:T(8,128)S(1)}, u32[]{:S(2)}, u32[]{:S(2)}) collective-permute-start(f32[400,128]{1,0:T(8,128)S(1)} %reduce_sum.9.refs_0_.mine_ref), channel_id=1, source_target_pairs={{0,1},{1,0},{2,3},{3,2},{4,5},{5,4},{6,7},{7,6},{8,9},{9,8},{10,11... | collective-permute-start | bytes 614408 | tf_op jit(solution)/shard_map/ppermute | solution.py:477
  95.1 13.6 %collective-permute-start.3 = (f32[400,128]{1,0:T(8,128)S(1)}, f32[400,128]{1,0:T(8,128)S(1)}, u32[]{:S(2)}, u32[]{:S(2)}) collective-permute-start(f32[400,128]{1,0:T(8,128)S(1)} %reduce_sum.9.refs_0_.mine_ref), channel_id=1, source_target_pairs={{0,2},{2,4},{4,6},{6,0},{1,3},{3,5},{5,7},{7,1},{8,10},{10,12},{12... | collective-permute-start | bytes 614408 | tf_op jit(solution)/shard_map/ppermute | solution.py:472
  95.7 20.2 %collective-permute-start.2 = (f32[400,128]{1,0:T(8,128)S(1)}, f32[400,128]{1,0:T(8,128)S(1)}, u32[]{:S(2)}, u32[]{:S(2)}) collective-permute-start(f32[400,128]{1,0:T(8,128)S(1)} %reduce_sum.9.refs_0_.mine_ref), channel_id=1, source_target_pairs={{0,4},{2,6},{4,0},{6,2},{1,5},{3,7},{5,1},{7,3},{8,12},{10,14},{12... | collective-permute-start | bytes 614408 | tf_op jit(solution)/shard_map/ppermute | solution.py:472
  97.8 18.2 %collective-permute-start.1 = (f32[400,128]{1,0:T(8,128)S(1)}, f32[400,128]{1,0:T(8,128)S(1)}, u32[]{:S(2)}, u32[]{:S(2)}) collective-permute-start(f32[400,128]{1,0:T(8,128)S(1)} %reduce_sum.9.refs_0_.mine_ref), channel_id=1, source_target_pairs={{0,6},{2,0},{4,2},{6,4},{1,7},{3,1},{5,3},{7,5},{8,14},{10,8},{12,... | collective-permute-start | bytes 614408 | tf_op jit(solution)/shard_map/ppermute | solution.py:472
  98.9 18.8 %copy-start.1 = (f32[400,128]{1,0:T(8,128)}, f32[400,128]{1,0:T(8,128)S(1)}, u32[]{:S(2)}) copy-start(f32[400,128]{1,0:T(8,128)S(1)} %collective-permute-done.4.refs_4_.other_ref) | copy-start | bytes 614404
  98.9 18.1 %collective-permute-start.7 = (f32[400,128]{1,0:T(8,128)S(1)}, f32[400,128]{1,0:T(8,128)S(1)}, u32[]{:S(2)}, u32[]{:S(2)}) collective-permute-start(f32[400,128]{1,0:T(8,128)S(1)} %collective-permute-done.4.refs_4_.other_ref), channel_id=1, source_target_pairs={{0,2},{2,4},{4,6},{6,0},{1,3},{3,5},{5,7},{7,1},{8,10},{10,12},{12... | collective-permute-start | bytes 614408 | tf_op jit(solution)/shard_map/ppermute | solution.py:472
  99.8 17.1 %collective-permute-start.6 = (f32[400,128]{1,0:T(8,128)S(1)}, f32[400,128]{1,0:T(8,128)S(1)}, u32[]{:S(2)}, u32[]{:S(2)}) collective-permute-start(f32[400,128]{1,0:T(8,128)S(1)} %collective-permute-done.4.refs_4_.other_ref), channel_id=1, source_target_pairs={{0,4},{2,6},{4,0},{6,2},{1,5},{3,7},{5,1},{7,3},{8,12},{10,14},{12... | collective-permute-start | bytes 614408 | tf_op jit(solution)/shard_map/ppermute | solution.py:472
  108.6 9.0 %copy-start.5 = (f32[400,128]{1,0:T(8,128)}, f32[400,128]{1,0:T(8,128)S(1)}, u32[]{:S(2)}) copy-start(f32[400,128]{1,0:T(8,128)S(1)} %collective-permute-done.3.refs_3_) | copy-start | bytes 614404
  108.6 9.0 %collective-permute-start.5 = (f32[400,128]{1,0:T(8,128)S(1)}, f32[400,128]{1,0:T(8,128)S(1)}, u32[]{:S(2)}, u32[]{:S(2)}) collective-permute-start(f32[400,128]{1,0:T(8,128)S(1)} %collective-permute-done.4.refs_4_.other_ref), channel_id=1, source_target_pairs={{0,6},{2,0},{4,2},{6,4},{1,7},{3,1},{5,3},{7,5},{8,14},{10,8},{12,... | collective-permute-start | bytes 614408 | tf_op jit(solution)/shard_map/ppermute | solution.py:472
  109.5 16.1 %all-to-all-start.3 = ((f32[16,50,128]{2,1,0:T(8,128)}), f32[16,50,128]{2,1,0:T(8,128)S(1)}, u32[]{:S(2)}, u32[]{:S(2)}) async-start(f32[16,50,128]{2,1,0:T(8,128)} %pair_up.1), calls=%async_computation.3 | async-start | bytes 917504 | tf_op jit(solution)/shard_map/all_to_all | solution.py:481
  115.9 1.7 copy-start.6
  115.9 1.7 copy-start.7
  117.0 0.7 copy-start.8
  117.0 0.8 copy-start.9
  117.7 0.7 copy-start.10
  127.5 8.8 %copy-start.2 = (s32[3]{0:T(128)S(1)}, s32[3]{0:T(128)}, u32[]{:S(2)}) copy-start(s32[3]{0:T(128)} %pad_add_fusion.scalars) | copy-start | bytes 40
  127.5 8.8 %copy-start.3 = (f32[640,640]{1,0:T(8,128)S(1)}, f32[640,640]{1,0:T(8,128)}, u32[]{:S(2)}) copy-start(f32[640,640]{1,0:T(8,128)} %own_start.1.x_ref) | copy-start | bytes 4915204
  127.5 35.9 %all-to-all-start.4 = ((f32[64,50,128]{2,1,0:T(8,128)}), f32[64,50,128]{2,1,0:T(8,128)S(1)}, u32[]{:S(2)}, u32[]{:S(2)}) async-start(f32[64,50,128]{2,1,0:T(8,128)} %gather_fusion.1), calls=%async_computation.4 | async-start | bytes 3670016 | tf_op jit(solution)/shard_map/all_to_all | solution.py:481

commit v5 on v4

--- a/solution.py
+++ b/solution.py
@@ -268,15 +268,35 @@
     ]
 
 
-def own_start_kernel(scalars, *refs):
-    gathered, (o_ref, x, a, b, r, _, sem) = refs[:GROUPS], refs[GROUPS:]
+def join_kernel(_, *refs):
+    o_ref = refs[-1]
+    lines = refs[0].shape[0]
+    for k, ref in enumerate(refs[:-1]):
+        o_ref[k * lines : (k + 1) * lines] = ref[...]
+
+
+def join(after, blocks):
+    lines, lanes = blocks[0].shape
+    return pl.pallas_call(
+        join_kernel,
+        out_shape=jax.ShapeDtypeStruct((len(blocks) * lines, lanes), F32),
+        in_specs=[pl.BlockSpec(memory_space=pltpu.HBM)] + [WHOLE] * len(blocks),
+        out_specs=WHOLE,
+        compiler_params=params(),
+        cost_estimate=cost(lines, 8 * len(blocks) * lines * lanes),
+        name="join",
+    )(after, *blocks)
+
+
+def own_start_kernel(scalars, mine_ref, other_ref, o_ref, x, a, b, r, _, sem):
     n = x.shape[0]
     chips = GROUPS // 2
+    lines = mine_ref.shape[0] // chips
     parts = []
-    for core, first in enumerate(half_starts(scalars[0], n // 2)):
+    for ref, first in zip((mine_ref, other_ref), half_starts(scalars[0], n // 2), strict=True):
         for ahead in range(chips):
             start = first + lax.rem(scalars[2] + ahead, chips) * (n // GROUPS)
-            parts.append((gathered[core * chips + ahead], start))
+            parts.append((ref.at[ahead * lines : (ahead + 1) * lines], start))
     start_polar(parts, x)
     iterate_singly(EARLY, x, a, b, r)
     copy = pltpu.make_async_copy(x, o_ref, sem)
@@ -284,17 +304,17 @@
     copy.wait()
 
 
-def own_start(scalars, gathered, n):
+def own_start(scalars, mine, other, n):
     return pl.pallas_call(
         own_start_kernel,
         out_shape=jax.ShapeDtypeStruct((n, n), F32),
-        in_specs=[pl.BlockSpec(memory_space=pltpu.SMEM)] + [WHOLE] * GROUPS,
+        in_specs=[pl.BlockSpec(memory_space=pltpu.SMEM), WHOLE, WHOLE],
         out_specs=pl.BlockSpec(memory_space=pltpu.HBM),
         scratch_shapes=polar_scratch(n) + [pltpu.SemaphoreType.DMA],
         compiler_params=params(ALL_VMEM),
         cost_estimate=cost(EARLY * 12 * n**3, 8 * n * n),
         name="own_start",
-    )(scalars, *gathered)
+    )(scalars, mine, other)
 
 
 def own_finish_kernel(scalars, x_ref, l_ref, columns_ref, o_ref, x, a, b, r, g, blocks, result, sems, out_sems):
@@ -503,11 +523,12 @@
     chunk = jnp.sum(exchange(pair, "x"), axis=0)
 
     other_chunk = swap_cores(chunk)
-    spread = exchange(pair_up(chunk, other_chunk), "sector")
+    pieces = pair_up(chunk, other_chunk)
+    spread = exchange(pieces, "sector")
 
     where = jnp.stack([core, group_here, chip]).astype(jnp.int32)
-    gathered = from_chips(chunk) + from_chips(other_chunk)
-    early, spread = lax.optimization_barrier((own_start(where, gathered, n), spread))
+    mine = join(pieces, from_chips(chunk))
+    early, spread = lax.optimization_barrier((own_start(where, mine, swap_cores(mine), n), spread))
     source_pieces = deliver(spread, readers)
     own_rows, half3 = own_finish(where, early, stacked_left)
     half3, source_pieces = lax.optimization_barrier((half3, source_pieces))

time: 194 us -> 195 us (level)
  starting transfers between devices: 48.7 us -> 30.5 us
  Pallas kernels: 89.1 us -> 99.2 us
  blocking collectives: 25.6 us -> 30.1 us
  waiting for transfers between devices: 23 us -> 27 us
    ppermute x2 -> x3, starting transfers between devices: 12.1 us -> 0.26 us  [swap_cores(): return lax.ppermute(block, 'core', [(0, 1), (1, 0)])]
    pallas_call x1, Pallas kernels: 8.7 us -> 18.8 us  [partial_sigma(): pl.pallas_call(sigma_kernel, out_shape=(jax.ShapeDtypeStruct((lines // 2,...]
    all_to_all x1, blocking collectives: 16 us -> 20.5 us  [exchange(): return lax.all_to_all(pieces, axes, split_axis=0, concat_axis=0, tiled=True)]
    all_to_all x4, starting transfers between devices: 30.3 us -> 26.4 us  [exchange(): return lax.all_to_all(pieces, axes, split_axis=0, concat_axis=0, tiled=True)]
    all_to_all x4, waiting for transfers between devices: 12.2 us -> 15.6 us  [exchange(): return lax.all_to_all(pieces, axes, split_axis=0, concat_axis=0, tiled=True)]
    ppermute x6 -> x3, starting transfers between devices: 6.32 us -> 3.78 us  [from_chips(): lax.ppermute(block, 'x', [(j, (j - ahead) % chips) for j in range(chips)])]
    ppermute x6 -> x3, waiting for transfers between devices: 8.9 us -> 9.09 us  [from_chips(): lax.ppermute(block, 'x', [(j, (j - ahead) % chips) for j in range(chips)])]
  transfers between devices with their start and end apart: 12 -> 10, of which waited for: 7 -> 7; matrix products, arithmetic and copies ran while one was open for 0% -> 0% of each run, Pallas kernels for 25% -> 25%
where the time goes in v5:
time: 195 us; the launch traced here: 194 us
  Pallas kernels  99.2 us (51%)
  starting transfers between devices  30.5 us (16%)
  blocking collectives  30.1 us (15%)
  waiting for transfers between devices  27 us (14%)
  local copies, waits for them, and re-layouts  4.89 us (3%)
    pallas_call x1, Pallas kernels, rotate_by_source(): pl.pallas_call(source_kernel, out_shape=jax.ShapeDtypeStruct((k, n, n), F...  30.2 us
    all_to_all x4, starting transfers between devices, exchange(): return lax.all_to_all(pieces, axes, split_axis=0, concat_axis=0, tiled=True)  26.4 us
    pallas_call x1, Pallas kernels, own_finish(): pl.pallas_call(own_finish_kernel, out_shape=(jax.ShapeDtypeStruct((n // G...  26.4 us
    all_to_all x1, blocking collectives, exchange(): return lax.all_to_all(pieces, axes, split_axis=0, concat_axis=0, tiled=True)  20.5 us
    pallas_call x1, Pallas kernels, partial_sigma(): pl.pallas_call(sigma_kernel, out_shape=(jax.ShapeDtypeStruct((lines // 2,...  18.8 us
    all_to_all x4, waiting for transfers between devices, exchange(): return lax.all_to_all(pieces, axes, split_axis=0, concat_axis=0, tiled=True)  15.6 us
    pallas_call x1, Pallas kernels, prepare(): pl.pallas_call(prepare_kernel, grid=(k,), out_shape=(jax.ShapeDtypeStruct...  14 us
    all_gather x1, blocking collectives, shards(): readers = lax.all_gather(shift_map[0], 'x').T.reshape(-1)  9.67 us
  transfers between devices with their start and end apart: 10, of which 7 were waited for; matrix products, arithmetic and copies ran while one was open for 0% of the time, Pallas kernels for 25%

profile of v5, /device:TPU:0, one launch (start us, length us, event | category | flops | bytes accessed | tf_op | source)
XLA Modules:
  0.0 194.1 jit_solution(13579474789340657450)
XLA Ops:
  0.6 0.0 copy-start.3
  0.6 1.8 cut.1
  2.5 8.1 %all-to-all-start = ((f32[16,50,128]{2,1,0:T(8,128)}), f32[16,50,128]{2,1,0:T(8,128)S(1)}, u32[]{:S(2)}, u32[]{:S(2)}) async-start(f32[16,50,128]{2,1,0:T(8,128)} %cut.1), calls=%async_computation | async-start | bytes 917504 | tf_op jit(solution)/shard_map/all_to_all | solution.py:501
  10.6 0.0 copy-done.3
  10.6 9.7 %all-gather = s32[4,1,16]{2,1,0:T(1,128)S(1)} all-gather(s32[1,1,16]{2,1,0:T(1,128)S(1)} %bitcast.22), channel_id=1, replica_groups=mesh['sector'=16,'x'=4,'core'=2] {'x'}, dimensions={0}, use_global_device_ids=true | all-gather | bytes 320 | tf_op jit(solution)/shard_map/all_gather | solution.py:515
  20.3 0.1 copy.9
  20.4 0.1 reshape.12
  20.5 0.9 all-to-all-done
  21.4 1.9 gather_fusion
  23.3 7.5 %all-to-all-start.1 = ((f32[64,50,128]{2,1,0:T(8,128)}), f32[64,50,128]{2,1,0:T(8,128)S(1)}, u32[]{:S(2)}, u32[]{:S(2)}) async-start(f32[64,50,128]{2,1,0:T(8,128)} %gather_fusion), calls=%async_computation.1 | async-start | bytes 3670016 | tf_op jit(solution)/shard_map/all_to_all | solution.py:501
  31.5 14.0 %prepare.1 = (bf16[4,640,1920]{2,1,0:T(8,128)(2,1)}, bf16[4,1920,640]{2,1,0:T(8,128)(2,1)}, bf16[1920,2560]{1,0:T(8,128)(2,1)}) custom-call(f32[4,640,640]{2,1,0:T(8,128)} %bitcast.17, f32[4,640,640]{2,1,0:T(8,128)} %bitcast.18), custom_call_target="tpu_custom_call" | custom-call | flops 19660800 | bytes 42598400 | tf_op jit(solution)/shard_map/prepare/pallas_call | solution.py:77
  45.4 0.1 pad_add_fusion.1.scalars
  45.5 10.6 %all-to-all-done.1.w_ref = f32[64,50,128]{2,1,0:T(8,128)S(1)} async-done(((f32[64,50,128]{2,1,0:T(8,128)}), f32[64,50,128]{2,1,0:T(8,128)S(1)}, u32[]{:S(2)}, u32[]{:S(2)}) %all-to-all-start.1) | async-done | bytes 1638432 | tf_op jit(solution)/shard_map/all_to_all | solution.py:501
  56.1 18.8 %partial_sigma.1 = (f32[1600,128]{1,0:T(8,128)S(1)}, f32[1600,128]{1,0:T(8,128)S(1)}) custom-call(s32[2]{0:T(128)S(1)} %pad_add_fusion.1.scalars, f32[64,50,128]{2,1,0:T(8,128)S(1)} %all-to-all-done.1.w_ref, bf16[4,640,1920]{2,1,0:T(8,128)(2,1)} %get-tuple-element.13.l_ref, bf16[4,1920,640]{2,1,0:T(8,128)(2,1)} %get-tuple-element.14.r_ref), custom_call_target="tpu_custom_call" | custom-call | flops 12582912000 | bytes 26214400 | tf_op jit(solution)/shard_map/partial_sigma/pallas_call | solution.py:160
  75.0 0.1 collective-permute-start
  75.1 2.3 %collective-permute-done = f32[1600,128]{1,0:T(8,128)S(1)} collective-permute-done((f32[1600,128]{1,0:T(8,128)S(1)}, f32[1600,128]{1,0:T(8,128)S(1)}, u32[]{:S(2)}, u32[]{:S(2)}) %collective-permute-start) | collective-permute-done | bytes 819232 | tf_op jit(solution)/shard_map/ppermute | solution.py:497
  77.4 0.1 add.7
  77.5 20.5 %all_to_all.25 = f32[4,400,128]{2,1,0:T(8,128)S(1)} all-to-all(f32[4,400,128]{2,1,0:T(8,128)S(1)} %bitcast.19), channel_id=1, replica_groups=mesh['sector'=16,'x'=4,'core'=2] {'x'}, dimensions={0} | all-to-all | bytes 1638400 | tf_op jit(solution)/shard_map/all_to_all | solution.py:501
  98.0 0.1 collective-permute-start.1
  98.1 0.6 collective-permute-start.4
  98.7 2.1 %collective-permute-start.3 = (f32[400,128]{1,0:T(8,128)S(1)}, f32[400,128]{1,0:T(8,128)S(1)}, u32[]{:S(2)}, u32[]{:S(2)}) collective-permute-start(f32[400,128]{1,0:T(8,128)S(1)} %reduce_sum.9.mine_ref.refs_0_), channel_id=1, source_target_pairs={{0,4},{2,6},{4,0},{6,2},{1,5},{3,7},{5,1},{7,3},{8,12},{10,14},{12... | collective-permute-start | bytes 614408 | tf_op jit(solution)/shard_map/ppermute | solution.py:492
  100.8 1.1 collective-permute-start.2
  101.9 0.0 collective-permute-done.1.other_ref
  101.9 0.8 pair_up.1._
  102.7 8.5 %collective-permute-done.4.refs_3_ = f32[400,128]{1,0:T(8,128)S(1)} collective-permute-done((f32[400,128]{1,0:T(8,128)S(1)}, f32[400,128]{1,0:T(8,128)S(1)}, u32[]{:S(2)}, u32[]{:S(2)}) %collective-permute-start.4) | collective-permute-done | bytes 204832 | tf_op jit(solution)/shard_map/ppermute | solution.py:492
  111.2 0.0 collective-permute-done.3.refs_2_
  111.2 0.6 collective-permute-done.2.refs_1_
  111.8 0.1 join.1.mine_ref
  111.9 0.0 copy-start
  111.9 0.1 collective-permute-start.5
  112.0 3.8 %all-to-all-start.3 = ((f32[16,50,128]{2,1,0:T(8,128)}), f32[16,50,128]{2,1,0:T(8,128)S(1)}, u32[]{:S(2)}, u32[]{:S(2)}) async-start(f32[16,50,128]{2,1,0:T(8,128)} %pair_up.1._), calls=%async_computation.3 | async-start | bytes 917504 | tf_op jit(solution)/shard_map/all_to_all | solution.py:501
  115.7 0.6 pad_add_fusion.scalars
  116.3 0.0 collective-permute-done.5.other_ref
  116.3 0.0 copy-done
  116.3 0.0 copy-start.4
  116.3 0.9 copy-done.4
  117.2 7.1 %own_start.1.x_ref = f32[640,640]{1,0:T(8,128)} custom-call(s32[3]{0:T(128)} %pad_add_fusion.scalars, f32[1600,128]{1,0:T(8,128)} %copy-done, f32[1600,128]{1,0:T(8,128)} %copy-done.4), custom_call_target="tpu_custom_call" | custom-call | flops 3145728000 | bytes 3276800 | tf_op jit(solution)/shard_map/own_start/pallas_call | solution.py:308
  124.3 2.9 %all-to-all-done.3 = f32[16,50,128]{2,1,0:T(8,128)S(1)} async-done(((f32[16,50,128]{2,1,0:T(8,128)}), f32[16,50,128]{2,1,0:T(8,128)S(1)}, u32[]{:S(2)}, u32[]{:S(2)}) %all-to-all-start.3) | async-done | bytes 409632 | tf_op jit(solution)/shard_map/all_to_all | solution.py:501
  127.3 1.9 gather_fusion.1
  129.2 0.0 copy-start.1
  129.2 0.0 copy-start.2
  129.2 7.0 %all-to-all-start.4 = ((f32[64,50,128]{2,1,0:T(8,128)}), f32[64,50,128]{2,1,0:T(8,128)S(1)}, u32[]{:S(2)}, u32[]{:S(2)}) async-start(f32[64,50,128]{2,1,0:T(8,128)} %gather_fusion.1), calls=%async_computation.4 | async-start | bytes 3670016 | tf_op jit(solution)/shard_map/all_to_all | solution.py:501
  136.2 0.0 copy-done.1
  136.2 0.0 copy-done.2
  136.2 26.4 %own_finish.1 = (f32[80,640]{1,0:T(8,128)}, bf16[4,640,1920]{2,1,0:T(8,128)(2,1)}) custom-call(s32[3]{0:T(128)S(1)} %copy-done.1, f32[640,640]{1,0:T(8,128)S(1)} %copy-done.2, bf16[1920,2560]{1,0:T(8,128)(2,1)} %get-tuple-element.18.l_ref), custom_call_target="tpu_custom_call" | custom-call | flops 18874368000 | bytes 22937600 | tf_op jit(solution)/shard_map/own_finish/pallas_call | solution.py:362
  162.7 1.1 all-to-all-done.4.p_ref
  163.8 30.2 %rotate_by_source.1 = f32[4,640,640]{2,1,0:T(8,128)} custom-call(s32[3]{0:T(128)S(1)} %copy-done.1, f32[64,50,128]{2,1,0:T(8,128)S(1)} %all-to-all-done.4.p_ref, bf16[4,640,1920]{2,1,0:T(8,128)(2,1)} %get-tuple-element.23.h_ref), custom_call_target="tpu_custom_call" | custom-call | flops 22020096000 | bytes 16384000 | tf_op jit(solution)/shard_map/rotate_by_source/pallas_call | solution.py:419
  (2 shorter events, 0.0 us)
Async XLA Ops:
  0.6 10.0 %copy-start.3 = (s32[1,16]{1,0:T(1,128)S(1)}, s32[1,16]{1,0:T(1,128)}, u32[]{:S(2)}) copy-start(s32[1,16]{1,0:T(1,128)} %param.8) | copy-start | bytes 196
  2.5 18.9 %all-to-all-start = ((f32[16,50,128]{2,1,0:T(8,128)}), f32[16,50,128]{2,1,0:T(8,128)S(1)}, u32[]{:S(2)}, u32[]{:S(2)}) async-start(f32[16,50,128]{2,1,0:T(8,128)} %cut.1), calls=%async_computation | async-start | bytes 917504 | tf_op jit(solution)/shard_map/all_to_all | solution.py:501
  23.3 32.8 %all-to-all-start.1 = ((f32[64,50,128]{2,1,0:T(8,128)}), f32[64,50,128]{2,1,0:T(8,128)S(1)}, u32[]{:S(2)}, u32[]{:S(2)}) async-start(f32[64,50,128]{2,1,0:T(8,128)} %gather_fusion), calls=%async_computation.1 | async-start | bytes 3670016 | tf_op jit(solution)/shard_map/all_to_all | solution.py:501
  75.0 2.4 %collective-permute-start = (f32[1600,128]{1,0:T(8,128)S(1)}, f32[1600,128]{1,0:T(8,128)S(1)}, u32[]{:S(2)}, u32[]{:S(2)}) collective-permute-start(f32[1600,128]{1,0:T(8,128)S(1)} %get-tuple-element.16), channel_id=1, source_target_pairs={{0,1},{1,0},{2,3},{3,2},{4,5},{5,4},{6,7},{7,6},{8,9},{9,8},{10,11... | collective-permute-start | bytes 2457608 | tf_op jit(solution)/shard_map/ppermute | solution.py:497
  98.0 3.9 %collective-permute-start.1 = (f32[400,128]{1,0:T(8,128)S(1)}, f32[400,128]{1,0:T(8,128)S(1)}, u32[]{:S(2)}, u32[]{:S(2)}) collective-permute-start(f32[400,128]{1,0:T(8,128)S(1)} %reduce_sum.9.mine_ref.refs_0_), channel_id=1, source_target_pairs={{0,1},{1,0},{2,3},{3,2},{4,5},{5,4},{6,7},{7,6},{8,9},{9,8},{10,11... | collective-permute-start | bytes 614408 | tf_op jit(solution)/shard_map/ppermute | solution.py:497
  98.1 13.1 %collective-permute-start.4 = (f32[400,128]{1,0:T(8,128)S(1)}, f32[400,128]{1,0:T(8,128)S(1)}, u32[]{:S(2)}, u32[]{:S(2)}) collective-permute-start(f32[400,128]{1,0:T(8,128)S(1)} %reduce_sum.9.mine_ref.refs_0_), channel_id=1, source_target_pairs={{0,2},{2,4},{4,6},{6,0},{1,3},{3,5},{5,7},{7,1},{8,10},{10,12},{12... | collective-permute-start | bytes 614408 | tf_op jit(solution)/shard_map/ppermute | solution.py:492
  98.7 12.5 %collective-permute-start.3 = (f32[400,128]{1,0:T(8,128)S(1)}, f32[400,128]{1,0:T(8,128)S(1)}, u32[]{:S(2)}, u32[]{:S(2)}) collective-permute-start(f32[400,128]{1,0:T(8,128)S(1)} %reduce_sum.9.mine_ref.refs_0_), channel_id=1, source_target_pairs={{0,4},{2,6},{4,0},{6,2},{1,5},{3,7},{5,1},{7,3},{8,12},{10,14},{12... | collective-permute-start | bytes 614408 | tf_op jit(solution)/shard_map/ppermute | solution.py:492
  100.8 11.0 %collective-permute-start.2 = (f32[400,128]{1,0:T(8,128)S(1)}, f32[400,128]{1,0:T(8,128)S(1)}, u32[]{:S(2)}, u32[]{:S(2)}) collective-permute-start(f32[400,128]{1,0:T(8,128)S(1)} %reduce_sum.9.mine_ref.refs_0_), channel_id=1, source_target_pairs={{0,6},{2,0},{4,2},{6,4},{1,7},{3,1},{5,3},{7,5},{8,14},{10,8},{12,... | collective-permute-start | bytes 614408 | tf_op jit(solution)/shard_map/ppermute | solution.py:492
  111.9 4.5 %copy-start = (f32[1600,128]{1,0:T(8,128)}, f32[1600,128]{1,0:T(8,128)S(1)}, u32[]{:S(2)}) copy-start(f32[1600,128]{1,0:T(8,128)S(1)} %join.1.mine_ref) | copy-start | bytes 2457604
  111.9 4.4 %collective-permute-start.5 = (f32[1600,128]{1,0:T(8,128)S(1)}, f32[1600,128]{1,0:T(8,128)S(1)}, u32[]{:S(2)}, u32[]{:S(2)}) collective-permute-start(f32[1600,128]{1,0:T(8,128)S(1)} %join.1.mine_ref), channel_id=1, source_target_pairs={{0,1},{1,0},{2,3},{3,2},{4,5},{5,4},{6,7},{7,6},{8,9},{9,8},{10,11... | collective-permute-start | bytes 2457608 | tf_op jit(solution)/shard_map/ppermute | solution.py:497
  112.0 15.3 %all-to-all-start.3 = ((f32[16,50,128]{2,1,0:T(8,128)}), f32[16,50,128]{2,1,0:T(8,128)S(1)}, u32[]{:S(2)}, u32[]{:S(2)}) async-start(f32[16,50,128]{2,1,0:T(8,128)} %pair_up.1._), calls=%async_computation.3 | async-start | bytes 917504 | tf_op jit(solution)/shard_map/all_to_all | solution.py:501
  116.3 0.9 copy-start.4
  129.2 7.1 %copy-start.1 = (s32[3]{0:T(128)S(1)}, s32[3]{0:T(128)}, u32[]{:S(2)}) copy-start(s32[3]{0:T(128)} %pad_add_fusion.scalars) | copy-start | bytes 40
  129.2 7.1 %copy-start.2 = (f32[640,640]{1,0:T(8,128)S(1)}, f32[640,640]{1,0:T(8,128)}, u32[]{:S(2)}) copy-start(f32[640,640]{1,0:T(8,128)} %own_start.1.x_ref) | copy-start | bytes 4915204
  129.2 34.6 %all-to-all-start.4 = ((f32[64,50,128]{2,1,0:T(8,128)}), f32[64,50,128]{2,1,0:T(8,128)S(1)}, u32[]{:S(2)}, u32[]{:S(2)}) async-start(f32[64,50,128]{2,1,0:T(8,128)} %gather_fusion.1), calls=%async_computation.4 | async-start | bytes 3670016 | tf_op jit(solution)/shard_map/all_to_all | solution.py:501

commit v6 on v4

--- a/solution.py
+++ b/solution.py
@@ -108,74 +108,73 @@
     return pl.multiple_of(core * half, half), pl.multiple_of((1 - core) * half, half)
 
 
-def sigma_kernel(scalars, w_ref, l_ref, r_ref, own_ref, other_ref, w3, mid, acc, lines):
-    step = pl.program_id(0)
+def sigma_kernel(scalars, w_ref, l_ref, r_ref, own_ref, other_ref, w3, mid, acc, lines, left, right, l_sems, r_sems):
     n = acc.shape[0]
-
-    @pl.when(step == 0)
-    def _():
-        pieces, count, _ = w_ref.shape
-        chips = pieces // SECTORS
-        for piece in range(pieces):
-            start = (piece % chips * SECTORS + piece // chips) * count
-            lines[start : start + count] = w_ref[piece]
-        part = n // chips
-        for chip in range(chips):
-            for t, lanes in tiles(n):
-                start = chip * SECTORS * count + t * part
-                high, low = halves(lines[start : start + part])
-                for third, v in enumerate((high, low, high)):
-                    w3[third * n + chip * part : third * n + (chip + 1) * part, lanes] = v
-
-    @pl.when(step < scalars[0])
-    def _():
-        left_form(mid, mm(l_ref[0], w3[...]))
-        term = mm(mid[...], r_ref[0])
-
-        @pl.when(step == 0)
-        def _():
-            acc[...] = term
-
-        @pl.when(step > 0)
-        def _():
-            acc[...] += term
-
-    @pl.when(step == pl.num_programs(0) - 1)
-    def _():
-        chunk = n // GROUPS
-        count = chunk * n // LANES
-        for ref, start in zip((own_ref, other_ref), half_starts(scalars[1], n // 2), strict=True):
-            for chip in range(GROUPS // 2):
-                rows = pl.ds(pl.multiple_of(start + chip * chunk, chunk), chunk)
-                lines_of(ref.at[chip * count : (chip + 1) * count], acc[rows])
+    operators = left.shape[0]
+
+    def reads(w):
+        return (
+            pltpu.make_async_copy(l_ref.at[w], left.at[w], l_sems.at[w]),
+            pltpu.make_async_copy(r_ref.at[w], right.at[w], r_sems.at[w]),
+        )
+
+    def arrived(w, carry=0):
+        for read in reads(w):
+            read.wait()
+        return carry
+
+    for w in range(operators):
+        for read in reads(w):
+            read.start()
+    pieces, count, _ = w_ref.shape
+    chips = pieces // SECTORS
+    for piece in range(pieces):
+        start = (piece % chips * SECTORS + piece // chips) * count
+        lines[start : start + count] = w_ref[piece]
+    part = n // chips
+    for chip in range(chips):
+        for t, lanes in tiles(n):
+            start = chip * SECTORS * count + t * part
+            high, low = halves(lines[start : start + part])
+            for third, v in enumerate((high, low, high)):
+                w3[third * n + chip * part : third * n + (chip + 1) * part, lanes] = v
+    acc[...] = jnp.zeros_like(acc)
+
+    def operator(w, carry):
+        arrived(w)
+        left_form(mid, mm(left[w], w3[...]))
+        acc[...] += mm(mid[...], right[w])
+        return carry
+
+    lax.fori_loop(0, scalars[0], operator, 0)
+    lax.fori_loop(scalars[0], operators, arrived, 0)
+    chunk = n // GROUPS
+    count = chunk * n // LANES
+    for ref, start in zip((own_ref, other_ref), half_starts(scalars[1], n // 2), strict=True):
+        for chip in range(GROUPS // 2):
+            rows = pl.ds(pl.multiple_of(start + chip * chunk, chunk), chunk)
+            lines_of(ref.at[chip * count : (chip + 1) * count], acc[rows])
 
 
 def partial_sigma(scalars, pieces, left3, right3):
     k, n = left3.shape[:2]
     lines = n * n // LANES
-
-    def active(w, s):
-        return (jnp.minimum(w, s[0] - 1), 0, 0)
-
+    hbm = pl.BlockSpec(memory_space=pltpu.HBM)
     return pl.pallas_call(
         sigma_kernel,
         out_shape=(jax.ShapeDtypeStruct((lines // 2, LANES), F32),) * 2,
-        grid_spec=pltpu.PrefetchScalarGridSpec(
-            num_scalar_prefetch=1,
-            grid=(k,),
-            in_specs=[
-                pl.BlockSpec(pieces.shape, lambda w, s: (0, 0, 0)),
-                pl.BlockSpec((1, n, 3 * n), active),
-                pl.BlockSpec((1, 3 * n, n), active),
-            ],
-            out_specs=(pl.BlockSpec((lines // 2, LANES), lambda w, s: (0, 0)),) * 2,
-            scratch_shapes=[
-                pltpu.VMEM((3 * n, n), BF16),
-                pltpu.VMEM((n, 3 * n), BF16),
-                pltpu.VMEM((n, n), F32),
-                pltpu.VMEM((lines, LANES), F32),
-            ],
-        ),
+        in_specs=[pl.BlockSpec(memory_space=pltpu.SMEM), WHOLE, hbm, hbm],
+        out_specs=(WHOLE, WHOLE),
+        scratch_shapes=[
+            pltpu.VMEM((3 * n, n), BF16),
+            pltpu.VMEM((n, 3 * n), BF16),
+            pltpu.VMEM((n, n), F32),
+            pltpu.VMEM((lines, LANES), F32),
+            pltpu.VMEM((k, n, 3 * n), BF16),
+            pltpu.VMEM((k, 3 * n, n), BF16),
+            pltpu.SemaphoreType.DMA((k,)),
+            pltpu.SemaphoreType.DMA((k,)),
+        ],
         compiler_params=params(),
         cost_estimate=cost(12 * k * n**3, 16 * k * n * n),
         name="partial_sigma",

time: 194 us -> 194 us (level)
  starting transfers between devices: 48.7 us -> 34.1 us
  blocking collectives: 25.6 us -> 38.5 us
    all_to_all x1, blocking collectives: 16 us -> 28.8 us  [exchange(): return lax.all_to_all(pieces, axes, split_axis=0, concat_axis=0, tiled=True)]
    ppermute x2, starting transfers between devices: 12.1 us -> 1.87 us  [swap_cores(): return lax.ppermute(block, 'core', [(0, 1), (1, 0)])]
    all_to_all x4, starting transfers between devices: 30.3 us -> 25.9 us  [exchange(): return lax.all_to_all(pieces, axes, split_axis=0, concat_axis=0, tiled=True)]
    ppermute x6, waiting for transfers between devices: 8.9 us -> 11 us  [from_chips(): lax.ppermute(block, 'x', [(j, (j - ahead) % chips) for j in range(chips)])]
where the time goes in v6:
time: 194 us; the launch traced here: 193 us
  Pallas kernels  88.5 us (46%)
  blocking collectives  38.5 us (20%)
  starting transfers between devices  34.1 us (18%)
  waiting for transfers between devices  24.9 us (13%)
  local copies, waits for them, and re-layouts  4.77 us (2%)
    pallas_call x1, Pallas kernels, rotate_by_source(): pl.pallas_call(source_kernel, out_shape=jax.ShapeDtypeStruct((k, n, n), F...  30.2 us
    all_to_all x1, blocking collectives, exchange(): return lax.all_to_all(pieces, axes, split_axis=0, concat_axis=0, tiled=True)  28.8 us
    pallas_call x1, Pallas kernels, own_finish(): pl.pallas_call(own_finish_kernel, out_shape=(jax.ShapeDtypeStruct((n // G...  26.4 us
    all_to_all x4, starting transfers between devices, exchange(): return lax.all_to_all(pieces, axes, split_axis=0, concat_axis=0, tiled=True)  25.9 us
    pallas_call x1, Pallas kernels, prepare(): pl.pallas_call(prepare_kernel, grid=(k,), out_shape=(jax.ShapeDtypeStruct...  14 us
    all_to_all x4, waiting for transfers between devices, exchange(): return lax.all_to_all(pieces, axes, split_axis=0, concat_axis=0, tiled=True)  12 us
    ppermute x6, waiting for transfers between devices, from_chips(): lax.ppermute(block, 'x', [(j, (j - ahead) % chips) for j in range(chips)])  11 us
    all_gather x1, blocking collectives, shards(): readers = lax.all_gather(shift_map[0], 'x').T.reshape(-1)  9.67 us
  transfers between devices with their start and end apart: 12, of which 7 were waited for; matrix products, arithmetic and copies ran while one was open for 0% of the time, Pallas kernels for 25%

profile of v6, /device:TPU:0, one launch (start us, length us, event | category | flops | bytes accessed | tf_op | source)
XLA Modules:
  0.0 193.2 jit_solution(4363421322688745496)
XLA Ops:
  0.6 0.0 copy-start.4
  0.6 1.8 cut.1
  2.5 8.1 %all-to-all-start = ((f32[16,50,128]{2,1,0:T(8,128)}), f32[16,50,128]{2,1,0:T(8,128)S(1)}, u32[]{:S(2)}, u32[]{:S(2)}) async-start(f32[16,50,128]{2,1,0:T(8,128)} %cut.1), calls=%async_computation | async-start | bytes 917504 | tf_op jit(solution)/shard_map/all_to_all | solution.py:480
  10.6 9.7 %all-gather = s32[4,1,16]{2,1,0:T(1,128)S(1)} all-gather(s32[1,1,16]{2,1,0:T(1,128)S(1)} %bitcast.22), channel_id=1, replica_groups=mesh['sector'=16,'x'=4,'core'=2] {'x'}, dimensions={0}, use_global_device_ids=true | all-gather | bytes 320 | tf_op jit(solution)/shard_map/all_gather | solution.py:494
  20.3 0.1 copy.9
  20.4 0.1 reshape.12
  20.5 0.9 all-to-all-done
  21.4 1.9 gather_fusion
  23.3 7.5 %all-to-all-start.1 = ((f32[64,50,128]{2,1,0:T(8,128)}), f32[64,50,128]{2,1,0:T(8,128)S(1)}, u32[]{:S(2)}, u32[]{:S(2)}) async-start(f32[64,50,128]{2,1,0:T(8,128)} %gather_fusion), calls=%async_computation.1 | async-start | bytes 3670016 | tf_op jit(solution)/shard_map/all_to_all | solution.py:480
  31.5 14.0 %prepare.1 = (bf16[4,640,1920]{2,1,0:T(8,128)(2,1)}, bf16[4,1920,640]{2,1,0:T(8,128)(2,1)}, bf16[1920,2560]{1,0:T(8,128)(2,1)}) custom-call(f32[4,640,640]{2,1,0:T(8,128)} %bitcast.17, f32[4,640,640]{2,1,0:T(8,128)} %bitcast.18), custom_call_target="tpu_custom_call" | custom-call | flops 19660800 | bytes 42598400 | tf_op jit(solution)/shard_map/prepare/pallas_call | solution.py:77
  45.4 0.1 pad_add_fusion.1.scalars
  45.5 10.6 %all-to-all-done.1.w_ref = f32[64,50,128]{2,1,0:T(8,128)S(1)} async-done(((f32[64,50,128]{2,1,0:T(8,128)}), f32[64,50,128]{2,1,0:T(8,128)S(1)}, u32[]{:S(2)}, u32[]{:S(2)}) %all-to-all-start.1) | async-done | bytes 1638432 | tf_op jit(solution)/shard_map/all_to_all | solution.py:480
  56.1 8.1 %partial_sigma.1 = (f32[1600,128]{1,0:T(8,128)S(1)}, f32[1600,128]{1,0:T(8,128)S(1)}) custom-call(s32[2]{0:T(128)S(1)} %pad_add_fusion.1.scalars, f32[64,50,128]{2,1,0:T(8,128)S(1)} %all-to-all-done.1.w_ref, bf16[4,640,1920]{2,1,0:T(8,128)(2,1)} %get-tuple-element.13.l_ref, bf16[4,1920,640]{2,1,0:T(8,128)(2,1)} %get-tuple-element.14.r_ref), custom_call_target="tpu_custom_call" | custom-call | flops 12582912000 | bytes 26214400 | tf_op jit(solution)/shard_map/partial_sigma/pallas_call | solution.py:163
  64.2 1.8 collective-permute-start
  66.0 2.0 %collective-permute-done = f32[1600,128]{1,0:T(8,128)S(1)} collective-permute-done((f32[1600,128]{1,0:T(8,128)S(1)}, f32[1600,128]{1,0:T(8,128)S(1)}, u32[]{:S(2)}, u32[]{:S(2)}) %collective-permute-start) | collective-permute-done | bytes 819232 | tf_op jit(solution)/shard_map/ppermute | solution.py:476
  68.0 0.1 add.7
  68.1 28.8 %all_to_all.25 = f32[4,400,128]{2,1,0:T(8,128)S(1)} all-to-all(f32[4,400,128]{2,1,0:T(8,128)S(1)} %bitcast.19), channel_id=1, replica_groups=mesh['sector'=16,'x'=4,'core'=2] {'x'}, dimensions={0} | all-to-all | bytes 1638400 | tf_op jit(solution)/shard_map/all_to_all | solution.py:480
  96.9 0.0 copy-start
  96.9 0.1 collective-permute-start.4
  97.0 0.6 collective-permute-start.3
  97.7 2.1 %collective-permute-start.2 = (f32[400,128]{1,0:T(8,128)S(1)}, f32[400,128]{1,0:T(8,128)S(1)}, u32[]{:S(2)}, u32[]{:S(2)}) collective-permute-start(f32[400,128]{1,0:T(8,128)S(1)} %reduce_sum.9.refs_0_.mine_ref), channel_id=1, source_target_pairs={{0,4},{2,6},{4,0},{6,2},{1,5},{3,7},{5,1},{7,3},{8,12},{10,14},{12... | collective-permute-start | bytes 614408 | tf_op jit(solution)/shard_map/ppermute | solution.py:471
  99.7 1.1 collective-permute-start.1
  100.8 0.0 collective-permute-done.4.refs_4_.other_ref
  100.8 0.9 collective-permute-start.7
  101.8 1.6 collective-permute-start.6
  103.3 7.2 %collective-permute-done.3.refs_3_ = f32[400,128]{1,0:T(8,128)S(1)} collective-permute-done((f32[400,128]{1,0:T(8,128)S(1)}, f32[400,128]{1,0:T(8,128)S(1)}, u32[]{:S(2)}, u32[]{:S(2)}) %collective-permute-start.3) | collective-permute-done | bytes 204832 | tf_op jit(solution)/shard_map/ppermute | solution.py:471
  110.6 0.0 collective-permute-start.5
  110.6 0.8 pair_up.1
  111.4 3.7 %all-to-all-start.3 = ((f32[16,50,128]{2,1,0:T(8,128)}), f32[16,50,128]{2,1,0:T(8,128)S(1)}, u32[]{:S(2)}, u32[]{:S(2)}) async-start(f32[16,50,128]{2,1,0:T(8,128)} %pair_up.1), calls=%async_computation.3 | async-start | bytes 917504 | tf_op jit(solution)/shard_map/all_to_all | solution.py:480
  115.2 0.6 pad_add_fusion.scalars
  115.8 0.0 collective-permute-done.2.refs_2_
  115.8 0.0 collective-permute-done.1.refs_1_
  115.8 0.0 copy-start.7
  115.8 3.1 %collective-permute-done.7.refs_7_ = f32[400,128]{1,0:T(8,128)S(1)} collective-permute-done((f32[400,128]{1,0:T(8,128)S(1)}, f32[400,128]{1,0:T(8,128)S(1)}, u32[]{:S(2)}, u32[]{:S(2)}) %collective-permute-start.7) | collective-permute-done | bytes 204832 | tf_op jit(solution)/shard_map/ppermute | solution.py:471
  118.9 0.0 collective-permute-done.6.refs_6_
  118.9 0.7 collective-permute-done.5.refs_5_
  119.6 0.0 copy-done.6
  119.6 0.0 copy-done.7
  119.6 0.0 copy-done.8
  119.6 0.1 copy-done.9
  119.7 0.7 copy-done.10
  120.4 7.2 %own_start.1.x_ref = f32[640,640]{1,0:T(8,128)} custom-call(s32[3]{0:T(128)} %pad_add_fusion.scalars, f32[400,128]{1,0:T(8,128)} %copy-done, f32[400,128]{1,0:T(8,128)} %copy-done.7, f32[400,128]{1,0:T(8,128)} %copy-done.6, f32[400,128]{1,0:T(8,128)} %copy-done.5, f32[400,128]{1,0:T(8,128)} %copy-done.1, f32[400,128]{1,0:T(8,128)} %copy-done.10, ...), custom_call_target="tpu_custom_call" | custom-call | flops 3145728000 | bytes 3276800 | tf_op jit(solution)/shard_map/own_start/pallas_call | solution.py:287
  127.5 0.0 all-to-all-done.3
  127.6 1.9 gather_fusion.1
  129.5 6.5 %all-to-all-start.4 = ((f32[64,50,128]{2,1,0:T(8,128)}), f32[64,50,128]{2,1,0:T(8,128)S(1)}, u32[]{:S(2)}, u32[]{:S(2)}) async-start(f32[64,50,128]{2,1,0:T(8,128)} %gather_fusion.1), calls=%async_computation.4 | async-start | bytes 3670016 | tf_op jit(solution)/shard_map/all_to_all | solution.py:480
  136.0 26.4 %own_finish.1 = (f32[80,640]{1,0:T(8,128)}, bf16[4,640,1920]{2,1,0:T(8,128)(2,1)}) custom-call(s32[3]{0:T(128)S(1)} %copy-done.2, f32[640,640]{1,0:T(8,128)S(1)} %copy-done.3, bf16[1920,2560]{1,0:T(8,128)(2,1)} %get-tuple-element.18.l_ref), custom_call_target="tpu_custom_call" | custom-call | flops 18874368000 | bytes 22937600 | tf_op jit(solution)/shard_map/own_finish/pallas_call | solution.py:341
  162.4 0.4 all-to-all-done.4.p_ref
  162.9 30.2 %rotate_by_source.1 = f32[4,640,640]{2,1,0:T(8,128)} custom-call(s32[3]{0:T(128)S(1)} %copy-done.2, f32[64,50,128]{2,1,0:T(8,128)S(1)} %all-to-all-done.4.p_ref, bf16[4,640,1920]{2,1,0:T(8,128)(2,1)} %get-tuple-element.23.h_ref), custom_call_target="tpu_custom_call" | custom-call | flops 22020096000 | bytes 16384000 | tf_op jit(solution)/shard_map/rotate_by_source/pallas_call | solution.py:398
  (16 shorter events, 0.1 us)
Async XLA Ops:
  0.6 10.0 %copy-start.4 = (s32[1,16]{1,0:T(1,128)S(1)}, s32[1,16]{1,0:T(1,128)}, u32[]{:S(2)}) copy-start(s32[1,16]{1,0:T(1,128)} %param.8) | copy-start | bytes 196
  2.5 18.9 %all-to-all-start = ((f32[16,50,128]{2,1,0:T(8,128)}), f32[16,50,128]{2,1,0:T(8,128)S(1)}, u32[]{:S(2)}, u32[]{:S(2)}) async-start(f32[16,50,128]{2,1,0:T(8,128)} %cut.1), calls=%async_computation | async-start | bytes 917504 | tf_op jit(solution)/shard_map/all_to_all | solution.py:480
  23.3 32.8 %all-to-all-start.1 = ((f32[64,50,128]{2,1,0:T(8,128)}), f32[64,50,128]{2,1,0:T(8,128)S(1)}, u32[]{:S(2)}, u32[]{:S(2)}) async-start(f32[64,50,128]{2,1,0:T(8,128)} %gather_fusion), calls=%async_computation.1 | async-start | bytes 3670016 | tf_op jit(solution)/shard_map/all_to_all | solution.py:480
  64.2 3.7 %collective-permute-start = (f32[1600,128]{1,0:T(8,128)S(1)}, f32[1600,128]{1,0:T(8,128)S(1)}, u32[]{:S(2)}, u32[]{:S(2)}) collective-permute-start(f32[1600,128]{1,0:T(8,128)S(1)} %get-tuple-element.16), channel_id=1, source_target_pairs={{0,1},{1,0},{2,3},{3,2},{4,5},{5,4},{6,7},{7,6},{8,9},{9,8},{10,11... | collective-permute-start | bytes 2457608 | tf_op jit(solution)/shard_map/ppermute | solution.py:476
  96.9 22.6 %copy-start = (f32[400,128]{1,0:T(8,128)}, f32[400,128]{1,0:T(8,128)S(1)}, u32[]{:S(2)}) copy-start(f32[400,128]{1,0:T(8,128)S(1)} %reduce_sum.9.refs_0_.mine_ref) | copy-start | bytes 614404
  96.9 3.9 %collective-permute-start.4 = (f32[400,128]{1,0:T(8,128)S(1)}, f32[400,128]{1,0:T(8,128)S(1)}, u32[]{:S(2)}, u32[]{:S(2)}) collective-permute-start(f32[400,128]{1,0:T(8,128)S(1)} %reduce_sum.9.refs_0_.mine_ref), channel_id=1, source_target_pairs={{0,1},{1,0},{2,3},{3,2},{4,5},{5,4},{6,7},{7,6},{8,9},{9,8},{10,11... | collective-permute-start | bytes 614408 | tf_op jit(solution)/shard_map/ppermute | solution.py:476
  97.0 13.6 %collective-permute-start.3 = (f32[400,128]{1,0:T(8,128)S(1)}, f32[400,128]{1,0:T(8,128)S(1)}, u32[]{:S(2)}, u32[]{:S(2)}) collective-permute-start(f32[400,128]{1,0:T(8,128)S(1)} %reduce_sum.9.refs_0_.mine_ref), channel_id=1, source_target_pairs={{0,2},{2,4},{4,6},{6,0},{1,3},{3,5},{5,7},{7,1},{8,10},{10,12},{12... | collective-permute-start | bytes 614408 | tf_op jit(solution)/shard_map/ppermute | solution.py:471
  97.7 18.2 %collective-permute-start.2 = (f32[400,128]{1,0:T(8,128)S(1)}, f32[400,128]{1,0:T(8,128)S(1)}, u32[]{:S(2)}, u32[]{:S(2)}) collective-permute-start(f32[400,128]{1,0:T(8,128)S(1)} %reduce_sum.9.refs_0_.mine_ref), channel_id=1, source_target_pairs={{0,4},{2,6},{4,0},{6,2},{1,5},{3,7},{5,1},{7,3},{8,12},{10,14},{12... | collective-permute-start | bytes 614408 | tf_op jit(solution)/shard_map/ppermute | solution.py:471
  99.7 16.1 %collective-permute-start.1 = (f32[400,128]{1,0:T(8,128)S(1)}, f32[400,128]{1,0:T(8,128)S(1)}, u32[]{:S(2)}, u32[]{:S(2)}) collective-permute-start(f32[400,128]{1,0:T(8,128)S(1)} %reduce_sum.9.refs_0_.mine_ref), channel_id=1, source_target_pairs={{0,6},{2,0},{4,2},{6,4},{1,7},{3,1},{5,3},{7,5},{8,14},{10,8},{12,... | collective-permute-start | bytes 614408 | tf_op jit(solution)/shard_map/ppermute | solution.py:471
  100.8 18.8 %copy-start.1 = (f32[400,128]{1,0:T(8,128)}, f32[400,128]{1,0:T(8,128)S(1)}, u32[]{:S(2)}) copy-start(f32[400,128]{1,0:T(8,128)S(1)} %collective-permute-done.4.refs_4_.other_ref) | copy-start | bytes 614404
  100.8 18.1 %collective-permute-start.7 = (f32[400,128]{1,0:T(8,128)S(1)}, f32[400,128]{1,0:T(8,128)S(1)}, u32[]{:S(2)}, u32[]{:S(2)}) collective-permute-start(f32[400,128]{1,0:T(8,128)S(1)} %collective-permute-done.4.refs_4_.other_ref), channel_id=1, source_target_pairs={{0,2},{2,4},{4,6},{6,0},{1,3},{3,5},{5,7},{7,1},{8,10},{10,12},{12... | collective-permute-start | bytes 614408 | tf_op jit(solution)/shard_map/ppermute | solution.py:471
  101.8 17.1 %collective-permute-start.6 = (f32[400,128]{1,0:T(8,128)S(1)}, f32[400,128]{1,0:T(8,128)S(1)}, u32[]{:S(2)}, u32[]{:S(2)}) collective-permute-start(f32[400,128]{1,0:T(8,128)S(1)} %collective-permute-done.4.refs_4_.other_ref), channel_id=1, source_target_pairs={{0,4},{2,6},{4,0},{6,2},{1,5},{3,7},{5,1},{7,3},{8,12},{10,14},{12... | collective-permute-start | bytes 614408 | tf_op jit(solution)/shard_map/ppermute | solution.py:471
  110.6 9.0 %copy-start.5 = (f32[400,128]{1,0:T(8,128)}, f32[400,128]{1,0:T(8,128)S(1)}, u32[]{:S(2)}) copy-start(f32[400,128]{1,0:T(8,128)S(1)} %collective-permute-done.3.refs_3_) | copy-start | bytes 614404
  110.6 9.0 %collective-permute-start.5 = (f32[400,128]{1,0:T(8,128)S(1)}, f32[400,128]{1,0:T(8,128)S(1)}, u32[]{:S(2)}, u32[]{:S(2)}) collective-permute-start(f32[400,128]{1,0:T(8,128)S(1)} %collective-permute-done.4.refs_4_.other_ref), channel_id=1, source_target_pairs={{0,6},{2,0},{4,2},{6,4},{1,7},{3,1},{5,3},{7,5},{8,14},{10,8},{12,... | collective-permute-start | bytes 614408 | tf_op jit(solution)/shard_map/ppermute | solution.py:471
  111.4 16.1 %all-to-all-start.3 = ((f32[16,50,128]{2,1,0:T(8,128)}), f32[16,50,128]{2,1,0:T(8,128)S(1)}, u32[]{:S(2)}, u32[]{:S(2)}) async-start(f32[16,50,128]{2,1,0:T(8,128)} %pair_up.1), calls=%async_computation.3 | async-start | bytes 917504 | tf_op jit(solution)/shard_map/all_to_all | solution.py:480
  115.8 3.8 %copy-start.6 = (f32[400,128]{1,0:T(8,128)}, f32[400,128]{1,0:T(8,128)S(1)}, u32[]{:S(2)}) copy-start(f32[400,128]{1,0:T(8,128)S(1)} %collective-permute-done.2.refs_2_) | copy-start | bytes 614404
  115.8 3.8 %copy-start.7 = (f32[400,128]{1,0:T(8,128)}, f32[400,128]{1,0:T(8,128)S(1)}, u32[]{:S(2)}) copy-start(f32[400,128]{1,0:T(8,128)S(1)} %collective-permute-done.1.refs_1_) | copy-start | bytes 614404
  118.9 0.7 copy-start.8
  118.9 0.8 copy-start.9
  119.7 0.7 copy-start.10
  129.5 6.5 %copy-start.2 = (s32[3]{0:T(128)S(1)}, s32[3]{0:T(128)}, u32[]{:S(2)}) copy-start(s32[3]{0:T(128)} %pad_add_fusion.scalars) | copy-start | bytes 40
  129.5 6.5 %copy-start.3 = (f32[640,640]{1,0:T(8,128)S(1)}, f32[640,640]{1,0:T(8,128)}, u32[]{:S(2)}) copy-start(f32[640,640]{1,0:T(8,128)} %own_start.1.x_ref) | copy-start | bytes 4915204
  129.5 33.4 %all-to-all-start.4 = ((f32[64,50,128]{2,1,0:T(8,128)}), f32[64,50,128]{2,1,0:T(8,128)S(1)}, u32[]{:S(2)}, u32[]{:S(2)}) async-start(f32[64,50,128]{2,1,0:T(8,128)} %gather_fusion.1), calls=%async_computation.4 | async-start | bytes 3670016 | tf_op jit(solution)/shard_map/all_to_all | solution.py:480

commit v7 on v6

--- a/solution.py
+++ b/solution.py
@@ -267,15 +267,35 @@
     ]
 
 
-def own_start_kernel(scalars, *refs):
-    gathered, (o_ref, x, a, b, r, _, sem) = refs[:GROUPS], refs[GROUPS:]
+def join_kernel(_, *refs):
+    o_ref = refs[-1]
+    lines = refs[0].shape[0]
+    for k, ref in enumerate(refs[:-1]):
+        o_ref[k * lines : (k + 1) * lines] = ref[...]
+
+
+def join(after, blocks):
+    lines, lanes = blocks[0].shape
+    return pl.pallas_call(
+        join_kernel,
+        out_shape=jax.ShapeDtypeStruct((len(blocks) * lines, lanes), F32),
+        in_specs=[pl.BlockSpec(memory_space=pltpu.HBM)] + [WHOLE] * len(blocks),
+        out_specs=WHOLE,
+        compiler_params=params(),
+        cost_estimate=cost(lines, 8 * len(blocks) * lines * lanes),
+        name="join",
+    )(after, *blocks)
+
+
+def own_start_kernel(scalars, mine_ref, other_ref, o_ref, x, a, b, r, _, sem):
     n = x.shape[0]
     chips = GROUPS // 2
+    lines = mine_ref.shape[0] // chips
     parts = []
-    for core, first in enumerate(half_starts(scalars[0], n // 2)):
+    for ref, first in zip((mine_ref, other_ref), half_starts(scalars[0], n // 2), strict=True):
         for ahead in range(chips):
             start = first + lax.rem(scalars[2] + ahead, chips) * (n // GROUPS)
-            parts.append((gathered[core * chips + ahead], start))
+            parts.append((ref.at[ahead * lines : (ahead + 1) * lines], start))
     start_polar(parts, x)
     iterate_singly(EARLY, x, a, b, r)
     copy = pltpu.make_async_copy(x, o_ref, sem)
@@ -283,17 +303,17 @@
     copy.wait()
 
 
-def own_start(scalars, gathered, n):
+def own_start(scalars, mine, other, n):
     return pl.pallas_call(
         own_start_kernel,
         out_shape=jax.ShapeDtypeStruct((n, n), F32),
-        in_specs=[pl.BlockSpec(memory_space=pltpu.SMEM)] + [WHOLE] * GROUPS,
+        in_specs=[pl.BlockSpec(memory_space=pltpu.SMEM), WHOLE, WHOLE],
         out_specs=pl.BlockSpec(memory_space=pltpu.HBM),
         scratch_shapes=polar_scratch(n) + [pltpu.SemaphoreType.DMA],
         compiler_params=params(ALL_VMEM),
         cost_estimate=cost(EARLY * 12 * n**3, 8 * n * n),
         name="own_start",
-    )(scalars, *gathered)
+    )(scalars, mine, other)
 
 
 def own_finish_kernel(scalars, x_ref, l_ref, columns_ref, o_ref, x, a, b, r, g, blocks, result, sems, out_sems):
@@ -502,11 +522,12 @@
     chunk = jnp.sum(exchange(pair, "x"), axis=0)
 
     other_chunk = swap_cores(chunk)
-    spread = exchange(pair_up(chunk, other_chunk), "sector")
+    pieces = pair_up(chunk, other_chunk)
+    spread = exchange(pieces, "sector")
 
     where = jnp.stack([core, group_here, chip]).astype(jnp.int32)
-    gathered = from_chips(chunk) + from_chips(other_chunk)
-    early, spread = lax.optimization_barrier((own_start(where, gathered, n), spread))
+    mine = join(pieces, from_chips(chunk))
+    early, spread = lax.optimization_barrier((own_start(where, mine, swap_cores(mine), n), spread))
     source_pieces = deliver(spread, readers)
     own_rows, half3 = own_finish(where, early, stacked_left)
     half3, source_pieces = lax.optimization_barrier((half3, source_pieces))

time: 194 us -> 193 us (level)
  blocking collectives: 38.5 us -> 29.7 us
  starting transfers between devices: 34.1 us -> 40.4 us
    all_to_all x1, blocking collectives: 28.8 us -> 20.1 us  [exchange(): return lax.all_to_all(pieces, axes, split_axis=0, concat_axis=0, tiled=True)]
    ppermute x2 -> x3, starting transfers between devices: 1.87 us -> 6.86 us  [swap_cores(): return lax.ppermute(block, 'core', [(0, 1), (1, 0)])]
    all_to_all x4, starting transfers between devices: 25.9 us -> 29.8 us  [exchange(): return lax.all_to_all(pieces, axes, split_axis=0, concat_axis=0, tiled=True)]
    all_to_all x4, waiting for transfers between devices: 12 us -> 15.2 us  [exchange(): return lax.all_to_all(pieces, axes, split_axis=0, concat_axis=0, tiled=True)]
    ppermute x6 -> x3, starting transfers between devices: 6.32 us -> 3.78 us  [from_chips(): lax.ppermute(block, 'x', [(j, (j - ahead) % chips) for j in range(chips)])]
    ppermute x6 -> x3, waiting for transfers between devices: 11 us -> 9.09 us  [from_chips(): lax.ppermute(block, 'x', [(j, (j - ahead) % chips) for j in range(chips)])]
  transfers between devices with their start and end apart: 12 -> 10, of which waited for: 7 -> 7; matrix products, arithmetic and copies ran while one was open for 0% -> 0% of each run, Pallas kernels for 25% -> 25%
where the time goes in v7:
time: 193 us; the launch traced here: 192 us
  Pallas kernels  88.5 us (46%)
  starting transfers between devices  40.4 us (21%)
  blocking collectives  29.7 us (15%)
  waiting for transfers between devices  26.3 us (14%)
  local copies, waits for them, and re-layouts  4.89 us (3%)
    pallas_call x1, Pallas kernels, rotate_by_source(): pl.pallas_call(source_kernel, out_shape=jax.ShapeDtypeStruct((k, n, n), F...  30.2 us
    all_to_all x4, starting transfers between devices, exchange(): return lax.all_to_all(pieces, axes, split_axis=0, concat_axis=0, tiled=True)  29.8 us
    pallas_call x1, Pallas kernels, own_finish(): pl.pallas_call(own_finish_kernel, out_shape=(jax.ShapeDtypeStruct((n // G...  26.4 us
    all_to_all x1, blocking collectives, exchange(): return lax.all_to_all(pieces, axes, split_axis=0, concat_axis=0, tiled=True)  20.1 us
    all_to_all x4, waiting for transfers between devices, exchange(): return lax.all_to_all(pieces, axes, split_axis=0, concat_axis=0, tiled=True)  15.2 us
    pallas_call x1, Pallas kernels, prepare(): pl.pallas_call(prepare_kernel, grid=(k,), out_shape=(jax.ShapeDtypeStruct...  14 us
    all_gather x1, blocking collectives, shards(): readers = lax.all_gather(shift_map[0], 'x').T.reshape(-1)  9.67 us
    ppermute x3, waiting for transfers between devices, from_chips(): lax.ppermute(block, 'x', [(j, (j - ahead) % chips) for j in range(chips)])  9.09 us
  transfers between devices with their start and end apart: 10, of which 7 were waited for; matrix products, arithmetic and copies ran while one was open for 0% of the time, Pallas kernels for 25%

profile of v7, /device:TPU:0, one launch (start us, length us, event | category | flops | bytes accessed | tf_op | source)
XLA Modules:
  0.0 192.2 jit_solution(15362266019813972758)
XLA Ops:
  0.6 0.0 copy-start.3
  0.6 1.8 cut.1
  2.5 8.1 %all-to-all-start = ((f32[16,50,128]{2,1,0:T(8,128)}), f32[16,50,128]{2,1,0:T(8,128)S(1)}, u32[]{:S(2)}, u32[]{:S(2)}) async-start(f32[16,50,128]{2,1,0:T(8,128)} %cut.1), calls=%async_computation | async-start | bytes 917504 | tf_op jit(solution)/shard_map/all_to_all | solution.py:500
  10.6 0.0 copy-done.3
  10.6 9.7 %all-gather = s32[4,1,16]{2,1,0:T(1,128)S(1)} all-gather(s32[1,1,16]{2,1,0:T(1,128)S(1)} %bitcast.22), channel_id=1, replica_groups=mesh['sector'=16,'x'=4,'core'=2] {'x'}, dimensions={0}, use_global_device_ids=true | all-gather | bytes 320 | tf_op jit(solution)/shard_map/all_gather | solution.py:514
  20.3 0.1 copy.9
  20.4 0.1 reshape.12
  20.5 0.9 all-to-all-done
  21.4 1.9 gather_fusion
  23.3 7.5 %all-to-all-start.1 = ((f32[64,50,128]{2,1,0:T(8,128)}), f32[64,50,128]{2,1,0:T(8,128)S(1)}, u32[]{:S(2)}, u32[]{:S(2)}) async-start(f32[64,50,128]{2,1,0:T(8,128)} %gather_fusion), calls=%async_computation.1 | async-start | bytes 3670016 | tf_op jit(solution)/shard_map/all_to_all | solution.py:500
  31.5 14.0 %prepare.1 = (bf16[4,640,1920]{2,1,0:T(8,128)(2,1)}, bf16[4,1920,640]{2,1,0:T(8,128)(2,1)}, bf16[1920,2560]{1,0:T(8,128)(2,1)}) custom-call(f32[4,640,640]{2,1,0:T(8,128)} %bitcast.17, f32[4,640,640]{2,1,0:T(8,128)} %bitcast.18), custom_call_target="tpu_custom_call" | custom-call | flops 19660800 | bytes 42598400 | tf_op jit(solution)/shard_map/prepare/pallas_call | solution.py:77
  45.4 0.1 pad_add_fusion.1.scalars
  45.5 10.6 %all-to-all-done.1.w_ref = f32[64,50,128]{2,1,0:T(8,128)S(1)} async-done(((f32[64,50,128]{2,1,0:T(8,128)}), f32[64,50,128]{2,1,0:T(8,128)S(1)}, u32[]{:S(2)}, u32[]{:S(2)}) %all-to-all-start.1) | async-done | bytes 1638432 | tf_op jit(solution)/shard_map/all_to_all | solution.py:500
  56.1 8.1 %partial_sigma.1 = (f32[1600,128]{1,0:T(8,128)S(1)}, f32[1600,128]{1,0:T(8,128)S(1)}) custom-call(s32[2]{0:T(128)S(1)} %pad_add_fusion.1.scalars, f32[64,50,128]{2,1,0:T(8,128)S(1)} %all-to-all-done.1.w_ref, bf16[4,640,1920]{2,1,0:T(8,128)(2,1)} %get-tuple-element.13.l_ref, bf16[4,1920,640]{2,1,0:T(8,128)(2,1)} %get-tuple-element.14.r_ref), custom_call_target="tpu_custom_call" | custom-call | flops 12582912000 | bytes 26214400 | tf_op jit(solution)/shard_map/partial_sigma/pallas_call | solution.py:163
  64.2 6.7 %collective-permute-start = (f32[1600,128]{1,0:T(8,128)S(1)}, f32[1600,128]{1,0:T(8,128)S(1)}, u32[]{:S(2)}, u32[]{:S(2)}) collective-permute-start(f32[1600,128]{1,0:T(8,128)S(1)} %get-tuple-element.16), channel_id=1, source_target_pairs={{0,1},{1,0},{2,3},{3,2},{4,5},{5,4},{6,7},{7,6},{8,9},{9,8},{10,11... | collective-permute-start | bytes 2457608 | tf_op jit(solution)/shard_map/ppermute | solution.py:496
  70.9 2.0 %collective-permute-done = f32[1600,128]{1,0:T(8,128)S(1)} collective-permute-done((f32[1600,128]{1,0:T(8,128)S(1)}, f32[1600,128]{1,0:T(8,128)S(1)}, u32[]{:S(2)}, u32[]{:S(2)}) %collective-permute-start) | collective-permute-done | bytes 819232 | tf_op jit(solution)/shard_map/ppermute | solution.py:496
  72.9 0.1 add.7
  73.0 20.1 %all_to_all.25 = f32[4,400,128]{2,1,0:T(8,128)S(1)} all-to-all(f32[4,400,128]{2,1,0:T(8,128)S(1)} %bitcast.19), channel_id=1, replica_groups=mesh['sector'=16,'x'=4,'core'=2] {'x'}, dimensions={0} | all-to-all | bytes 1638400 | tf_op jit(solution)/shard_map/all_to_all | solution.py:500
  93.1 0.1 collective-permute-start.1
  93.2 0.6 collective-permute-start.4
  93.8 2.1 %collective-permute-start.3 = (f32[400,128]{1,0:T(8,128)S(1)}, f32[400,128]{1,0:T(8,128)S(1)}, u32[]{:S(2)}, u32[]{:S(2)}) collective-permute-start(f32[400,128]{1,0:T(8,128)S(1)} %reduce_sum.9.mine_ref.refs_0_), channel_id=1, source_target_pairs={{0,4},{2,6},{4,0},{6,2},{1,5},{3,7},{5,1},{7,3},{8,12},{10,14},{12... | collective-permute-start | bytes 614408 | tf_op jit(solution)/shard_map/ppermute | solution.py:491
  95.9 1.1 collective-permute-start.2
  97.0 0.0 collective-permute-done.1.other_ref
  97.0 0.8 pair_up.1._
  97.8 8.5 %collective-permute-done.4.refs_3_ = f32[400,128]{1,0:T(8,128)S(1)} collective-permute-done((f32[400,128]{1,0:T(8,128)S(1)}, f32[400,128]{1,0:T(8,128)S(1)}, u32[]{:S(2)}, u32[]{:S(2)}) %collective-permute-start.4) | collective-permute-done | bytes 204832 | tf_op jit(solution)/shard_map/ppermute | solution.py:491
  106.3 0.0 collective-permute-done.3.refs_2_
  106.3 0.6 collective-permute-done.2.refs_1_
  106.9 0.1 join.1.mine_ref
  106.9 0.0 copy-start
  107.0 0.1 collective-permute-start.5
  107.1 6.8 %all-to-all-start.3 = ((f32[16,50,128]{2,1,0:T(8,128)}), f32[16,50,128]{2,1,0:T(8,128)S(1)}, u32[]{:S(2)}, u32[]{:S(2)}) async-start(f32[16,50,128]{2,1,0:T(8,128)} %pair_up.1._), calls=%async_computation.3 | async-start | bytes 917504 | tf_op jit(solution)/shard_map/all_to_all | solution.py:500
  113.8 0.6 pad_add_fusion.scalars
  114.4 0.0 collective-permute-done.5.other_ref
  114.4 0.0 copy-done
  114.4 0.0 copy-start.4
  114.4 0.9 copy-done.4
  115.3 7.1 %own_start.1.x_ref = f32[640,640]{1,0:T(8,128)} custom-call(s32[3]{0:T(128)} %pad_add_fusion.scalars, f32[1600,128]{1,0:T(8,128)} %copy-done, f32[1600,128]{1,0:T(8,128)} %copy-done.4), custom_call_target="tpu_custom_call" | custom-call | flops 3145728000 | bytes 3276800 | tf_op jit(solution)/shard_map/own_start/pallas_call | solution.py:307
  122.4 2.9 %all-to-all-done.3 = f32[16,50,128]{2,1,0:T(8,128)S(1)} async-done(((f32[16,50,128]{2,1,0:T(8,128)}), f32[16,50,128]{2,1,0:T(8,128)S(1)}, u32[]{:S(2)}, u32[]{:S(2)}) %all-to-all-start.3) | async-done | bytes 409632 | tf_op jit(solution)/shard_map/all_to_all | solution.py:500
  125.3 1.9 gather_fusion.1
  127.2 0.0 copy-start.1
  127.2 0.0 copy-start.2
  127.2 7.4 %all-to-all-start.4 = ((f32[64,50,128]{2,1,0:T(8,128)}), f32[64,50,128]{2,1,0:T(8,128)S(1)}, u32[]{:S(2)}, u32[]{:S(2)}) async-start(f32[64,50,128]{2,1,0:T(8,128)} %gather_fusion.1), calls=%async_computation.4 | async-start | bytes 3670016 | tf_op jit(solution)/shard_map/all_to_all | solution.py:500
  134.6 0.0 copy-done.1
  134.6 0.0 copy-done.2
  134.6 26.4 %own_finish.1 = (f32[80,640]{1,0:T(8,128)}, bf16[4,640,1920]{2,1,0:T(8,128)(2,1)}) custom-call(s32[3]{0:T(128)S(1)} %copy-done.1, f32[640,640]{1,0:T(8,128)S(1)} %copy-done.2, bf16[1920,2560]{1,0:T(8,128)(2,1)} %get-tuple-element.18.l_ref), custom_call_target="tpu_custom_call" | custom-call | flops 18874368000 | bytes 22937600 | tf_op jit(solution)/shard_map/own_finish/pallas_call | solution.py:361
  161.0 0.8 all-to-all-done.4.p_ref
  161.8 30.2 %rotate_by_source.1 = f32[4,640,640]{2,1,0:T(8,128)} custom-call(s32[3]{0:T(128)S(1)} %copy-done.1, f32[64,50,128]{2,1,0:T(8,128)S(1)} %all-to-all-done.4.p_ref, bf16[4,640,1920]{2,1,0:T(8,128)(2,1)} %get-tuple-element.23.h_ref), custom_call_target="tpu_custom_call" | custom-call | flops 22020096000 | bytes 16384000 | tf_op jit(solution)/shard_map/rotate_by_source/pallas_call | solution.py:418
  (2 shorter events, 0.0 us)
Async XLA Ops:
  0.6 10.0 %copy-start.3 = (s32[1,16]{1,0:T(1,128)S(1)}, s32[1,16]{1,0:T(1,128)}, u32[]{:S(2)}) copy-start(s32[1,16]{1,0:T(1,128)} %param.8) | copy-start | bytes 196
  2.5 18.9 %all-to-all-start = ((f32[16,50,128]{2,1,0:T(8,128)}), f32[16,50,128]{2,1,0:T(8,128)S(1)}, u32[]{:S(2)}, u32[]{:S(2)}) async-start(f32[16,50,128]{2,1,0:T(8,128)} %cut.1), calls=%async_computation | async-start | bytes 917504 | tf_op jit(solution)/shard_map/all_to_all | solution.py:500
  23.3 32.8 %all-to-all-start.1 = ((f32[64,50,128]{2,1,0:T(8,128)}), f32[64,50,128]{2,1,0:T(8,128)S(1)}, u32[]{:S(2)}, u32[]{:S(2)}) async-start(f32[64,50,128]{2,1,0:T(8,128)} %gather_fusion), calls=%async_computation.1 | async-start | bytes 3670016 | tf_op jit(solution)/shard_map/all_to_all | solution.py:500
  64.2 8.6 %collective-permute-start = (f32[1600,128]{1,0:T(8,128)S(1)}, f32[1600,128]{1,0:T(8,128)S(1)}, u32[]{:S(2)}, u32[]{:S(2)}) collective-permute-start(f32[1600,128]{1,0:T(8,128)S(1)} %get-tuple-element.16), channel_id=1, source_target_pairs={{0,1},{1,0},{2,3},{3,2},{4,5},{5,4},{6,7},{7,6},{8,9},{9,8},{10,11... | collective-permute-start | bytes 2457608 | tf_op jit(solution)/shard_map/ppermute | solution.py:496
  93.1 3.9 %collective-permute-start.1 = (f32[400,128]{1,0:T(8,128)S(1)}, f32[400,128]{1,0:T(8,128)S(1)}, u32[]{:S(2)}, u32[]{:S(2)}) collective-permute-start(f32[400,128]{1,0:T(8,128)S(1)} %reduce_sum.9.mine_ref.refs_0_), channel_id=1, source_target_pairs={{0,1},{1,0},{2,3},{3,2},{4,5},{5,4},{6,7},{7,6},{8,9},{9,8},{10,11... | collective-permute-start | bytes 614408 | tf_op jit(solution)/shard_map/ppermute | solution.py:496
  93.2 13.1 %collective-permute-start.4 = (f32[400,128]{1,0:T(8,128)S(1)}, f32[400,128]{1,0:T(8,128)S(1)}, u32[]{:S(2)}, u32[]{:S(2)}) collective-permute-start(f32[400,128]{1,0:T(8,128)S(1)} %reduce_sum.9.mine_ref.refs_0_), channel_id=1, source_target_pairs={{0,2},{2,4},{4,6},{6,0},{1,3},{3,5},{5,7},{7,1},{8,10},{10,12},{12... | collective-permute-start | bytes 614408 | tf_op jit(solution)/shard_map/ppermute | solution.py:491
  93.8 12.5 %collective-permute-start.3 = (f32[400,128]{1,0:T(8,128)S(1)}, f32[400,128]{1,0:T(8,128)S(1)}, u32[]{:S(2)}, u32[]{:S(2)}) collective-permute-start(f32[400,128]{1,0:T(8,128)S(1)} %reduce_sum.9.mine_ref.refs_0_), channel_id=1, source_target_pairs={{0,4},{2,6},{4,0},{6,2},{1,5},{3,7},{5,1},{7,3},{8,12},{10,14},{12... | collective-permute-start | bytes 614408 | tf_op jit(solution)/shard_map/ppermute | solution.py:491
  95.9 11.0 %collective-permute-start.2 = (f32[400,128]{1,0:T(8,128)S(1)}, f32[400,128]{1,0:T(8,128)S(1)}, u32[]{:S(2)}, u32[]{:S(2)}) collective-permute-start(f32[400,128]{1,0:T(8,128)S(1)} %reduce_sum.9.mine_ref.refs_0_), channel_id=1, source_target_pairs={{0,6},{2,0},{4,2},{6,4},{1,7},{3,1},{5,3},{7,5},{8,14},{10,8},{12,... | collective-permute-start | bytes 614408 | tf_op jit(solution)/shard_map/ppermute | solution.py:491
  106.9 7.5 %copy-start = (f32[1600,128]{1,0:T(8,128)}, f32[1600,128]{1,0:T(8,128)S(1)}, u32[]{:S(2)}) copy-start(f32[1600,128]{1,0:T(8,128)S(1)} %join.1.mine_ref) | copy-start | bytes 2457604
  107.0 7.5 %collective-permute-start.5 = (f32[1600,128]{1,0:T(8,128)S(1)}, f32[1600,128]{1,0:T(8,128)S(1)}, u32[]{:S(2)}, u32[]{:S(2)}) collective-permute-start(f32[1600,128]{1,0:T(8,128)S(1)} %join.1.mine_ref), channel_id=1, source_target_pairs={{0,1},{1,0},{2,3},{3,2},{4,5},{5,4},{6,7},{7,6},{8,9},{9,8},{10,11... | collective-permute-start | bytes 2457608 | tf_op jit(solution)/shard_map/ppermute | solution.py:496
  107.1 18.2 %all-to-all-start.3 = ((f32[16,50,128]{2,1,0:T(8,128)}), f32[16,50,128]{2,1,0:T(8,128)S(1)}, u32[]{:S(2)}, u32[]{:S(2)}) async-start(f32[16,50,128]{2,1,0:T(8,128)} %pair_up.1._), calls=%async_computation.3 | async-start | bytes 917504 | tf_op jit(solution)/shard_map/all_to_all | solution.py:500
  114.4 0.9 copy-start.4
  127.2 7.4 %copy-start.1 = (s32[3]{0:T(128)S(1)}, s32[3]{0:T(128)}, u32[]{:S(2)}) copy-start(s32[3]{0:T(128)} %pad_add_fusion.scalars) | copy-start | bytes 40
  127.2 7.4 %copy-start.2 = (f32[640,640]{1,0:T(8,128)S(1)}, f32[640,640]{1,0:T(8,128)}, u32[]{:S(2)}) copy-start(f32[640,640]{1,0:T(8,128)} %own_start.1.x_ref) | copy-start | bytes 4915204
  127.2 34.6 %all-to-all-start.4 = ((f32[64,50,128]{2,1,0:T(8,128)}), f32[64,50,128]{2,1,0:T(8,128)S(1)}, u32[]{:S(2)}, u32[]{:S(2)}) async-start(f32[64,50,128]{2,1,0:T(8,128)} %gather_fusion.1), calls=%async_computation.4 | async-start | bytes 3670016 | tf_op jit(solution)/shard_map/all_to_all | solution.py:500
